TPU v7x, 32 devices: a whole 2x2x4 slice. The times are simulated.
32 devices in a mesh: dp: 4 (over y, x), expert: 4 (over z), tensor: 2 (over core).
Axes of the slice: x: 2, y: 2, z: 4, core: 2. Of those that a mesh axis runs over, the one named last changes fastest.
Arguments:
- tokens: bfloat16 [4096, 2048], P(('dp', 'expert')), may hold values from -6 to 6
- segments: int32 [4, 1024], P('dp', 'expert'), may hold values from 0 to 7, never falling along the last dimension, each value on 1 to 512 neighbouring positions
- routes: int32 [4096, 4], P(('dp', 'expert')), may hold values from 0 to 7, all different within a row; in each aligned block of 256 rows (0 to 255, 256 to 511, ...) at most 192 rows name the same one
- norm1_gain: bfloat16 [2048], replicated, may hold values from 0.5 to 1.5
- q_weight: bfloat16 [2048, 2048], P(None, 'tensor'), may hold values from -0.125 to 0.125
- k_weight: bfloat16 [2048, 2048], P(None, 'tensor'), may hold values from -0.125 to 0.125
- v_weight: bfloat16 [2048, 2048], P(None, 'tensor'), may hold values from -0.125 to 0.125
- o_weight: bfloat16 [2048, 2048], P(None, 'tensor'), may hold values from -0.5 to 0.5
- norm2_gain: bfloat16 [2048], replicated, may hold values from 0.5 to 1.5
- router_weight: bfloat16 [2048, 8], replicated, may hold values from -0.0625 to 0.0625
- shared_gate_vector: bfloat16 [2048], replicated, may hold values from -0.125 to 0.125
- shared_gate_weight: bfloat16 [2048, 5632], P(None, 'tensor'), may hold values from -0.125 to 0.125
- shared_up_weight: bfloat16 [2048, 5632], P(None, 'tensor'), may hold values from -0.125 to 0.125
- shared_down_weight: bfloat16 [2048, 5632], P(None, 'tensor'), may hold values from -0.25 to 0.25
- expert_gate_weight: bfloat16 [8, 2048, 1408], P('expert', None, 'tensor'), may hold values from -0.125 to 0.125
- expert_up_weight: bfloat16 [8, 2048, 1408], P('expert', None, 'tensor'), may hold values from -0.125 to 0.125
- expert_down_weight: bfloat16 [8, 2048, 1408], P('expert', None, 'tensor'), may hold values from -1 to 1
- out_grad: bfloat16 [4096, 2048], P(('dp', 'expert')), may hold values from -6 to 6
Outputs:
- layer_out: float32 [4096, 2048], P(('dp', 'expert'))
- input_grad: float32 [4096, 2048], P(('dp', 'expert'))
- rms_stats: float32 [2, 4096], P(None, ('dp', 'expert'))
- norm1_gain_grad: float32 [2048], P(('dp', 'expert'))
- q_weight_grad: float32 [2048, 2048], P(('dp', 'expert'), 'tensor')
- k_weight_grad: float32 [2048, 2048], P(('dp', 'expert'), 'tensor')
- v_weight_grad: float32 [2048, 2048], P(('dp', 'expert'), 'tensor')
- o_weight_grad: float32 [2048, 2048], P(('dp', 'expert'), 'tensor')
- norm2_gain_grad: float32 [2048], P(('dp', 'expert'))
- router_grad: float32 [2048, 8], P(('dp', 'expert'))
- shared_vector_grad: float32 [2048], P(('dp', 'expert'))
- shared_gate_grad: float32 [2048, 5632], P(('dp', 'expert'), 'tensor')
- shared_up_grad: float32 [2048, 5632], P(('dp', 'expert'), 'tensor')
- shared_down_grad: float32 [2048, 5632], P(('dp', 'expert'), 'tensor')
- expert_gate_grad: float32 [8, 2048, 1408], P('expert', 'dp', 'tensor')
- expert_up_grad: float32 [8, 2048, 1408], P('expert', 'dp', 'tensor')
- expert_down_grad: float32 [8, 2048, 1408], P('expert', 'dp', 'tensor')
Inputs may be any that keep to these rules, and one draw needn't show every extreme that they name: `segments`: document numbers never fall along a sequence; each of the 8 documents of a sequence is present and holds 1 to 512 tokens, one exactly 512. `routes`: the 4 experts of a token differ. Among the 256 tokens of one index of dp and expert, no expert is named more than 192 times, a bound that some block reaches.
All inputs are finite; a program needn't handle non-finite values.
Results may differ from a plain program's by a relative error of at most 0.02.
Values may be sent and summed in bfloat16 or wider, within the bound.
A program may use at most 384 MiB of HBM per device.

v0:
```python
import functools

import jax
import jax.numpy as jnp
from jax import lax
from jax.experimental import pallas as pl
from jax.experimental.pallas import tpu as pltpu
from jax.sharding import PartitionSpec as P

HD = 128
MESH = pl.DeviceIdType.MESH
PIECES = 2
STRIP = 16
epsilon = 1e-06
f32 = jnp.float32
bf16 = jnp.bfloat16
UP, DOWN = 0, 1


def here():
    return lax.axis_index("expert"), lax.axis_index("tensor")


def greet(nz):
    z, c = here()
    barrier = pltpu.get_barrier_semaphore()

    def tell(device):
        pl.semaphore_signal(barrier, inc=1, device_id=device, device_id_type=MESH)

    tell({"tensor": 1 - c})
    for d in range(1, nz):
        tell({"expert": lax.rem(z + d, nz)})
    pl.semaphore_wait(barrier, nz)


def remote(src, dst, send, recv, device):
    return pltpu.make_async_remote_copy(
        src_ref=src, dst_ref=dst, send_sem=send, recv_sem=recv, device_id=device, device_id_type=MESH
    )


def strips(rows, step):
    def one(i, carry):
        step(pl.ds(pl.multiple_of(i * STRIP, STRIP), STRIP))
        return carry

    lax.fori_loop(0, rows // STRIP, one, 0)


GATHER_SEMS = 4


def gather_sems(nz):
    return [pltpu.SemaphoreType.DMA((2, nz, PIECES))] * GATHER_SEMS + [pltpu.SemaphoreType.DMA]


class Gather:
    def __init__(self, nz, own, out, z_send, z_recv, s_send, s_recv, local_sem):
        self.nz, self.own, self.out = nz, own, out
        self.z_send, self.z_recv, self.s_send, self.s_recv, self.local_sem = z_send, z_recv, s_send, s_recv, local_sem
        self.z, self.c = here()
        self.rows = own.shape[0]
        self.piece = self.rows // PIECES

    def origin(self, way, d):
        return self.z - d if way == UP else self.z + d

    def inside(self, way, d):
        return self.z >= d if way == UP else self.z + d < self.nz

    def onward(self, way):
        return self.z < self.nz - 1 if way == UP else self.z > 0

    def place(self, block, core, p):
        start = (block * 2 + core) * self.rows + p * self.piece
        return self.out.at[pl.ds(pl.multiple_of(start, self.piece), self.piece)]

    def source(self, way, d, p):
        if d == 0:
            return self.own.at[pl.ds(p * self.piece, self.piece)]
        return self.place(self.origin(way, d), self.c, p)

    def along(self, way, d, p):
        device = {"expert": self.z + 1 if way == UP else self.z - 1}
        dst = self.place(self.origin(way, d), self.c, p)
        return remote(self.source(way, d, p), dst, self.z_send.at[way, d, p], self.z_recv.at[way, d, p], device)

    def across(self, way, d, p):
        dst = self.place(self.origin(way, d), self.c, p)
        return remote(
            self.source(way, d, p), dst, self.s_send.at[way, d, p], self.s_recv.at[way, d, p], {"tensor": 1 - self.c}
        )

    def arrived(self, way, d, p):
        dst = self.place(self.origin(way, d), self.c, p)
        remote(dst, dst, self.z_send.at[way, d - 1, p], self.z_recv.at[way, d - 1, p], {"tensor": 1 - self.c}).wait_recv()

    def crossed(self, way, d, p):
        dst = self.place(self.origin(way, d), 1 - self.c, p)
        remote(dst, dst, self.s_send.at[way, d, p], self.s_recv.at[way, d, p], {"tensor": 1 - self.c}).wait_recv()

    def mine(self):
        dst = self.out.at[pl.ds(pl.multiple_of((self.z * 2 + self.c) * self.rows, self.rows), self.rows)]
        return pltpu.make_async_copy(self.own, dst, self.local_sem)

    def start_along(self, way):
        @pl.when(self.onward(way))
        def _():
            for p in range(PIECES):
                self.along(way, 0, p).start()

    def start_across(self):
        for p in range(PIECES):
            self.across(UP, 0, p).start()
        self.mine().start()

    def event(self, d, p):
        for way in (UP, DOWN):

            @pl.when(self.inside(way, d))
            def _(way=way):
                self.arrived(way, d, p)
                pl.when(self.onward(way))(lambda: self.along(way, d, p).start())
                self.across(way, d, p).start()

    def finish(self):
        for p in range(PIECES):
            self.crossed(UP, 0, p)
            self.across(UP, 0, p).wait_send()
            for way in (UP, DOWN):
                pl.when(self.onward(way))(lambda way=way, p=p: self.along(way, 0, p).wait_send())
                for d in range(1, self.nz):

                    @pl.when(self.inside(way, d))
                    def _(way=way, d=d, p=p):
                        self.crossed(way, d, p)
                        self.across(way, d, p).wait_send()
                        pl.when(self.onward(way))(lambda: self.along(way, d, p).wait_send())

        self.mine().wait()


def gather_rows(nz, own, out, *sems):
    gather = Gather(nz, own, out, *sems)
    gather.start_along(UP)
    gather.start_along(DOWN)
    gather.start_across()
    for d in range(1, nz):
        for p in range(PIECES):
            gather.event(d, p)
    gather.finish()


REDUCE_SCRATCH = 8


def reduce_scratch(nz, rows, width):
    return [
        pltpu.VMEM((nz, rows, width), bf16),
        pltpu.VMEM((nz + 1, rows, width), bf16),
        pltpu.VMEM((nz, rows, width), bf16),
        pltpu.VMEM((rows, width), f32),
        pltpu.SemaphoreType.DMA((nz, PIECES)),
        pltpu.SemaphoreType.DMA((nz, PIECES)),
        pltpu.SemaphoreType.DMA((nz, PIECES)),
        pltpu.SemaphoreType.DMA((nz + 1, PIECES)),
    ]


def block_order(nz, z, s):
    down = 2 * z // nz
    far = jnp.maximum(z, nz - 1 - z)
    near = nz - 1 - far
    late = s - (far - near)
    distance = jnp.where(late < 0, far - s, near - late // 2)
    sign = (1 - 2 * down) * jnp.where(late < 0, 1, 1 - 2 * lax.rem(late + nz * 2, 2))
    return z + sign * distance


class Reducer:
    def __init__(self, nz, part, side, inbox, outbox, total, s_send, s_recv, z_send, z_recv):
        self.nz, self.part, self.side, self.inbox, self.outbox, self.total = nz, part, side, inbox, outbox, total
        self.s_send, self.s_recv, self.z_send, self.z_recv = s_send, s_recv, z_send, z_recv
        self.z, self.c = here()
        self.rows = total.shape[0]
        self.piece = self.rows // PIECES

    def block(self, s):
        return block_order(self.nz, self.z, s)

    def cut(self, p):
        return pl.ds(p * self.piece, self.piece)

    def across(self, block, p):
        start = (block * 2 + 1 - self.c) * self.rows + p * self.piece
        src = self.part.at[pl.ds(pl.multiple_of(start, self.piece), self.piece)]
        return remote(
            src, self.side.at[block, self.cut(p)], self.s_send.at[block, p], self.s_recv.at[block, p],
            {"tensor": 1 - self.c},
        )

    def along(self, block, p):
        up = block > self.z
        slot = jnp.where(block == self.z - 1, self.nz, block)
        return remote(
            self.outbox.at[block, self.cut(p)], self.inbox.at[slot, self.cut(p)], self.z_send.at[block, p],
            self.z_recv.at[slot, p], {"expert": self.z + jnp.where(up, 1, -1)},
        )

    def arrived(self, slot, p):
        dst = self.inbox.at[slot, self.cut(p)]
        remote(dst, dst, self.z_send.at[0, p], self.z_recv.at[slot, p], {"tensor": 1 - self.c}).wait_recv()

    def mine(self, block, at):
        base = (block * 2 + self.c) * self.rows
        own = self.part[pl.ds(pl.multiple_of(base + at.start, STRIP), STRIP), :].astype(f32)
        return own + self.side[block, at, :].astype(f32)

    def strips(self, p, step):
        def one(i, carry):
            step(pl.ds(pl.multiple_of(p * self.piece + i * STRIP, STRIP), STRIP))
            return carry

        lax.fori_loop(0, self.piece // STRIP, one, 0)

    def ends(self):
        return jnp.logical_or(self.z == 0, self.z == self.nz - 1)

    def begin(self, s):
        for p in range(PIECES):
            self.across(self.block(s), p).start()

    def forward(self, s):
        block = self.block(s)
        behind = jnp.where(block > self.z, self.z, self.nz - 1 - self.z) > 0
        for p in range(PIECES):
            self.across(block, p).wait_recv()

            @pl.when(behind)
            def _(p=p):
                self.arrived(block, p)

                def add(at):
                    self.outbox[block, at, :] = (self.mine(block, at) + self.inbox[block, at, :].astype(f32)).astype(bf16)

                self.strips(p, add)

            @pl.when(jnp.logical_not(behind))
            def _(p=p):
                def keep(at):
                    self.outbox[block, at, :] = self.mine(block, at).astype(bf16)

                self.strips(p, keep)

            self.along(block, p).start()

    def finish(self):
        z, nz = self.z, self.nz
        for p in range(PIECES):
            self.across(z, p).wait_recv()

            def first(at):
                self.total[at, :] = self.mine(z, at)

            self.strips(p, first)
            for slot, some in ((z, z > 0), (nz, z < nz - 1)):

                @pl.when(some)
                def _(slot=slot, p=p):
                    self.arrived(slot, p)

                    def add(at):
                        self.total[at, :] += self.inbox[slot, at, :].astype(f32)

                    self.strips(p, add)

    def drain(self):
        def one(s, carry):
            block = self.block(s)
            for p in range(PIECES):
                self.across(block, p).wait_send()
                pl.when(s < self.nz - 1)(lambda p=p: self.along(block, p).wait_send())
            return carry

        lax.fori_loop(0, self.nz, one, 0)


def params(name, **more):
    return pltpu.CompilerParams(
        collective_id=name, has_side_effects=True, vmem_limit_bytes=56 * 1024 * 1024, **more
    )


VMEM = pl.BlockSpec(memory_space=pltpu.VMEM)
ANY = pl.BlockSpec(memory_space=pl.ANY)


def norm_rows(values, gain):
    inverse = lax.rsqrt(jnp.mean(values * values, axis=-1, keepdims=True) + epsilon)
    return values * inverse * gain, inverse


def norm_back(values, gain, upstream):
    inverse = lax.rsqrt(jnp.mean(values * values, axis=-1, keepdims=True) + epsilon)
    scaled = upstream * gain
    inner = jnp.mean(scaled * values, axis=-1, keepdims=True)
    change = inverse * scaled - values * inverse * inverse * inverse * inner
    return change, upstream * values * inverse


def attend(nz, x, gain, upstream, marks, weights, out_weight, gain2, name):
    rows, width = x.shape
    seq = nz * 2 * rows
    cols = weights[0].shape[1] // nz
    heads = cols // HD
    full = 2 * rows
    strip = 32
    scale = HD ** (-0.5)

    def kernel(x_ref, gain_ref, up_ref, marks_ref, gain2_ref, wq_hbm, wk_hbm, wv_hbm, wo_hbm, n1_ref, dy_ref, all_ref, qkv_ref,
               p_ref, o_ref, n2_ref, h_ref, inv_ref, own, w, scores, seg_q, seg_k, heads_in, acc, give, take_in, own2, inv_own, wo,
               w_sem, m_send, m_recv, m_local, a_send, a_recv, e_send, e_recv, i_sems, *sems):
        z, c = here()
        at = pl.ds(pl.multiple_of(z * cols, cols), cols)
        loads = [
            pltpu.make_async_copy(src.at[:, at], w.at[:, pl.ds(i * cols, cols)], w_sem.at[i])
            for i, src in enumerate((wq_hbm, wk_hbm, wv_hbm))
        ]
        loads.append(pltpu.make_async_copy(wo_hbm, wo, w_sem.at[3]))
        for load in loads:
            load.start()

        def step(strip_at):
            normed, _ = norm_rows(x_ref[strip_at, :].astype(f32), gain_ref[...])
            own[strip_at, :] = normed.astype(bf16)

        strips(rows, step)
        greet(nz)
        n1 = Gather(nz, own, n1_ref, *sems[:5])
        dy = Gather(nz, up_ref, dy_ref, *sems[5:10])
        n2 = Gather(nz, own2, n2_ref, *sems[10:])
        n1.start_along(UP)
        n1.start_along(DOWN)
        n1.start_across()
        keep = pltpu.make_async_copy(marks_ref, all_ref.at[z], m_local)
        keep.start()

        def send(way, d):
            to = z + d if way == UP else z - d
            return remote(marks_ref, all_ref.at[z], m_send.at[way, d], m_recv.at[way, d], {"expert": to})

        def take(way, d):
            dst = all_ref.at[z - d if way == UP else z + d]
            remote(dst, dst, m_send.at[way, d], m_recv.at[way, d], {"tensor": 1 - c}).wait_recv()

        for d in range(1, nz):
            for way in (UP, DOWN):
                pl.when(z + d < nz if way == UP else z >= d)(lambda way=way, d=d: send(way, d).start())

        def follow(d):
            pl.when(z == d)(lambda: dy.start_along(UP))
            pl.when(nz - 1 - z == d)(lambda: dy.start_along(DOWN))

        follow(0)
        for d in range(1, nz):
            for p in range(PIECES):
                n1.event(d, p)
            follow(d)
        dy.start_across()
        keep.wait()
        for d in range(1, nz):
            for way in (UP, DOWN):
                pl.when(z + d < nz if way == UP else z >= d)(lambda way=way, d=d: send(way, d).wait_send())
                pl.when(z >= d if way == UP else z + d < nz)(lambda way=way, d=d: take(way, d))
        n1.finish()
        for load in loads:
            load.wait()

        def project(first, last):
            def one(i, carry):
                to = pl.ds(pl.multiple_of(i * full, full), full)
                qkv_ref[to, :] = jnp.dot(n1_ref[to, :], w[...], preferred_element_type=f32).astype(bf16)
                return carry

            lax.fori_loop(first, last, one, 0)

        def label():
            for b in range(nz):
                some = all_ref[b].astype(f32)
                seg_q[b * full : (b + 1) * full, :] = some.T[:, :1]
                seg_k[:, b * full : (b + 1) * full] = some[:1, :]

        def head(i):
            length = (i + 1) * full

            def one(h, carry):
                def part(k):
                    return pl.ds(pl.multiple_of(k * cols + h * HD, HD), HD)

                base = i * full
                scores[:, :length] = lax.dot_general(
                    qkv_ref[base : base + full, part(0)], qkv_ref[:length, part(1)], (((1,), (1,)), ((), ())),
                    preferred_element_type=f32,
                )

                def soften(j, inner):
                    local = pl.ds(pl.multiple_of(j * strip, strip), strip)
                    row = pl.ds(pl.multiple_of(base + j * strip, strip), strip)
                    place_q = base + j * strip + lax.broadcasted_iota(jnp.int32, (strip, length), 0)
                    place_k = lax.broadcasted_iota(jnp.int32, (strip, length), 1)
                    allowed = jnp.logical_and(place_k <= place_q, seg_k[:, :length] == seg_q[row, :])
                    value = jnp.where(allowed, scores[local, :length] * scale, -jnp.inf)
                    value = jnp.exp(value - jnp.max(value, axis=-1, keepdims=True))
                    share = 1.0 / jnp.sum(value, axis=-1, keepdims=True)
                    p_ref[h, row, :length] = (value * share).astype(bf16)
                    return inner

                lax.fori_loop(0, full // strip, soften, 0)
                if length < seq:
                    p_ref[h, base : base + full, length:] = jnp.zeros((full, seq - length), bf16)
                o_ref[base : base + full, pl.ds(pl.multiple_of(h * HD, HD), HD)] = jnp.dot(
                    p_ref[h, base : base + full, :length], qkv_ref[:length, part(2)], preferred_element_type=f32
                ).astype(bf16)
                return carry

            lax.fori_loop(0, heads, one, 0)

        works = [label] + [functools.partial(head, i) for i in range(nz)]
        left_events = [(d, p) for d in range(1, nz) for p in range(PIECES)]

        def events(count=None):
            for _ in range(len(left_events) if count is None else count):
                dy.event(*left_events.pop(0))

        project(0, 2)
        events(1)
        project(2, nz)
        events(1)
        for work in works:
            work()
            if len(left_events) > 2:
                events(1)

        def inside(way, d):
            return z + d < nz if way == UP else z >= d

        def send_heads(way, d):
            to = z + d if way == UP else z - d
            src = o_ref.at[pl.ds(pl.multiple_of(to * full, full), full)]
            return remote(src, heads_in.at[way, d], a_send.at[way, d], a_recv.at[way, d], {"expert": to})

        for d in range(nz - 1, 0, -1):
            for way in (UP, DOWN):
                pl.when(inside(way, d))(lambda way=way, d=d: send_heads(way, d).start())

        tile = 512 if width % 512 == 0 else width

        def put(block, left, fresh):
            at = pl.ds(pl.multiple_of(block * cols, cols), cols)

            def one(i, carry):
                to = pl.ds(pl.multiple_of(i * tile, tile), tile)
                value = lax.dot_general(
                    left(), wo[to, at], (((1,), (1,)), ((), ())), preferred_element_type=f32
                )
                acc[:, to] = value if fresh else acc[:, to] + value
                return carry

            lax.fori_loop(0, width // tile, one, 0)

        put(z, lambda: o_ref[pl.ds(pl.multiple_of(z * full, full), full), :], True)
        events()
        for d in range(1, nz):
            for way in (UP, DOWN):
                @pl.when(z >= d if way == UP else z + d < nz)
                def _(way=way, d=d):
                    remote(
                        heads_in.at[way, d], heads_in.at[way, d], a_send.at[way, d], a_recv.at[way, d], {"tensor": 1 - c}
                    ).wait_recv()
                    put(z - d if way == UP else z + d, lambda: heads_in[way, d], False)

        def pack(at):
            give[at, :] = acc[pl.ds(pl.multiple_of((1 - c) * rows + at.start, STRIP), STRIP), :].astype(bf16)

        strips(rows, pack)
        swap = remote(give, take_in, e_send, e_recv, {"tensor": 1 - c})
        swap.start()
        swap.wait_recv()

        def norm_two(at):
            mixed = acc[pl.ds(pl.multiple_of(c * rows + at.start, STRIP), STRIP), :] + take_in[at, :].astype(f32)
            h = x_ref[at, :].astype(f32) + mixed
            normed, inverse = norm_rows(h, gain2_ref[...])
            h_ref[at, :] = h
            own2[at, :] = normed.astype(bf16)
            inv_own[at, :] = jnp.broadcast_to(inverse, (STRIP, 128))

        strips(rows, norm_two)
        spot = inv_ref.at[pl.ds(pl.multiple_of(c * rows, rows), rows)]
        keep_inv = pltpu.make_async_copy(inv_own, spot, i_sems.at[0])
        pass_on = remote(inv_own, spot, i_sems.at[1], i_sems.at[2], {"tensor": 1 - c})
        keep_inv.start()
        pass_on.start()
        n2.start_along(UP)
        n2.start_along(DOWN)
        n2.start_across()
        for d in range(1, nz):
            for p in range(PIECES):
                n2.event(d, p)
        n2.finish()
        dy.finish()
        keep_inv.wait()
        pass_on.wait()
        swap.wait_send()
        for d in range(1, nz):
            for way in (UP, DOWN):
                pl.when(inside(way, d))(lambda way=way, d=d: send_heads(way, d).wait_send())

    return pl.pallas_call(
        kernel,
        out_shape=[
            jax.ShapeDtypeStruct((seq, width), bf16),
            jax.ShapeDtypeStruct((seq, width), bf16),
            jax.ShapeDtypeStruct((nz,) + marks.shape, jnp.int32),
            jax.ShapeDtypeStruct((seq, 3 * cols), bf16),
            jax.ShapeDtypeStruct((heads, seq, seq), bf16),
            jax.ShapeDtypeStruct((seq, cols), bf16),
            jax.ShapeDtypeStruct((seq, width), bf16),
            jax.ShapeDtypeStruct((rows, width), f32),
            jax.ShapeDtypeStruct((full, 128), f32),
        ],
        in_specs=[VMEM] * 5 + [ANY] * 4,
        out_specs=[VMEM, ANY, VMEM, VMEM, VMEM, VMEM, ANY, VMEM, ANY],
        scratch_shapes=[
            pltpu.VMEM((rows, width), bf16), pltpu.VMEM((width, 3 * cols), bf16), pltpu.VMEM((full, seq), f32),
            pltpu.VMEM((seq, 1), f32), pltpu.VMEM((1, seq), f32),
            pltpu.VMEM((2, nz, full, cols), bf16),
            pltpu.VMEM((full, width), f32),
            pltpu.VMEM((rows, width), bf16),
            pltpu.VMEM((rows, width), bf16),
            pltpu.VMEM((rows, width), bf16),
            pltpu.VMEM((rows, 128), f32),
            pltpu.VMEM(out_weight.shape, bf16),
            pltpu.SemaphoreType.DMA((4,)),
            pltpu.SemaphoreType.DMA((2, nz)), pltpu.SemaphoreType.DMA((2, nz)), pltpu.SemaphoreType.DMA,
            pltpu.SemaphoreType.DMA((2, nz)),
            pltpu.SemaphoreType.DMA((2, nz)),
            pltpu.SemaphoreType.DMA,
            pltpu.SemaphoreType.DMA,
            pltpu.SemaphoreType.DMA((3,)),
        ]
        + gather_sems(nz) * 3,
        compiler_params=params(name),
    )(x, gain, upstream, marks, gain2, *weights, out_weight)


def swap_rows(nz, own, out_ref, sems):
    z, c = here()
    rows = own.shape[0]
    spot = out_ref.at[pl.ds(pl.multiple_of(c * rows, rows), rows)]
    keep = pltpu.make_async_copy(own, spot, sems.at[0])
    pass_on = remote(own, spot, sems.at[1], sems.at[2], {"tensor": 1 - c})
    keep.start()
    pass_on.start()
    keep.wait()
    pass_on.wait()


TILE = 256
TALL = 512
LANES = 128


def nt_dot(left, right):
    return lax.dot_general(left, right, (((1,), (1,)), ((), ())), preferred_element_type=f32)


def nn_dot(left, right):
    return jnp.dot(left, right, preferred_element_type=f32)


def tiles(count, step, size=TILE):
    def one(i, carry):
        step(i, pl.ds(pl.multiple_of(i * size, size), size))
        return carry

    lax.fori_loop(0, count, one, 0)


def padded(columns):
    return -(-columns // LANES) * LANES


def window(columns, place):
    first = place * columns // LANES * LANES
    return first, place * columns - first


def window_width(columns, places):
    return max(padded(window(columns, i)[1] + columns) for i in range(places))


def hidden_layer(nz, n2, dy, gate, weights, groups):
    seq, width = n2.shape
    shared = weights[0].ndim == 2
    experts = 1 if shared else weights[0].shape[0]
    buffers = min(experts, 2)
    ffn = weights[0].shape[1] // nz if shared else weights[0].shape[1]
    held = window_width(ffn, nz) if shared else ffn
    kept = held if shared else padded(ffn)
    block = width // groups
    lane = min(block, TILE)
    per = TILE // lane
    count, slabs = seq // TILE, width // TILE
    strip = 32
    product = nn_dot if shared else nt_dot
    w_shape = (width, held) if shared else (held, width)

    def kernel(n2_hbm, dy_hbm, wg_hbm, wu_hbm, wd_hbm, gate_ref, grad_hbm, da_hbm, db_hbm, gu_hbm, dgate_ref,
               n2_ref, dy_ref, wg, wu, wd, a, b, back, da, db, gu, turned, slab, in_sem, row_sem, out_sem, slab_sem):
        z = lax.axis_index("expert")
        first = pl.multiple_of(z * ffn // LANES * LANES, LANES)
        skip = z * ffn - first

        def pick(ref, e):
            return ref.at[:, pl.ds(first, held)] if shared else ref.at[e]

        def weight(i, e):
            slot = lax.rem(e, buffers)
            src, dst = ((wg_hbm, wg), (wu_hbm, wu), (wd_hbm, wd))[i]
            return pltpu.make_async_copy(pick(src, e), dst.at[slot], in_sem.at[i, slot])

        rows_in = [
            pltpu.make_async_copy(n2_hbm, n2_ref, row_sem.at[0]), pltpu.make_async_copy(dy_hbm, dy_ref, row_sem.at[1])
        ]
        weight(0, 0).start()
        rows_in[0].start()
        weight(1, 0).start()
        weight(2, 0).start()
        rows_in[1].start()
        if kept > held:
            for ref in (da, db, gu):
                ref[:, held:] = jnp.zeros((seq, kept - held), bf16)

        def expert(e, carry):
            slot = lax.rem(e, buffers)
            weight(0, e).wait()
            pl.when(e == 0)(rows_in[0].wait)

            def one(i, at):
                a[at, :] = product(n2_ref[at, :], wg[slot])

            tiles(seq // TALL, one, TALL)
            weight(1, e).wait()

            def two(i, at):
                b[at, :] = product(n2_ref[at, :], wu[slot])

            tiles(seq // TALL, two, TALL)
            weight(2, e).wait()
            pl.when(e == 0)(rows_in[1].wait)
            if experts > 1:

                @pl.when(e + 1 < experts)
                def _():
                    for i in range(3):
                        weight(i, e + 1).start()

            def three(i, at):
                back[...] = product(dy_ref[at, :], wd[slot])

                def point(j, carry):
                    row = pl.ds(pl.multiple_of(i * TILE + j * strip, strip), strip)
                    local = pl.ds(pl.multiple_of(j * strip, strip), strip)
                    av, bv, kv, gv = a[row, :], b[row, :], back[local, :], gate_ref[e, row, :]
                    sig = 1.0 / (1.0 + jnp.exp(-av))
                    act = av * sig
                    u = act * bv
                    if shared:
                        column = lax.broadcasted_iota(jnp.int32, (strip, held), 1)
                        mine = jnp.logical_and(column >= skip, column < skip + ffn)
                        u, kv = jnp.where(mine, u, 0.0), jnp.where(mine, kv, 0.0)
                    dgate_ref[e, row, :] = jnp.sum(u * kv, axis=-1, keepdims=True)
                    gu[row, :held] = (gv * u).astype(bf16)
                    du = gv * kv
                    da[row, :held] = (du * bv * (sig + act * (1.0 - sig))).astype(bf16)
                    db[row, :held] = (du * act).astype(bf16)
                    return carry

                lax.fori_loop(0, TILE // strip, point, 0)
                for k, ref in enumerate((da, db, gu)):
                    turned[k, :, at] = ref[at, :held].T

            tiles(count, three)
            saves = [
                pltpu.make_async_copy(src, dst.at[e], out_sem.at[i])
                for i, (src, dst) in enumerate(((da, da_hbm), (db, db_hbm), (gu, gu_hbm)))
            ]
            for save in saves:
                save.start()

            def leave(i):
                slot = lax.rem(i, 2)
                below = pl.ds(pl.multiple_of(e * 3 * ffn, 16), 3 * ffn)
                if per > 1:
                    dst = grad_hbm.at[pl.ds(i * per, per), below]
                else:
                    many = block // TILE
                    to = pl.ds(pl.multiple_of(lax.rem(i, many) * TILE, TILE), TILE)
                    dst = grad_hbm.at[pl.ds(i // many, 1), below, to]
                return pltpu.make_async_copy(slab.at[slot], dst, slab_sem.at[slot])

            def four(i, at):
                slot = lax.rem(i, 2)
                pl.when(i >= 2)(lambda: leave(i).wait())
                for k, right in enumerate((n2_ref, n2_ref, dy_ref)):
                    left = turned[k, pl.ds(pl.multiple_of(skip, 16), ffn), :] if shared else turned[k]
                    value = nn_dot(left, right[:, at]).astype(bf16)
                    for j in range(per):
                        slab[slot, j, k * ffn : (k + 1) * ffn, :] = value[:, j * lane : (j + 1) * lane]
                leave(i).start()

            tiles(slabs, four)
            leave(slabs - 2).wait()
            leave(slabs - 1).wait()
            for save in saves:
                save.wait()
            return carry

        if experts == 1:
            expert(0, 0)
        else:
            lax.fori_loop(0, experts, expert, 0)

    hidden = jax.ShapeDtypeStruct((experts, seq, kept), bf16)
    return pl.pallas_call(
        kernel,
        out_shape=[
            jax.ShapeDtypeStruct((groups, experts * 3 * ffn, block), bf16), hidden, hidden, hidden,
            jax.ShapeDtypeStruct((experts, seq, 1), f32),
        ],
        in_specs=[ANY] * 5 + [VMEM],
        out_specs=[ANY] * 4 + [VMEM],
        scratch_shapes=[
            pltpu.VMEM((seq, width), bf16), pltpu.VMEM((seq, width), bf16),
            pltpu.VMEM((buffers,) + w_shape, bf16), pltpu.VMEM((buffers,) + w_shape, bf16), pltpu.VMEM((buffers,) + w_shape, bf16),
            pltpu.VMEM((seq, held), f32), pltpu.VMEM((seq, held), f32), pltpu.VMEM((TILE, held), f32),
            pltpu.VMEM((seq, kept), bf16), pltpu.VMEM((seq, kept), bf16), pltpu.VMEM((seq, kept), bf16),
            pltpu.VMEM((3, held, seq), bf16),
            pltpu.VMEM((2, per, 3 * ffn, lane), bf16),
            pltpu.SemaphoreType.DMA((3, buffers)), pltpu.SemaphoreType.DMA((2,)), pltpu.SemaphoreType.DMA((3,)),
            pltpu.SemaphoreType.DMA((2,)),
        ],
        compiler_params=pltpu.CompilerParams(vmem_limit_bytes=58 * 1024 * 1024),
    )(n2, dy, *weights, gate)


PART = 512


class Products:
    def __init__(self, nz, experts, shared, extra):
        self.nz, self.experts, self.shared = nz, experts, shared
        _, self.seq, self.kept = experts[0][0][0].shape
        _, self.ffn, self.width = experts[0][1][0].shape
        self.held = shared[0][0][0].shape[2]
        self.own = shared[0][1].shape[1] // nz
        self.more = [] if extra is None else list(extra)
        self.inputs = (
            [left[0] for left, _ in experts] + [right[0] for _, right in experts] + [left[0] for left, _ in shared]
            + [right for _, right in shared] + self.more
        )
        ne, ns = len(experts), len(shared)
        self.specs = [ANY] * (2 * (ne + ns)) + [VMEM] * len(self.more)
        self.scratch = [
            pltpu.VMEM((self.seq, ne * self.kept), bf16), pltpu.VMEM((ne * self.kept, self.width), bf16),
            pltpu.VMEM((self.seq, ns * self.held), bf16), pltpu.VMEM((self.width, ns * self.held), bf16),
            pltpu.SemaphoreType.DMA((self.width // PART, ne + ns)), pltpu.SemaphoreType.DMA((nz, ne + ns)),
        ]

    def bind(self, refs, scratch):
        ne, ns = len(self.experts), len(self.shared)
        self.left, self.right, self.sleft, self.sright, self.r_sem, self.l_sem = scratch
        self.e_left, self.e_right = refs[:ne], refs[ne : 2 * ne]
        self.s_left, self.s_right = refs[2 * ne : 2 * ne + ns], refs[2 * ne + ns : 2 * (ne + ns)]
        self.small = refs[2 * (ne + ns) :]
        self.first = pl.multiple_of(lax.axis_index("expert") * self.own // LANES * LANES, LANES)

    def rights(self, j):
        to = pl.ds(pl.multiple_of(j * PART, PART), PART)
        for i, (_, (_, index)) in enumerate(self.experts):
            dst = self.right.at[pl.ds(i * self.kept, self.ffn), to]
            yield pltpu.make_async_copy(self.e_right[i].at[index, :, to], dst, self.r_sem.at[j, i])
        for i in range(len(self.shared)):
            src = self.s_right[i].at[to, pl.ds(self.first, self.held)]
            dst = self.sright.at[to, pl.ds(i * self.held, self.held)]
            yield pltpu.make_async_copy(src, dst, self.r_sem.at[j, len(self.experts) + i])

    def lefts(self, b):
        rows = self.seq // self.nz
        at = pl.ds(pl.multiple_of(b * rows, rows), rows)
        for i, ((_, index), _) in enumerate(self.experts):
            dst = self.left.at[at, pl.ds(i * self.kept, self.kept)]
            yield pltpu.make_async_copy(self.e_left[i].at[index, at], dst, self.l_sem.at[b, i])
        for i, ((_, index), _) in enumerate(self.shared):
            dst = self.sleft.at[at, pl.ds(i * self.held, self.held)]
            yield pltpu.make_async_copy(self.s_left[i].at[index, at], dst, self.l_sem.at[b, len(self.experts) + i])

    def fetch(self, order):
        for copy in self.lefts(order(0)):
            copy.start()
        for j in range(self.width // PART):
            for copy in self.rights(j):
                copy.start()
        for k in range(1, self.nz):
            for copy in self.lefts(order(k)):
                copy.start()
        if self.kept > self.ffn:
            for i in range(len(self.experts)):
                self.right[i * self.kept + self.ffn : (i + 1) * self.kept, :] = jnp.zeros(
                    (self.kept - self.ffn, self.width), bf16
                )

    def block(self, k, b, out, start, end):
        rows = self.seq // self.nz
        at = pl.ds(pl.multiple_of(b * rows, rows), rows)
        if start == 0:
            for copy in self.lefts(b):
                copy.wait()

        def one(j, carry):
            @pl.when(k == 0)
            def _():
                for copy in self.rights(j):
                    copy.wait()

            to = pl.ds(pl.multiple_of(j * PART, PART), PART)
            value = nn_dot(self.left[at, :], self.right[:, to]) + nt_dot(self.sleft[at, :], self.sright[to, :])
            if self.more:
                value += nt_dot(self.small[0][at, :], self.small[1][to, :])
            out[at, to] = value.astype(bf16)
            return carry

        lax.fori_loop(start, end, one, 0)


def reduce_and_gather(nz, products, h, gain, upstream, name):
    rows, width = h.shape
    n_in, n_scratch = len(products.inputs), len(products.scratch)

    def kernel(*refs):
        p_refs, (h_ref, gain_ref, up_ref, out_ref, dh_ref, gg_ref) = refs[:n_in], refs[n_in : n_in + 6]
        rest = refs[n_in + 6 :]
        p_scratch, (part, own), rest = rest[:n_scratch], rest[n_scratch : n_scratch + 2], rest[n_scratch + 2 :]
        scratch, sems = rest[:REDUCE_SCRATCH], rest[REDUCE_SCRATCH:]
        total = scratch[3]
        products.bind(p_refs, p_scratch)
        reducer = Reducer(nz, part, *scratch)
        products.fetch(reducer.block)
        greet(nz)
        ends = reducer.ends()

        def one(s, carry):
            products.block(s, reducer.block(s), part, 0, 1)
            pl.when(jnp.logical_and(ends, s >= 1))(lambda: reducer.forward(s - 1))
            products.block(s, reducer.block(s), part, 1, width // PART)
            reducer.begin(s)
            pl.when(jnp.logical_and(jnp.logical_not(ends), s >= 2))(lambda: reducer.forward(s - 2))
            return carry

        lax.fori_loop(0, nz, one, 0)
        pl.when(jnp.logical_not(ends))(lambda: reducer.forward(nz - 2))
        reducer.finish()
        gg_ref[...] = jnp.zeros_like(gg_ref)

        def step(at):
            change, along = norm_back(h_ref[at, :], gain_ref[...], total[at, :])
            dh = up_ref[at, :].astype(f32) + change
            dh_ref[at, :] = dh
            own[at, :] = dh.astype(bf16)
            gg_ref[...] += along

        strips(rows, step)
        gather_rows(nz, own, out_ref, *sems)
        reducer.drain()

    return pl.pallas_call(
        kernel,
        out_shape=[
            jax.ShapeDtypeStruct((nz * 2 * rows, width), bf16),
            jax.ShapeDtypeStruct((rows, width), f32),
            jax.ShapeDtypeStruct((STRIP, width), f32),
        ],
        in_specs=products.specs + [VMEM] * 3,
        out_specs=[ANY, VMEM, VMEM],
        scratch_shapes=products.scratch
        + [pltpu.VMEM((nz * 2 * rows, width), bf16), pltpu.VMEM((rows, width), bf16)]
        + reduce_scratch(nz, rows, width)
        + gather_sems(nz),
        compiler_params=params(name),
    )(*products.inputs, h, gain, upstream)


def reduce_last(nz, d_heads, weights, x, gain, dh, products, h, name):
    rows, width = x.shape
    n_in, n_scratch = len(products.inputs), len(products.scratch)

    def kernel(*refs):
        p_refs, (d_ref, w_ref, x_ref, gain_ref, dh_ref, h_ref, in_ref, out_ref, gg_ref) = (
            refs[:n_in], refs[n_in : n_in + 9],
        )
        rest = refs[n_in + 9 :]
        p_scratch, (d_part, b_part, own, sems), rest = (
            rest[:n_scratch], rest[n_scratch : n_scratch + 4], rest[n_scratch + 4 :],
        )
        d_scratch, b_scratch = rest[:REDUCE_SCRATCH], rest[REDUCE_SCRATCH:]
        d_total, b_total = d_scratch[3], b_scratch[3]
        products.bind(p_refs, p_scratch)
        first, second = Reducer(nz, d_part, *d_scratch), Reducer(nz, b_part, *b_scratch)
        products.fetch(second.block)
        greet(nz)
        z, c = here()
        ends = first.ends()
        middle = jnp.logical_not(ends)

        def inner(block):
            at = pl.ds(pl.multiple_of(block * 2 * rows, 2 * rows), 2 * rows)

            def one(j, carry):
                to = pl.ds(pl.multiple_of(j * PART, PART), PART)
                d_part[at, to] = nt_dot(d_ref[at, :], w_ref[to, :]).astype(bf16)
                return carry

            lax.fori_loop(0, width // PART, one, 0)

        def one(s, carry):
            inner(first.block(s))
            first.begin(s)
            pl.when(jnp.logical_and(ends, s >= 1))(lambda: first.forward(s - 1))
            return carry

        def two(s, carry):
            products.block(s, second.block(s), b_part, 0, width // PART)
            second.begin(s)

            @pl.when(s >= 1)
            def _():
                pl.when(ends)(lambda: second.forward(s - 1))
                pl.when(middle)(lambda: first.forward(s - 1))

            return carry

        def three(s, carry):
            pl.when(middle)(lambda: second.forward(s))
            return carry

        lax.fori_loop(0, nz, one, 0)
        lax.fori_loop(0, nz, two, 0)
        lax.fori_loop(0, nz - 1, three, 0)
        first.finish()
        gg_ref[...] = jnp.zeros_like(gg_ref)

        def step(at):
            change, along = norm_back(x_ref[at, :].astype(f32), gain_ref[...], d_total[at, :])
            own[0, at, :] = dh_ref[at, :] + change
            gg_ref[...] += along

        strips(rows, step)

        def leave(i, ref):
            spot = ref.at[pl.ds(pl.multiple_of(c * rows, rows), rows)]
            return (
                pltpu.make_async_copy(own.at[i], spot, sems.at[i, 0]),
                remote(own.at[i], spot, sems.at[i, 1], sems.at[i, 2], {"tensor": 1 - c}),
            )

        for copy in leave(0, in_ref):
            copy.start()
        second.finish()

        def last(at):
            own[1, at, :] = h_ref[at, :] + b_total[at, :]

        strips(rows, last)
        for copy in leave(1, out_ref):
            copy.start()
        first.drain()
        second.drain()
        for copy in (*leave(0, in_ref), *leave(1, out_ref)):
            copy.wait()

    return pl.pallas_call(
        kernel,
        out_shape=[
            jax.ShapeDtypeStruct((2 * rows, width), f32),
            jax.ShapeDtypeStruct((2 * rows, width), f32),
            jax.ShapeDtypeStruct((STRIP, width), f32),
        ],
        in_specs=products.specs + [VMEM] * 6,
        out_specs=[ANY, ANY, VMEM],
        scratch_shapes=products.scratch
        + [
            pltpu.VMEM((nz * 2 * rows, width), bf16), pltpu.VMEM((nz * 2 * rows, width), bf16),
            pltpu.VMEM((2, rows, width), f32), pltpu.SemaphoreType.DMA((2, 3)),
        ]
        + reduce_scratch(nz, rows, width) * 2,
        compiler_params=params(name),
    )(*products.inputs, d_heads, weights, x, gain, dh, h)


def assemble(nz, box, columns):
    block = box.shape[2]
    count = 3

    def kernel(box_ref, *outs):
        for k in range(count):
            for b in range(nz):
                value = box_ref[b, k * columns : (k + 1) * columns, :].astype(f32).T
                outs[k][:, b * columns : (b + 1) * columns] = value

    return pl.pallas_call(
        kernel,
        out_shape=[jax.ShapeDtypeStruct((block, nz * columns), f32)] * count,
        in_specs=[VMEM],
        out_specs=[VMEM] * count,
        compiler_params=pltpu.CompilerParams(vmem_limit_bytes=40 * 1024 * 1024),
    )(box)


def finish_gradients(nz, part, splits, small, experts, name):
    n, rows, lanes = small.shape
    block = part.shape[0] // nz
    cols = part.shape[1] // splits
    local, kinds, ffn, width = experts.shape

    def kernel(part_ref, small_ref, experts_ref, *rest):
        outs, (sum_ref,), e_outs = rest[:splits], rest[splits : splits + 1], rest[splits + 1 : splits + 1 + kinds]
        (box, s_box, total, other, wide, send_sem, recv_sem, s_send, s_recv, swap_sem, out_sem) = rest[splits + 1 + kinds :]
        z, c = here()
        me = lax.axis_index("dp") * nz + z
        barrier = pltpu.get_barrier_semaphore()

        def peer(k):
            at = lax.rem(me + k, n)
            return at, {"dp": at // nz, "expert": lax.rem(at, nz)}

        pl.semaphore_signal(barrier, inc=1, device_id={"tensor": 1 - c}, device_id_type=MESH)
        for k in range(1, n):
            pl.semaphore_signal(barrier, inc=1, device_id=peer(k)[1], device_id_type=MESH)
        pl.semaphore_wait(barrier, n)

        def send(way, d):
            to = z + d if way == UP else z - d
            src = part_ref.at[pl.ds(pl.multiple_of(to * block, block), block)]
            return remote(src, box.at[z], send_sem.at[way, d], recv_sem.at[way, d], {"expert": to})

        def take(way, d):
            dst = box.at[z - d if way == UP else z + d]
            remote(dst, dst, send_sem.at[way, d], recv_sem.at[way, d], {"tensor": 1 - c}).wait_recv()

        def send_small(k):
            at, device = peer(k)
            return remote(small_ref.at[at], s_box.at[k], s_send.at[k], s_recv.at[k], device)

        for k in range(1, n):
            send_small(k).start()
        for d in range(nz - 1, 0, -1):
            for way in (UP, DOWN):
                pl.when(z + d < nz if way == UP else z >= d)(lambda way=way, d=d: send(way, d).start())
        box[z] = part_ref[pl.ds(pl.multiple_of(z * block, block), block), :]
        leaves = [pltpu.make_async_copy(wide.at[i], e_outs[i], out_sem.at[i]) for i in range(kinds)]
        for i in range(kinds):
            for e in range(local):
                def widen(at, i=i, e=e):
                    wide[i, e, at, :] = experts_ref[e, i, at, :].astype(f32)

                strips(ffn, widen)
            leaves[i].start()
        total[...] = small_ref[me]
        for k in range(1, n):
            send_small(k).wait_recv()
            total[...] += s_box[k]
        swap = remote(total, other, swap_sem.at[0], swap_sem.at[1], {"tensor": 1 - c})
        swap.start()
        swap.wait_recv()
        sum_ref[...] = total[...] + other[...]
        for d in range(1, nz):
            for way in (UP, DOWN):
                pl.when(z >= d if way == UP else z + d < nz)(lambda way=way, d=d: take(way, d))
        for j in range(splits):
            for b in range(nz):
                outs[j][:, b * cols : (b + 1) * cols] = box[b, :, j * cols : (j + 1) * cols].astype(f32)
        swap.wait_send()
        for k in range(1, n):
            send_small(k).wait_send()
        for d in range(1, nz):
            for way in (UP, DOWN):
                pl.when(z + d < nz if way == UP else z >= d)(lambda way=way, d=d: send(way, d).wait_send())
        for leave in leaves:
            leave.wait()

    return pl.pallas_call(
        kernel,
        out_shape=[jax.ShapeDtypeStruct((block, nz * cols), f32)] * splits
        + [jax.ShapeDtypeStruct((rows, lanes), f32)]
        + [jax.ShapeDtypeStruct((local, ffn, width), f32)] * kinds,
        in_specs=[VMEM] * 3,
        out_specs=[VMEM] * (splits + 1) + [ANY] * kinds,
        scratch_shapes=[
            pltpu.VMEM((nz, block, part.shape[1]), bf16), pltpu.VMEM((n, rows, lanes), f32),
            pltpu.VMEM((rows, lanes), f32), pltpu.VMEM((rows, lanes), f32),
            pltpu.VMEM((kinds, local, ffn, width), f32),
            pltpu.SemaphoreType.DMA((2, nz)), pltpu.SemaphoreType.DMA((2, nz)),
            pltpu.SemaphoreType.DMA((n,)), pltpu.SemaphoreType.DMA((n,)), pltpu.SemaphoreType.DMA((2,)),
            pltpu.SemaphoreType.DMA((kinds,)),
        ],
        compiler_params=params(name),
    )(part, small, experts)


def cross_rows(left, right):
    return lax.dot_general(left, right, (((0,), (0,)), ((), ())), preferred_element_type=f32)


def cross_cols(left, right):
    return lax.dot_general(left, right, (((1,), (1,)), ((), ())), preferred_element_type=f32)


def dot(left, right):
    return jnp.dot(left, right, preferred_element_type=f32)


def two_parts(values):
    high = values.astype(bf16)
    return high, (values - high.astype(f32)).astype(bf16)


def body(
    tokens, segments, routes, norm1_gain, q_weight, k_weight, v_weight, o_weight, norm2_gain,
    router_weight, shared_gate_vector, shared_gate_weight, shared_up_weight, shared_down_weight,
    expert_gate_weight, expert_up_weight, expert_down_weight, out_grad,
):
    nz = lax.axis_size("expert")
    nc = lax.axis_size("tensor")
    z = lax.axis_index("expert")
    c = lax.axis_index("tensor")
    rows, width = tokens.shape
    own_rows = rows // nc
    local_count, _, ffn = expert_gate_weight.shape
    expert_count = local_count * nz
    head_cols = q_weight.shape[1] // nz
    shared_cols = shared_gate_weight.shape[1] // nz
    heads = head_cols // HD
    seq = rows * nz
    scale = HD ** (-0.5)
    gain1 = norm1_gain.astype(f32)[None]
    gain2 = norm2_gain.astype(f32)[None]

    def own(values):
        return lax.dynamic_slice_in_dim(values, c * own_rows, own_rows, 0)

    def head_slice(values):
        return lax.dynamic_slice_in_dim(values, z * head_cols, head_cols, 1)

    x_all_rows = tokens.astype(f32)
    inverse_one_rows = lax.rsqrt(jnp.mean(x_all_rows * x_all_rows, axis=-1) + epsilon)
    x = own(tokens)
    marks = jnp.concatenate([segments, routes.T, jnp.zeros((7 - routes.shape[1], rows), jnp.int32)], axis=0)
    upstream = own(out_grad)
    n1, dy, all_marks, qkv, p_low, o, n2, h, inverse_two = attend(
        nz, x, gain1, upstream, marks, (q_weight, k_weight, v_weight), o_weight, gain2, 0
    )
    all_routes = jnp.transpose(all_marks[:, 1 : 1 + routes.shape[1]], (0, 2, 1)).reshape(seq, routes.shape[1])
    wo = head_slice(o_weight)
    w_heads = jnp.concatenate([head_slice(q_weight), head_slice(k_weight), head_slice(v_weight)], axis=1)
    q, k, v = (qkv[:, i * head_cols : (i + 1) * head_cols].reshape(seq, heads, HD) for i in range(3))
    probs = jax.nn.softmax(dot(n2, router_weight), axis=-1)
    chosen = jnp.any(all_routes[:, :, None] == jnp.arange(expert_count)[None, None, :], axis=1)
    gates = jnp.where(chosen, probs, 0.0)
    sigma = jax.nn.sigmoid(dot(n2, shared_gate_vector))

    turned = [jnp.swapaxes(w, 1, 2) for w in (expert_gate_weight, expert_up_weight, expert_down_weight)]
    shared_weights = (shared_gate_weight, shared_up_weight, shared_down_weight)
    ndp = lax.axis_size("dp")
    grad_s, da_s, db_s, gu_s, dgate_s = hidden_layer(nz, n2, dy, sigma[None, :, None], shared_weights, ndp * nz)
    n2_now, dgate_s = lax.optimization_barrier((n2, dgate_s))
    gate = jnp.swapaxes(lax.dynamic_slice_in_dim(gates, z * local_count, local_count, 1), 0, 1)[:, :, None]
    grad_e, da_e, db_e, gu_e, dgate_e = hidden_layer(nz, n2_now, dy, gate, turned, ndp)

    d_expert = jnp.swapaxes(dgate_e[:, :, 0], 0, 1)
    d_probs = lax.dynamic_update_slice_in_dim(jnp.zeros_like(probs), d_expert, z * local_count, 1)
    d_probs = jnp.where(chosen, d_probs, 0.0)
    d_logits = probs * (d_probs - jnp.sum(probs * d_probs, axis=-1, keepdims=True))
    d_vector = dgate_s[0] * (sigma * (1.0 - sigma))[:, None]
    small = jnp.concatenate([d_logits, d_vector], axis=1)
    small_high, small_low = two_parts(small)
    small_weights = jnp.concatenate([router_weight, shared_gate_vector[:, None]], axis=1)
    fill = ((0, 0), (0, 128 - small.shape[1]))
    experts = range(local_count)
    d_n2 = Products(
        nz,
        [((da_e, i), (turned[0], i)) for i in experts] + [((db_e, i), (turned[1], i)) for i in experts],
        [((da_s, 0), shared_gate_weight), ((db_s, 0), shared_up_weight)],
        (jnp.pad(small_high, fill), jnp.pad(small_weights, fill)),
    )
    small_grad = cross_rows(n2, jnp.concatenate([small_high, small_low], axis=1))
    small_grad = small_grad[:, : expert_count + 1] + small_grad[:, expert_count + 1 :]


    def over_dp(grad):
        rows = grad.reshape(-1, grad.shape[-1])
        return lax.psum_scatter(rows, "dp", scatter_dimension=0, tiled=True)

    shared_part = over_dp(grad_s).reshape((nz,) + grad_s.shape[1:])
    expert_part = over_dp(grad_e).reshape(local_count, 3, ffn, -1)
    dhr, dh, grad_two = reduce_and_gather(nz, d_n2, h, gain2, upstream, 2)
    shared_part, dhr = lax.optimization_barrier((shared_part, dhr))
    shared_box = lax.all_to_all(shared_part, "expert", split_axis=0, concat_axis=0, tiled=True)
    d_o = dot(dhr, wo).astype(bf16).reshape(seq, heads, HD)
    grad_o = cross_rows(dhr, o)

    d_v = jnp.einsum("hqk,qhd->khd", p_low, d_o, preferred_element_type=f32)
    dp = jnp.einsum("qhd,khd->hqk", d_o, v, preferred_element_type=f32)
    mean = jnp.sum(d_o.astype(f32) * o.reshape(seq, heads, HD).astype(f32), axis=-1).T
    ds = (p_low.astype(f32) * (dp - mean[:, :, None])).astype(bf16)
    d_q = jnp.einsum("hqk,khd->qhd", ds, k, preferred_element_type=f32) * scale
    d_k = jnp.einsum("hqk,qhd->khd", ds, q, preferred_element_type=f32) * scale
    d_heads = jnp.concatenate([t.reshape(seq, head_cols).astype(bf16) for t in (d_q, d_k, d_v)], axis=1)
    s_gate, s_up, s_down = assemble(nz, shared_box, shared_cols)
    d_heads, s_gate = lax.optimization_barrier((d_heads, s_gate))
    grad_attention = jnp.concatenate(
        [cross_rows(n1, d_heads).astype(bf16), grad_o.astype(bf16)], axis=1
    )
    attention_part = over_dp(grad_attention)
    branch = Products(
        nz,
        [((gu_e, i), (turned[2], i)) for i in experts],
        [((gu_s, 0), shared_down_weight)],
        None,
    )
    dh_now, _ = lax.optimization_barrier((dh, grad_attention))
    input_grad, layer_out, grad_one = reduce_last(
        nz, d_heads, w_heads, x, gain1, dh_now, branch, h, 3
    )
    stats = jnp.stack([inverse_one_rows, inverse_two[:, 0]])

    small_rows = jnp.concatenate(
        [
            jnp.sum(grad_one, axis=0)[None], jnp.sum(grad_two, axis=0)[None], small_grad.T,
            jnp.zeros((13 - expert_count, width), f32),
        ],
        axis=0,
    )
    small_rows, expert_part = lax.optimization_barrier((small_rows, expert_part))
    count = ndp * nz
    small_blocks = jnp.swapaxes(small_rows.reshape(16, count, width // count), 0, 1)
    g_q, g_k, g_v, g_o, small_all, *wide = finish_gradients(nz, attention_part, 4, small_blocks, expert_part, 6)
    e_gate, e_up, e_down = (jnp.swapaxes(t, 1, 2) for t in wide)
    g_one, g_two, g_router, g_vector = small_all[0], small_all[1], small_all[2 : 2 + expert_count].T, small_all[2 + expert_count]
    return (
        layer_out, input_grad, stats, g_one, g_q, g_k, g_v, g_o, g_two, g_router, g_vector,
        s_gate, s_up, s_down, e_gate, e_up, e_down,
    )


def solution(mesh):
    both = ("dp", "expert")
    cols = P(None, "tensor")
    placed = (
        P(both, None), P("dp", "expert"), P(both, None), P(), cols, cols, cols, cols, P(), P(), P(),
        cols, cols, cols, P("expert", None, "tensor"), P("expert", None, "tensor"),
        P("expert", None, "tensor"), P(both, None),
    )
    split = P(both, "tensor")
    experts = P("expert", "dp", "tensor")
    return jax.shard_map(
        body,
        mesh=mesh,
        in_specs=placed,
        out_specs=(
            P(both, None), P(both, None), P(None, both), P(both), split, split, split, split, P(both),
            P(both, None), P(both), split, split, split, experts, experts, experts,
        ),
        check_vma=False,
    )
```

profile of v0, /device:TPU:8, one launch (start us, length us, event | category | flops | bytes accessed | tf_op | source)
XLA Modules:
  0.0 568.7 jit_solution(8892041461808085679)
XLA Ops:
  8.0 1.3 broadcast_in_dim.58
  9.3 1.3 broadcast_in_dim.59
  10.6 1.4 add_add_fusion.marks_ref
  12.0 2.3 constant_dynamic-slice_fusion.3
  14.2 132.5 %shard_map.305 = (bf16[1024,2048]{1,0:T(8,128)(2,1)}, bf16[1024,2048]{1,0:T(8,128)(2,1)}, s32[4,8,256]{2,1,0:T(8,128)}, bf16[1024,768]{1,0:T(8,128)(2,1)}, bf16[...) custom-call(bf16[128,2048]{1,0:T(8,128)(2,1)} %get-tuple-element.118, ...), custom_call_target="tpu_custom_call" | custom-call | tf_op jit(solution)/shard_map/pallas_call | solution.py:520
  146.7 3.4 fusion.23
  150.1 1.1 copy.123.gate_ref
  151.2 34.6 %shard_map.306 = (bf16[16,2112,128]{2,1,0:T(8,128)(2,1)}, bf16[1,1024,768]{2,1,0:T(8,128)(2,1)}, bf16[1,1024,768]{2,1,0:T(8,128)(2,1)}, bf16[1,1024,768]{2,1,0:T(8,128)(2,1)}, f32[1,1024,1]{2,1,0:T(8,128)}) custom-call(bf16[1024,2048]{1,0:T(8,128)(2,1)} %get-tuple-element.65.n2_hbm, bf16[1024,2048]{1,0:T(8,128)(2,1)} %get-tuple-element.63.dy_hbm, ...), custom_call_target="tpu_custom_call" | custom-call | tf_op jit(solution)/shard_map/pallas_call | solution.py:737
  186.5 3.4 fusion.22
  190.0 1.3 copy.124.gate_ref
  191.4 62.2 %shard_map.307 = (bf16[4,4224,512]{2,1,0:T(8,128)(2,1)}, bf16[2,1024,768]{2,1,0:T(8,128)(2,1)}, bf16[2,1024,768]{2,1,0:T(8,128)(2,1)}, bf16[2,1024,768]{2,1,0:T(8,128)(2,1)}, f32[2,1024,1]{2,1,0:T(8,128)}) custom-call(bf16[1024,2048]{1,0:T(8,128)(2,1)} %get-tuple-element.65.n2_hbm, bf16[1024,2048]{1,0:T(8,128)(2,1)} %get-tuple-element.63.dy_hbm, ...), custom_call_target="tpu_custom_call" | custom-call | tf_op jit(solution)/shard_map/pallas_call | solution.py:737
  255.7 0.9 pad.9.refs_13_
  257.4 91.5 %shard_map.308 = (bf16[1024,2048]{1,0:T(8,128)(2,1)}, f32[128,2048]{1,0:T(8,128)}, f32[16,2048]{1,0:T(8,128)}) custom-call(bf16[2,1024,768]{2,1,0:T(8,128)(2,1)} %get-tuple-element.72.refs_0_.refs_1_, bf16[2,1024,768]{2,1,0:T(8,128)(2,1)} %get-tuple-element.72.refs_0_.refs_1_, bf16[2,1024,768]{2,1,0:T(8,128)(2,1)} %get-tuple-element.73.refs_2_.refs_3_, ...), custom_call_target="tpu_custom_call" | custom-call | tf_op jit(solution)/shard_map/pallas_call | solution.py:888
  348.9 7.7 %all-to-all-start = ((bf16[4,2112,128]{2,1,0:T(8,128)(2,1)}), bf16[4,2112,128]{2,1,0:T(8,128)(2,1)S(1)}, u32[]{:S(2)}, u32[]{:S(2)}) async-start(bf16[4,2112,128]{2,1,0:T(8,128)(2,1)} %bitcast.101), calls=%async_computation.1 | async-start | bytes 4325376 | tf_op jit(solution)/shard_map/all_to_all | solution.py:1219
  356.7 1.2 copy.142
  357.9 2.3 fusion.21
  360.2 1.0 copy.141
  361.4 4.5 multiply_reduce_fusion.1
  366.0 2.2 multiply_convert_fusion
  368.2 1.9 copy-done.1
  370.1 2.3 fusion
  372.5 2.0 copy.143
  374.5 3.7 fusion.1
  378.2 2.0 copy.145
  380.2 2.9 convolution_convert_fusion.2
  383.4 2.4 pad_maximum_fusion.2.refs_6_
  385.8 3.6 convolution_convert_fusion.1
  389.4 14.4 %all-to-all-done.box_ref = bf16[4,2112,128]{2,1,0:T(8,128)(2,1)S(1)} async-done(((bf16[4,2112,128]{2,1,0:T(8,128)(2,1)}), bf16[4,2112,128]{2,1,0:T(8,128)(2,1)S(1)}, u32[]{:S(2)}, u32[]{:S(2)}) %all-to-all-start) | async-done | bytes 2162720 | tf_op jit(solution)/shard_map/all_to_all | solution.py:1219
  403.8 2.8 shard_map.309
  406.7 6.2 %convolution_convert_fusion = bf16[2048,768]{1,0:T(8,128)(2,1)S(1)} fusion(bf16[1024,2048]{1,0:T(8,128)(2,1)} %get-tuple-element.86, bf16[1024,768]{1,0:T(8,128)(2,1)} %pad_maximum_fusion.2.refs_6_), kind=kOutput, calls=%fused_computation.2 | convolution fusion | flops 3222798336 | bytes 8912896 | tf_op jit(solution)/shard_map/dot_general | solution.py:1123
  412.9 2.6 pad_maximum_fusion
  415.4 0.9 copy-done.20
  417.7 1.5 constant_dynamic-slice_fusion.2
  419.2 1.7 constant_dynamic-slice_fusion
  420.9 1.8 pad_maximum_fusion.1.refs_7_
  422.7 1.6 copy-done
  425.0 84.4 %shard_map.310 = (f32[256,2048]{1,0:T(8,128)}, f32[256,2048]{1,0:T(8,128)}, f32[16,2048]{1,0:T(8,128)}) custom-call(bf16[2,1024,768]{2,1,0:T(8,128)(2,1)} %get-tuple-element.67.refs_0_.refs_1_, bf16[2,1024,768]{2,1,0:T(8,128)(2,1)} %get-tuple-element.67.refs_0_.refs_1_, bf16[2,704,2048]{2,1,0:T(8,128)(2,1)} %bitcast.93, bf16[2,704,2048]{2,1,0:T(8,128)(2,1)} %bitcast.94, ...), custom_call_target="tpu_custom_call" | custom-call | tf_op jit(solution)/shard_map/pallas_call | solution.py:993
  509.4 0.9 reduce_sum.58
  511.2 36.3 %shard_map.311 = (f32[128,1024]{1,0:T(8,128)}, f32[128,1024]{1,0:T(8,128)}, f32[128,1024]{1,0:T(8,128)}, f32[128,1024]{1,0:T(8,128)}, f32[16,128]{1,0:T(8,128)},...) custom-call(bf16[512,1024]{1,0:T(8,128)(2,1)} %reduce-scatter.6.cloned.1.call-done.part_ref, ...), custom_call_target="tpu_custom_call" | custom-call | tf_op jit(solution)/shard_map/pallas_call | solution.py:1103
  547.5 1.3 slice_bitcast_fusion.2
  548.8 1.3 slice_bitcast_fusion.1
  550.1 1.3 copy.164
  551.4 1.3 copy.165
  552.7 0.8 copy.166
  555.9 1.6 copy.170
  557.5 1.6 copy.171
  559.1 1.3 copy-done.3
  560.3 1.6 copy.172
  (87 shorter events, 10.1 us)
Async XLA Ops:
  7.2 341.8 %reduce-scatter.4.cloned.1.call-start = ((), (), s32[]{:S(2)}) async-start(), calls=%async_computation.4 | async-start | bytes 10813440 | tf_op jit(solution)/shard_map/reduce_scatter | solution.py:1213
  185.8 0.8 copy-start.21
  185.8 0.8 copy-start.18
  185.8 324.7 %reduce-scatter.8.cloned.1.call-start = ((), (), s32[]{:S(2)}) async-start(), calls=%async_computation.6 | async-start | bytes 21626880 | tf_op jit(solution)/shard_map/reduce_scatter | solution.py:1213
  253.6 1.0 copy-start.13
  253.7 1.4 copy-start.11
  348.9 7.8 %copy-start.12 = (bf16[1024,256]{1,0:T(8,128)(2,1)S(1)}, bf16[1024,256]{1,0:T(8,128)(2,1)}, u32[]{:S(2)}) copy-start(bf16[1024,256]{1,0:T(8,128)(2,1)} %get-tuple-element.81) | copy-start | bytes 1572868
  348.9 54.9 %all-to-all-start = ((bf16[4,2112,128]{2,1,0:T(8,128)(2,1)}), bf16[4,2112,128]{2,1,0:T(8,128)(2,1)S(1)}, u32[]{:S(2)}, u32[]{:S(2)}) async-start(bf16[4,2112,128]{2,1,0:T(8,128)(2,1)} %bitcast.101), calls=%async_computation.1 | async-start | bytes 4325376 | tf_op jit(solution)/shard_map/all_to_all | solution.py:1219
  356.7 154.5 %reduce-scatter.6.cloned.1.call-start = ((), (), s32[]{:S(2)}) async-start(), calls=%async_computation.5 | async-start | bytes 5242880 | tf_op jit(solution)/shard_map/reduce_scatter | solution.py:1213
  361.4 4.6 copy-start.2
  361.4 4.6 copy-start.10
  366.0 4.2 copy-start.7
  368.2 2.0 copy-start.1
  415.4 0.9 copy-start.20
  415.4 1.0 copy-start.19
  415.4 1.4 copy-start.6
  420.9 3.4 copy-start
  511.1 40.2 %copy-start.8 = (f32[256,2048]{1,0:T(8,128)S(1)}, f32[256,2048]{1,0:T(8,128)}, u32[]{:S(2)}) copy-start(f32[256,2048]{1,0:T(8,128)} %get-tuple-element.139) | copy-start | bytes 6291460
  511.2 38.9 %copy-start.9 = (f32[256,2048]{1,0:T(8,128)S(1)}, f32[256,2048]{1,0:T(8,128)}, u32[]{:S(2)}) copy-start(f32[256,2048]{1,0:T(8,128)} %get-tuple-element.138) | copy-start | bytes 6291460
  550.1 2.7 copy-start.17
  550.1 3.5 copy-start.16
  551.4 2.9 copy-start.15
  551.4 3.7 copy-start.14
  551.4 4.5 copy-start.5
  554.3 3.2 copy-start.4
  557.5 2.9 copy-start.3
Sparse Core Ops, SparseCore 0:
  185.9 91.1 reduce-scatter.3
  280.2 158.0 reduce-scatter.7
  441.6 52.6 reduce-scatter.5
where the time goes:
time: 578 us; the launch traced here: 569 us
  Pallas kernels  444 us (77%)
  local copies, waits for them, and re-layouts  40.9 us (7%)
  matrix products  32.9 us (6%)
  waiting for transfers between devices  14.4 us (2%)
  between operations  14.4 us (2%)
  other arithmetic  13.4 us (2%)
  starting transfers between devices  8.15 us (1%)
    pallas_call x1, Pallas kernels, attend(): pl.pallas_call(kernel, out_shape=[jax.ShapeDtypeStruct((seq, width), bf16...  132 us
    pallas_call x2, Pallas kernels, hidden_layer(): pl.pallas_call(kernel, out_shape=[jax.ShapeDtypeStruct((groups, experts *...  96.8 us
    pallas_call x1, Pallas kernels, reduce_and_gather(): pl.pallas_call(kernel, out_shape=[jax.ShapeDtypeStruct((nz * 2 * rows, wi...  91.5 us
    pallas_call x1, Pallas kernels, reduce_last(): pl.pallas_call(kernel, out_shape=[jax.ShapeDtypeStruct((2 * rows, width),...  84.4 us
    pallas_call x1, Pallas kernels, finish_gradients(): pl.pallas_call(kernel, out_shape=[jax.ShapeDtypeStruct((block, nz * cols)...  36.3 us
    unnamed x54, local copies, waits for them, and re-layouts  18.4 us
    all_to_all x1, waiting for transfers between devices, body(): lax.all_to_all(shared_part, 'expert', split_axis=0, concat_axis=0, tiled=...  14.4 us
  transfers between devices with their start and end apart: 4, of which 1 were waited for; matrix products, arithmetic and copies ran while one was open for 10% of the time, Pallas kernels for 42%

commit v1 on v0

--- a/solution.py
+++ b/solution.py
@@ -124,9 +124,20 @@
                 pl.when(self.onward(way))(lambda: self.along(way, d, p).start())
                 self.across(way, d, p).start()
 
+    def settle(self, way, d):
+        for p in range(PIECES):
+            self.crossed(way, d, p)
+        if d == 0:
+            self.mine().wait()
+
+    def settle_all(self):
+        self.settle(UP, 0)
+        for d in range(1, self.nz):
+            for way in (UP, DOWN):
+                pl.when(self.inside(way, d))(functools.partial(self.settle, way, d))
+
     def finish(self):
         for p in range(PIECES):
-            self.crossed(UP, 0, p)
             self.across(UP, 0, p).wait_send()
             for way in (UP, DOWN):
                 pl.when(self.onward(way))(lambda way=way, p=p: self.along(way, 0, p).wait_send())
@@ -134,11 +145,8 @@
 
                     @pl.when(self.inside(way, d))
                     def _(way=way, d=d, p=p):
-                        self.crossed(way, d, p)
                         self.across(way, d, p).wait_send()
                         pl.when(self.onward(way))(lambda: self.along(way, d, p).wait_send())
-
-        self.mine().wait()
 
 
 def gather_rows(nz, own, out, *sems):
@@ -149,6 +157,7 @@
     for d in range(1, nz):
         for p in range(PIECES):
             gather.event(d, p)
+    gather.settle_all()
     gather.finish()
 
 
@@ -309,252 +318,6 @@
     return change, upstream * values * inverse
 
 
-def attend(nz, x, gain, upstream, marks, weights, out_weight, gain2, name):
-    rows, width = x.shape
-    seq = nz * 2 * rows
-    cols = weights[0].shape[1] // nz
-    heads = cols // HD
-    full = 2 * rows
-    strip = 32
-    scale = HD ** (-0.5)
-
-    def kernel(x_ref, gain_ref, up_ref, marks_ref, gain2_ref, wq_hbm, wk_hbm, wv_hbm, wo_hbm, n1_ref, dy_ref, all_ref, qkv_ref,
-               p_ref, o_ref, n2_ref, h_ref, inv_ref, own, w, scores, seg_q, seg_k, heads_in, acc, give, take_in, own2, inv_own, wo,
-               w_sem, m_send, m_recv, m_local, a_send, a_recv, e_send, e_recv, i_sems, *sems):
-        z, c = here()
-        at = pl.ds(pl.multiple_of(z * cols, cols), cols)
-        loads = [
-            pltpu.make_async_copy(src.at[:, at], w.at[:, pl.ds(i * cols, cols)], w_sem.at[i])
-            for i, src in enumerate((wq_hbm, wk_hbm, wv_hbm))
-        ]
-        loads.append(pltpu.make_async_copy(wo_hbm, wo, w_sem.at[3]))
-        for load in loads:
-            load.start()
-
-        def step(strip_at):
-            normed, _ = norm_rows(x_ref[strip_at, :].astype(f32), gain_ref[...])
-            own[strip_at, :] = normed.astype(bf16)
-
-        strips(rows, step)
-        greet(nz)
-        n1 = Gather(nz, own, n1_ref, *sems[:5])
-        dy = Gather(nz, up_ref, dy_ref, *sems[5:10])
-        n2 = Gather(nz, own2, n2_ref, *sems[10:])
-        n1.start_along(UP)
-        n1.start_along(DOWN)
-        n1.start_across()
-        keep = pltpu.make_async_copy(marks_ref, all_ref.at[z], m_local)
-        keep.start()
-
-        def send(way, d):
-            to = z + d if way == UP else z - d
-            return remote(marks_ref, all_ref.at[z], m_send.at[way, d], m_recv.at[way, d], {"expert": to})
-
-        def take(way, d):
-            dst = all_ref.at[z - d if way == UP else z + d]
-            remote(dst, dst, m_send.at[way, d], m_recv.at[way, d], {"tensor": 1 - c}).wait_recv()
-
-        for d in range(1, nz):
-            for way in (UP, DOWN):
-                pl.when(z + d < nz if way == UP else z >= d)(lambda way=way, d=d: send(way, d).start())
-
-        def follow(d):
-            pl.when(z == d)(lambda: dy.start_along(UP))
-            pl.when(nz - 1 - z == d)(lambda: dy.start_along(DOWN))
-
-        follow(0)
-        for d in range(1, nz):
-            for p in range(PIECES):
-                n1.event(d, p)
-            follow(d)
-        dy.start_across()
-        keep.wait()
-        for d in range(1, nz):
-            for way in (UP, DOWN):
-                pl.when(z + d < nz if way == UP else z >= d)(lambda way=way, d=d: send(way, d).wait_send())
-                pl.when(z >= d if way == UP else z + d < nz)(lambda way=way, d=d: take(way, d))
-        n1.finish()
-        for load in loads:
-            load.wait()
-
-        def project(first, last):
-            def one(i, carry):
-                to = pl.ds(pl.multiple_of(i * full, full), full)
-                qkv_ref[to, :] = jnp.dot(n1_ref[to, :], w[...], preferred_element_type=f32).astype(bf16)
-                return carry
-
-            lax.fori_loop(first, last, one, 0)
-
-        def label():
-            for b in range(nz):
-                some = all_ref[b].astype(f32)
-                seg_q[b * full : (b + 1) * full, :] = some.T[:, :1]
-                seg_k[:, b * full : (b + 1) * full] = some[:1, :]
-
-        def head(i):
-            length = (i + 1) * full
-
-            def one(h, carry):
-                def part(k):
-                    return pl.ds(pl.multiple_of(k * cols + h * HD, HD), HD)
-
-                base = i * full
-                scores[:, :length] = lax.dot_general(
-                    qkv_ref[base : base + full, part(0)], qkv_ref[:length, part(1)], (((1,), (1,)), ((), ())),
-                    preferred_element_type=f32,
-                )
-
-                def soften(j, inner):
-                    local = pl.ds(pl.multiple_of(j * strip, strip), strip)
-                    row = pl.ds(pl.multiple_of(base + j * strip, strip), strip)
-                    place_q = base + j * strip + lax.broadcasted_iota(jnp.int32, (strip, length), 0)
-                    place_k = lax.broadcasted_iota(jnp.int32, (strip, length), 1)
-                    allowed = jnp.logical_and(place_k <= place_q, seg_k[:, :length] == seg_q[row, :])
-                    value = jnp.where(allowed, scores[local, :length] * scale, -jnp.inf)
-                    value = jnp.exp(value - jnp.max(value, axis=-1, keepdims=True))
-                    share = 1.0 / jnp.sum(value, axis=-1, keepdims=True)
-                    p_ref[h, row, :length] = (value * share).astype(bf16)
-                    return inner
-
-                lax.fori_loop(0, full // strip, soften, 0)
-                if length < seq:
-                    p_ref[h, base : base + full, length:] = jnp.zeros((full, seq - length), bf16)
-                o_ref[base : base + full, pl.ds(pl.multiple_of(h * HD, HD), HD)] = jnp.dot(
-                    p_ref[h, base : base + full, :length], qkv_ref[:length, part(2)], preferred_element_type=f32
-                ).astype(bf16)
-                return carry
-
-            lax.fori_loop(0, heads, one, 0)
-
-        works = [label] + [functools.partial(head, i) for i in range(nz)]
-        left_events = [(d, p) for d in range(1, nz) for p in range(PIECES)]
-
-        def events(count=None):
-            for _ in range(len(left_events) if count is None else count):
-                dy.event(*left_events.pop(0))
-
-        project(0, 2)
-        events(1)
-        project(2, nz)
-        events(1)
-        for work in works:
-            work()
-            if len(left_events) > 2:
-                events(1)
-
-        def inside(way, d):
-            return z + d < nz if way == UP else z >= d
-
-        def send_heads(way, d):
-            to = z + d if way == UP else z - d
-            src = o_ref.at[pl.ds(pl.multiple_of(to * full, full), full)]
-            return remote(src, heads_in.at[way, d], a_send.at[way, d], a_recv.at[way, d], {"expert": to})
-
-        for d in range(nz - 1, 0, -1):
-            for way in (UP, DOWN):
-                pl.when(inside(way, d))(lambda way=way, d=d: send_heads(way, d).start())
-
-        tile = 512 if width % 512 == 0 else width
-
-        def put(block, left, fresh):
-            at = pl.ds(pl.multiple_of(block * cols, cols), cols)
-
-            def one(i, carry):
-                to = pl.ds(pl.multiple_of(i * tile, tile), tile)
-                value = lax.dot_general(
-                    left(), wo[to, at], (((1,), (1,)), ((), ())), preferred_element_type=f32
-                )
-                acc[:, to] = value if fresh else acc[:, to] + value
-                return carry
-
-            lax.fori_loop(0, width // tile, one, 0)
-
-        put(z, lambda: o_ref[pl.ds(pl.multiple_of(z * full, full), full), :], True)
-        events()
-        for d in range(1, nz):
-            for way in (UP, DOWN):
-                @pl.when(z >= d if way == UP else z + d < nz)
-                def _(way=way, d=d):
-                    remote(
-                        heads_in.at[way, d], heads_in.at[way, d], a_send.at[way, d], a_recv.at[way, d], {"tensor": 1 - c}
-                    ).wait_recv()
-                    put(z - d if way == UP else z + d, lambda: heads_in[way, d], False)
-
-        def pack(at):
-            give[at, :] = acc[pl.ds(pl.multiple_of((1 - c) * rows + at.start, STRIP), STRIP), :].astype(bf16)
-
-        strips(rows, pack)
-        swap = remote(give, take_in, e_send, e_recv, {"tensor": 1 - c})
-        swap.start()
-        swap.wait_recv()
-
-        def norm_two(at):
-            mixed = acc[pl.ds(pl.multiple_of(c * rows + at.start, STRIP), STRIP), :] + take_in[at, :].astype(f32)
-            h = x_ref[at, :].astype(f32) + mixed
-            normed, inverse = norm_rows(h, gain2_ref[...])
-            h_ref[at, :] = h
-            own2[at, :] = normed.astype(bf16)
-            inv_own[at, :] = jnp.broadcast_to(inverse, (STRIP, 128))
-
-        strips(rows, norm_two)
-        spot = inv_ref.at[pl.ds(pl.multiple_of(c * rows, rows), rows)]
-        keep_inv = pltpu.make_async_copy(inv_own, spot, i_sems.at[0])
-        pass_on = remote(inv_own, spot, i_sems.at[1], i_sems.at[2], {"tensor": 1 - c})
-        keep_inv.start()
-        pass_on.start()
-        n2.start_along(UP)
-        n2.start_along(DOWN)
-        n2.start_across()
-        for d in range(1, nz):
-            for p in range(PIECES):
-                n2.event(d, p)
-        n2.finish()
-        dy.finish()
-        keep_inv.wait()
-        pass_on.wait()
-        swap.wait_send()
-        for d in range(1, nz):
-            for way in (UP, DOWN):
-                pl.when(inside(way, d))(lambda way=way, d=d: send_heads(way, d).wait_send())
-
-    return pl.pallas_call(
-        kernel,
-        out_shape=[
-            jax.ShapeDtypeStruct((seq, width), bf16),
-            jax.ShapeDtypeStruct((seq, width), bf16),
-            jax.ShapeDtypeStruct((nz,) + marks.shape, jnp.int32),
-            jax.ShapeDtypeStruct((seq, 3 * cols), bf16),
-            jax.ShapeDtypeStruct((heads, seq, seq), bf16),
-            jax.ShapeDtypeStruct((seq, cols), bf16),
-            jax.ShapeDtypeStruct((seq, width), bf16),
-            jax.ShapeDtypeStruct((rows, width), f32),
-            jax.ShapeDtypeStruct((full, 128), f32),
-        ],
-        in_specs=[VMEM] * 5 + [ANY] * 4,
-        out_specs=[VMEM, ANY, VMEM, VMEM, VMEM, VMEM, ANY, VMEM, ANY],
-        scratch_shapes=[
-            pltpu.VMEM((rows, width), bf16), pltpu.VMEM((width, 3 * cols), bf16), pltpu.VMEM((full, seq), f32),
-            pltpu.VMEM((seq, 1), f32), pltpu.VMEM((1, seq), f32),
-            pltpu.VMEM((2, nz, full, cols), bf16),
-            pltpu.VMEM((full, width), f32),
-            pltpu.VMEM((rows, width), bf16),
-            pltpu.VMEM((rows, width), bf16),
-            pltpu.VMEM((rows, width), bf16),
-            pltpu.VMEM((rows, 128), f32),
-            pltpu.VMEM(out_weight.shape, bf16),
-            pltpu.SemaphoreType.DMA((4,)),
-            pltpu.SemaphoreType.DMA((2, nz)), pltpu.SemaphoreType.DMA((2, nz)), pltpu.SemaphoreType.DMA,
-            pltpu.SemaphoreType.DMA((2, nz)),
-            pltpu.SemaphoreType.DMA((2, nz)),
-            pltpu.SemaphoreType.DMA,
-            pltpu.SemaphoreType.DMA,
-            pltpu.SemaphoreType.DMA((3,)),
-        ]
-        + gather_sems(nz) * 3,
-        compiler_params=params(name),
-    )(x, gain, upstream, marks, gain2, *weights, out_weight)
-
-
 def swap_rows(nz, own, out_ref, sems):
     z, c = here()
     rows = own.shape[0]
@@ -576,6 +339,10 @@
     return lax.dot_general(left, right, (((1,), (1,)), ((), ())), preferred_element_type=f32)
 
 
+def tn_dot(left, right):
+    return lax.dot_general(left, right, (((0,), (0,)), ((), ())), preferred_element_type=f32)
+
+
 def nn_dot(left, right):
     return jnp.dot(left, right, preferred_element_type=f32)
 
@@ -603,33 +370,24 @@
 
 def hidden_layer(nz, n2, dy, gate, weights, groups):
     seq, width = n2.shape
-    shared = weights[0].ndim == 2
-    experts = 1 if shared else weights[0].shape[0]
+    experts = weights[0].shape[0]
     buffers = min(experts, 2)
-    ffn = weights[0].shape[1] // nz if shared else weights[0].shape[1]
-    held = window_width(ffn, nz) if shared else ffn
-    kept = held if shared else padded(ffn)
+    held = weights[0].shape[1]
+    ffn, kept = held, padded(held)
     block = width // groups
     lane = min(block, TILE)
     per = TILE // lane
     count, slabs = seq // TILE, width // TILE
     strip = 32
-    product = nn_dot if shared else nt_dot
-    w_shape = (width, held) if shared else (held, width)
+    w_shape = (held, width)
 
     def kernel(n2_hbm, dy_hbm, wg_hbm, wu_hbm, wd_hbm, gate_ref, grad_hbm, da_hbm, db_hbm, gu_hbm, dgate_ref,
                n2_ref, dy_ref, wg, wu, wd, a, b, back, da, db, gu, turned, slab, in_sem, row_sem, out_sem, slab_sem):
         z = lax.axis_index("expert")
-        first = pl.multiple_of(z * ffn // LANES * LANES, LANES)
-        skip = z * ffn - first
-
-        def pick(ref, e):
-            return ref.at[:, pl.ds(first, held)] if shared else ref.at[e]
-
         def weight(i, e):
             slot = lax.rem(e, buffers)
             src, dst = ((wg_hbm, wg), (wu_hbm, wu), (wd_hbm, wd))[i]
-            return pltpu.make_async_copy(pick(src, e), dst.at[slot], in_sem.at[i, slot])
+            return pltpu.make_async_copy(src.at[e], dst.at[slot], in_sem.at[i, slot])
 
         rows_in = [
             pltpu.make_async_copy(n2_hbm, n2_ref, row_sem.at[0]), pltpu.make_async_copy(dy_hbm, dy_ref, row_sem.at[1])
@@ -649,13 +407,13 @@
             pl.when(e == 0)(rows_in[0].wait)
 
             def one(i, at):
-                a[at, :] = product(n2_ref[at, :], wg[slot])
+                a[at, :] = nt_dot(n2_ref[at, :], wg[slot])
 
             tiles(seq // TALL, one, TALL)
             weight(1, e).wait()
 
             def two(i, at):
-                b[at, :] = product(n2_ref[at, :], wu[slot])
+                b[at, :] = nt_dot(n2_ref[at, :], wu[slot])
 
             tiles(seq // TALL, two, TALL)
             weight(2, e).wait()
@@ -668,20 +426,18 @@
                         weight(i, e + 1).start()
 
             def three(i, at):
-                back[...] = product(dy_ref[at, :], wd[slot])
+                back[...] = nt_dot(dy_ref[at, :], wd[slot])
 
                 def point(j, carry):
                     row = pl.ds(pl.multiple_of(i * TILE + j * strip, strip), strip)
                     local = pl.ds(pl.multiple_of(j * strip, strip), strip)
-                    av, bv, kv, gv = a[row, :], b[row, :], back[local, :], gate_ref[e, row, :]
+                    av, bv, kv = a[row, :], b[row, :], back[local, :]
+                    here_now = lax.broadcasted_iota(jnp.int32, (strip, gate.shape[1]), 1) == z * experts + e
+                    gv = jnp.sum(jnp.where(here_now, gate_ref[row, :], 0.0), axis=-1, keepdims=True)
                     sig = 1.0 / (1.0 + jnp.exp(-av))
                     act = av * sig
                     u = act * bv
-                    if shared:
-                        column = lax.broadcasted_iota(jnp.int32, (strip, held), 1)
-                        mine = jnp.logical_and(column >= skip, column < skip + ffn)
-                        u, kv = jnp.where(mine, u, 0.0), jnp.where(mine, kv, 0.0)
-                    dgate_ref[e, row, :] = jnp.sum(u * kv, axis=-1, keepdims=True)
+                    dgate_ref[row, :] += jnp.where(here_now, jnp.sum(u * kv, axis=-1, keepdims=True), 0.0)
                     gu[row, :held] = (gv * u).astype(bf16)
                     du = gv * kv
                     da[row, :held] = (du * bv * (sig + act * (1.0 - sig))).astype(bf16)
@@ -715,8 +471,7 @@
                 slot = lax.rem(i, 2)
                 pl.when(i >= 2)(lambda: leave(i).wait())
                 for k, right in enumerate((n2_ref, n2_ref, dy_ref)):
-                    left = turned[k, pl.ds(pl.multiple_of(skip, 16), ffn), :] if shared else turned[k]
-                    value = nn_dot(left, right[:, at]).astype(bf16)
+                    value = nn_dot(turned[k], right[:, at]).astype(bf16)
                     for j in range(per):
                         slab[slot, j, k * ffn : (k + 1) * ffn, :] = value[:, j * lane : (j + 1) * lane]
                 leave(i).start()
@@ -728,17 +483,15 @@
                 save.wait()
             return carry
 
-        if experts == 1:
-            expert(0, 0)
-        else:
-            lax.fori_loop(0, experts, expert, 0)
+        dgate_ref[...] = jnp.zeros_like(dgate_ref)
+        lax.fori_loop(0, experts, expert, 0)
 
     hidden = jax.ShapeDtypeStruct((experts, seq, kept), bf16)
     return pl.pallas_call(
         kernel,
         out_shape=[
             jax.ShapeDtypeStruct((groups, experts * 3 * ffn, block), bf16), hidden, hidden, hidden,
-            jax.ShapeDtypeStruct((experts, seq, 1), f32),
+            jax.ShapeDtypeStruct(gate.shape, f32),
         ],
         in_specs=[ANY] * 5 + [VMEM],
         out_specs=[ANY] * 4 + [VMEM],
@@ -754,6 +507,580 @@
         ],
         compiler_params=pltpu.CompilerParams(vmem_limit_bytes=58 * 1024 * 1024),
     )(n2, dy, *weights, gate)
+
+
+def forward_layer(nz, x, gain, upstream, marks, weights, out_weight, gain2, small, shared, groups, name):
+    rows, width = x.shape
+    seq = nz * 2 * rows
+    cols = weights[0].shape[1] // nz
+    heads = cols // HD
+    full = 2 * rows
+    strip = 32
+    scale = HD ** (-0.5)
+    ffn = shared[0].shape[1] // nz
+    held = window_width(ffn, nz)
+    block = width // groups
+    lane = min(block, TILE)
+    per = TILE // lane
+    slabs = width // TILE
+    gate_row = small.shape[0] - 1
+
+    def kernel(x_ref, gain_ref, up_ref, marks_ref, gain2_ref, small_ref, wq_hbm, wk_hbm, wv_hbm, wo_hbm, wg_hbm, wu_hbm, wd_hbm,
+               n1_hbm, dy_hbm, all_ref, qkv_hbm, p_hbm, o_hbm, n2_hbm, h_ref, inv_ref, logit_ref, grad_hbm, da_hbm, db_hbm,
+               gu_hbm, dgate_ref,
+               n1_ref, dy_ref, qkv_ref, p_ref, o_ref, n2_ref, own, w, scores, seg_q, seg_k, heads_in, acc, give, take_in, own2,
+               inv_own, wo, wg, wu, wd, da, db, gu, turned, slab,
+               w_sem, m_send, m_recv, m_local, a_send, a_recv, e_send, e_recv, i_sems, out_sem, slab_sem, *sems):
+        z, c = here()
+        at = pl.ds(pl.multiple_of(z * cols, cols), cols)
+        loads = [
+            pltpu.make_async_copy(src.at[:, at], w.at[:, pl.ds(i * cols, cols)], w_sem.at[i])
+            for i, src in enumerate((wq_hbm, wk_hbm, wv_hbm))
+        ]
+        loads.append(pltpu.make_async_copy(wo_hbm, wo, w_sem.at[3]))
+        first = pl.multiple_of(z * ffn // LANES * LANES, LANES)
+        skip = z * ffn - first
+        for i, (src, dst) in enumerate(((wg_hbm, wg), (wu_hbm, wu), (wd_hbm, wd))):
+            loads.append(pltpu.make_async_copy(src.at[:, pl.ds(first, held)], dst, w_sem.at[4 + i]))
+        saves = []
+
+        def save(src, dst):
+            saves.append(pltpu.make_async_copy(src, dst, out_sem.at[len(saves)]))
+            saves[-1].start()
+
+        for load in loads:
+            load.start()
+
+        def step(strip_at):
+            normed, _ = norm_rows(x_ref[strip_at, :].astype(f32), gain_ref[...])
+            own[strip_at, :] = normed.astype(bf16)
+
+        strips(rows, step)
+        greet(nz)
+        n1 = Gather(nz, own, n1_ref, *sems[:5])
+        dy = Gather(nz, up_ref, dy_ref, *sems[5:10])
+        n2 = Gather(nz, own2, n2_ref, *sems[10:])
+        n1.start_along(UP)
+        n1.start_along(DOWN)
+        n1.start_across()
+        keep = pltpu.make_async_copy(marks_ref, all_ref.at[z], m_local)
+        keep.start()
+
+        def send(way, d):
+            to = z + d if way == UP else z - d
+            return remote(marks_ref, all_ref.at[z], m_send.at[way, d], m_recv.at[way, d], {"expert": to})
+
+        def take(way, d):
+            dst = all_ref.at[z - d if way == UP else z + d]
+            remote(dst, dst, m_send.at[way, d], m_recv.at[way, d], {"tensor": 1 - c}).wait_recv()
+
+        for d in range(1, nz):
+            for way in (UP, DOWN):
+                pl.when(z + d < nz if way == UP else z >= d)(lambda way=way, d=d: send(way, d).start())
+
+        def follow(d):
+            pl.when(z == d)(lambda: dy.start_along(UP))
+            pl.when(nz - 1 - z == d)(lambda: dy.start_along(DOWN))
+
+        follow(0)
+        for d in range(1, nz):
+            for p in range(PIECES):
+                n1.event(d, p)
+            follow(d)
+        dy.start_across()
+        keep.wait()
+        for d in range(1, nz):
+            for way in (UP, DOWN):
+                pl.when(z + d < nz if way == UP else z >= d)(lambda way=way, d=d: send(way, d).wait_send())
+                pl.when(z >= d if way == UP else z + d < nz)(lambda way=way, d=d: take(way, d))
+        n1.settle_all()
+        n1.finish()
+        save(n1_ref, n1_hbm)
+        for load in loads:
+            load.wait()
+
+        def project(first, last):
+            def one(i, carry):
+                to = pl.ds(pl.multiple_of(i * full, full), full)
+                qkv_ref[to, :] = jnp.dot(n1_ref[to, :], w[...], preferred_element_type=f32).astype(bf16)
+                return carry
+
+            lax.fori_loop(first, last, one, 0)
+
+        def label():
+            for b in range(nz):
+                some = all_ref[b].astype(f32)
+                seg_q[b * full : (b + 1) * full, :] = some.T[:, :1]
+                seg_k[:, b * full : (b + 1) * full] = some[:1, :]
+
+        def head(i):
+            length = (i + 1) * full
+
+            def one(h, carry):
+                def part(k):
+                    return pl.ds(pl.multiple_of(k * cols + h * HD, HD), HD)
+
+                base = i * full
+                scores[:, :length] = lax.dot_general(
+                    qkv_ref[base : base + full, part(0)], qkv_ref[:length, part(1)], (((1,), (1,)), ((), ())),
+                    preferred_element_type=f32,
+                )
+
+                def soften(j, inner):
+                    local = pl.ds(pl.multiple_of(j * strip, strip), strip)
+                    row = pl.ds(pl.multiple_of(base + j * strip, strip), strip)
+                    place_q = base + j * strip + lax.broadcasted_iota(jnp.int32, (strip, length), 0)
+                    place_k = lax.broadcasted_iota(jnp.int32, (strip, length), 1)
+                    allowed = jnp.logical_and(place_k <= place_q, seg_k[:, :length] == seg_q[row, :])
+                    value = jnp.where(allowed, scores[local, :length] * scale, -jnp.inf)
+                    value = jnp.exp(value - jnp.max(value, axis=-1, keepdims=True))
+                    share = 1.0 / jnp.sum(value, axis=-1, keepdims=True)
+                    p_ref[h, row, :length] = (value * share).astype(bf16)
+                    return inner
+
+                lax.fori_loop(0, full // strip, soften, 0)
+                if length < seq:
+                    p_ref[h, base : base + full, length:] = jnp.zeros((full, seq - length), bf16)
+                o_ref[base : base + full, pl.ds(pl.multiple_of(h * HD, HD), HD)] = jnp.dot(
+                    p_ref[h, base : base + full, :length], qkv_ref[:length, part(2)], preferred_element_type=f32
+                ).astype(bf16)
+                return carry
+
+            lax.fori_loop(0, heads, one, 0)
+
+        works = [label] + [functools.partial(head, i) for i in range(nz)]
+        left_events = [(d, p) for d in range(1, nz) for p in range(PIECES)]
+
+        def events(count=None):
+            for _ in range(len(left_events) if count is None else count):
+                dy.event(*left_events.pop(0))
+
+        project(0, 2)
+        events(1)
+        project(2, nz)
+        events(1)
+        for work in works:
+            work()
+            if len(left_events) > 2:
+                events(1)
+
+        def inside(way, d):
+            return z + d < nz if way == UP else z >= d
+
+        def send_heads(way, d):
+            to = z + d if way == UP else z - d
+            src = o_ref.at[pl.ds(pl.multiple_of(to * full, full), full)]
+            return remote(src, heads_in.at[way, d], a_send.at[way, d], a_recv.at[way, d], {"expert": to})
+
+        for d in range(nz - 1, 0, -1):
+            for way in (UP, DOWN):
+                pl.when(inside(way, d))(lambda way=way, d=d: send_heads(way, d).start())
+
+        save(qkv_ref, qkv_hbm)
+        save(p_ref, p_hbm)
+        save(o_ref, o_hbm)
+        tile = 512 if width % 512 == 0 else width
+
+        def put(block, left, fresh):
+            at = pl.ds(pl.multiple_of(block * cols, cols), cols)
+
+            def one(i, carry):
+                to = pl.ds(pl.multiple_of(i * tile, tile), tile)
+                value = lax.dot_general(
+                    left(), wo[to, at], (((1,), (1,)), ((), ())), preferred_element_type=f32
+                )
+                acc[:, to] = value if fresh else acc[:, to] + value
+                return carry
+
+            lax.fori_loop(0, width // tile, one, 0)
+
+        put(z, lambda: o_ref[pl.ds(pl.multiple_of(z * full, full), full), :], True)
+        events()
+        for d in range(1, nz):
+            for way in (UP, DOWN):
+                @pl.when(z >= d if way == UP else z + d < nz)
+                def _(way=way, d=d):
+                    remote(
+                        heads_in.at[way, d], heads_in.at[way, d], a_send.at[way, d], a_recv.at[way, d], {"tensor": 1 - c}
+                    ).wait_recv()
+                    put(z - d if way == UP else z + d, lambda: heads_in[way, d], False)
+
+        def pack(at):
+            give[at, :] = acc[pl.ds(pl.multiple_of((1 - c) * rows + at.start, STRIP), STRIP), :].astype(bf16)
+
+        strips(rows, pack)
+        swap = remote(give, take_in, e_send, e_recv, {"tensor": 1 - c})
+        swap.start()
+        swap.wait_recv()
+
+        def norm_two(at):
+            mixed = acc[pl.ds(pl.multiple_of(c * rows + at.start, STRIP), STRIP), :] + take_in[at, :].astype(f32)
+            h = x_ref[at, :].astype(f32) + mixed
+            normed, inverse = norm_rows(h, gain2_ref[...])
+            h_ref[at, :] = h
+            own2[at, :] = normed.astype(bf16)
+            inv_own[at, :] = jnp.broadcast_to(inverse, (STRIP, 128))
+
+        strips(rows, norm_two)
+        spot = inv_ref.at[pl.ds(pl.multiple_of(c * rows, rows), rows)]
+        keep_inv = pltpu.make_async_copy(inv_own, spot, i_sems.at[0])
+        pass_on = remote(inv_own, spot, i_sems.at[1], i_sems.at[2], {"tensor": 1 - c})
+        keep_inv.start()
+        pass_on.start()
+        n2.start_along(UP)
+        n2.start_along(DOWN)
+        n2.start_across()
+        dy.settle_all()
+        dy.finish()
+        save(dy_ref, dy_hbm)
+        a, b, back = acc.at[:, pl.ds(0, held)], acc.at[:, pl.ds(held, held)], scores.at[:, pl.ds(0, held)]
+
+        def hidden(index):
+            at = pl.ds(pl.multiple_of(index * full, full), full)
+            logit_ref[at, :] = nt_dot(n2_ref[at, :], small_ref[...])
+            a[...] = nn_dot(n2_ref[at, :], wg[...])
+            b[...] = nn_dot(n2_ref[at, :], wu[...])
+            back[...] = nn_dot(dy_ref[at, :], wd[...])
+
+            def point(j, carry):
+                row = pl.ds(pl.multiple_of(index * full + j * strip, strip), strip)
+                local = pl.ds(pl.multiple_of(j * strip, strip), strip)
+                column = lax.broadcasted_iota(jnp.int32, (strip, held), 1)
+                valid = jnp.logical_and(column >= skip, column < skip + ffn)
+                av, bv = a[local, :], b[local, :]
+                kv = jnp.where(valid, back[local, :], 0.0)
+                gv = 1.0 / (1.0 + jnp.exp(-logit_ref[row, gate_row : gate_row + 1]))
+                sig = 1.0 / (1.0 + jnp.exp(-av))
+                act = av * sig
+                u = jnp.where(valid, act * bv, 0.0)
+                last = lax.broadcasted_iota(jnp.int32, (strip, small.shape[0]), 1) == gate_row
+                dgate_ref[row, :] = jnp.where(last, jnp.sum(u * kv, axis=-1, keepdims=True), 0.0)
+                gu[row, :] = (gv * u).astype(bf16)
+                du = gv * kv
+                da[row, :] = (du * bv * (sig + act * (1.0 - sig))).astype(bf16)
+                db[row, :] = (du * act).astype(bf16)
+                return carry
+
+            lax.fori_loop(0, full // strip, point, 0)
+            for k, ref in enumerate((da, db, gu)):
+                turned[k, :, at] = ref[at, :].T
+
+        def arrivals(d):
+            for way in (UP, DOWN):
+
+                @pl.when(n2.inside(way, d))
+                def _(way=way):
+                    n2.settle(way, d)
+
+        def pair(d):
+            def one(k, carry):
+                index = z + (2 * k - 1) * d
+                pl.when(jnp.logical_and(index >= 0, index < nz))(lambda: hidden(index))
+                return carry
+
+            arrivals(d)
+            lax.fori_loop(0, 2, one, 0)
+
+        n2.settle(UP, 0)
+        hidden(z)
+        for d in range(1, nz):
+            for p in range(PIECES):
+                n2.event(d, p)
+            if d > 1:
+                pair(d - 1)
+        pair(nz - 1)
+        n2.finish()
+        save(n2_ref, n2_hbm)
+        save(da, da_hbm.at[0])
+        save(db, db_hbm.at[0])
+        save(gu, gu_hbm.at[0])
+
+        def leave(i):
+            slot = lax.rem(i, 2)
+            if per > 1:
+                dst = grad_hbm.at[pl.ds(i * per, per)]
+            else:
+                many = block // TILE
+                to = pl.ds(pl.multiple_of(lax.rem(i, many) * TILE, TILE), TILE)
+                dst = grad_hbm.at[pl.ds(i // many, 1), :, to]
+            return pltpu.make_async_copy(slab.at[slot], dst, slab_sem.at[slot])
+
+        def four(i, at):
+            slot = lax.rem(i, 2)
+            pl.when(i >= 2)(lambda: leave(i).wait())
+            for k, right in enumerate((n2_ref, n2_ref, dy_ref)):
+                value = nn_dot(turned[k, pl.ds(pl.multiple_of(skip, 16), ffn), :], right[:, at]).astype(bf16)
+                for j in range(per):
+                    slab[slot, j, k * ffn : (k + 1) * ffn, :] = value[:, j * lane : (j + 1) * lane]
+            leave(i).start()
+
+        tiles(slabs, four)
+        leave(slabs - 2).wait()
+        leave(slabs - 1).wait()
+        keep_inv.wait()
+        pass_on.wait()
+        swap.wait_send()
+        for d in range(1, nz):
+            for way in (UP, DOWN):
+                pl.when(inside(way, d))(lambda way=way, d=d: send_heads(way, d).wait_send())
+        for copy in saves:
+            copy.wait()
+
+    hidden_shape = jax.ShapeDtypeStruct((1, seq, held), bf16)
+    return pl.pallas_call(
+        kernel,
+        out_shape=[
+            jax.ShapeDtypeStruct((seq, width), bf16),
+            jax.ShapeDtypeStruct((seq, width), bf16),
+            jax.ShapeDtypeStruct((nz,) + marks.shape, jnp.int32),
+            jax.ShapeDtypeStruct((seq, 3 * cols), bf16),
+            jax.ShapeDtypeStruct((heads, seq, seq), bf16),
+            jax.ShapeDtypeStruct((seq, cols), bf16),
+            jax.ShapeDtypeStruct((seq, width), bf16),
+            jax.ShapeDtypeStruct((rows, width), f32),
+            jax.ShapeDtypeStruct((full, 128), f32),
+            jax.ShapeDtypeStruct((seq, small.shape[0]), f32),
+            jax.ShapeDtypeStruct((groups, 3 * ffn, block), bf16),
+            hidden_shape, hidden_shape, hidden_shape,
+            jax.ShapeDtypeStruct((seq, small.shape[0]), f32),
+        ],
+        in_specs=[VMEM] * 6 + [ANY] * 7,
+        out_specs=[ANY, ANY, VMEM, ANY, ANY, ANY, ANY, VMEM, ANY, VMEM, ANY, ANY, ANY, ANY, VMEM],
+        scratch_shapes=[
+            pltpu.VMEM((seq, width), bf16), pltpu.VMEM((seq, width), bf16), pltpu.VMEM((seq, 3 * cols), bf16),
+            pltpu.VMEM((heads, seq, seq), bf16), pltpu.VMEM((seq, cols), bf16), pltpu.VMEM((seq, width), bf16),
+            pltpu.VMEM((rows, width), bf16), pltpu.VMEM((width, 3 * cols), bf16), pltpu.VMEM((full, seq), f32),
+            pltpu.VMEM((seq, 1), f32), pltpu.VMEM((1, seq), f32),
+            pltpu.VMEM((2, nz, full, cols), bf16),
+            pltpu.VMEM((full, width), f32),
+            pltpu.VMEM((rows, width), bf16), pltpu.VMEM((rows, width), bf16), pltpu.VMEM((rows, width), bf16),
+            pltpu.VMEM((rows, 128), f32), pltpu.VMEM(out_weight.shape, bf16),
+            pltpu.VMEM((width, held), bf16), pltpu.VMEM((width, held), bf16), pltpu.VMEM((width, held), bf16),
+            pltpu.VMEM((seq, held), bf16), pltpu.VMEM((seq, held), bf16), pltpu.VMEM((seq, held), bf16),
+            pltpu.VMEM((3, held, seq), bf16), pltpu.VMEM((2, per, 3 * ffn, lane), bf16),
+            pltpu.SemaphoreType.DMA((7,)),
+            pltpu.SemaphoreType.DMA((2, nz)), pltpu.SemaphoreType.DMA((2, nz)), pltpu.SemaphoreType.DMA,
+            pltpu.SemaphoreType.DMA((2, nz)), pltpu.SemaphoreType.DMA((2, nz)),
+            pltpu.SemaphoreType.DMA, pltpu.SemaphoreType.DMA, pltpu.SemaphoreType.DMA((3,)),
+            pltpu.SemaphoreType.DMA((9,)), pltpu.SemaphoreType.DMA((2,)),
+        ]
+        + gather_sems(nz) * 3,
+        compiler_params=pltpu.CompilerParams(
+            collective_id=name, has_side_effects=True, vmem_limit_bytes=63 * 1024 * 1024
+        ),
+    )(x, gain, upstream, marks, gain2, small, *weights, out_weight, *shared)
+
+
+def attention_back(nz, d_h, n1, qkv, probs, o, out_weight, groups, part, name):
+    seq, width = d_h.shape
+    heads = probs.shape[0]
+    cols = o.shape[1]
+    full = seq // nz
+    block = width // groups
+    lane = min(block, TILE)
+    per = TILE // lane
+    slabs = width // TILE
+    strip = 32
+    scale = HD ** (-0.5)
+
+    def kernel(dh_hbm, n1_hbm, qkv_ref, p_ref, o_ref, wo_hbm, part_hbm, heads_ref, grad_hbm, box_hbm,
+               b_send, b_recv, b_local, dh_ref, n1_ref, wo, d_o, scores, ds, dk, dv, turned, o_turned, slab, in_sem, slab_sem):
+        z, c = here()
+        at = pl.ds(pl.multiple_of(z * cols, cols), cols)
+        loads = [
+            pltpu.make_async_copy(wo_hbm.at[:, at], wo, in_sem.at[0]),
+            pltpu.make_async_copy(dh_hbm, dh_ref, in_sem.at[1]),
+            pltpu.make_async_copy(n1_hbm, n1_ref, in_sem.at[2]),
+        ]
+        for load in loads:
+            load.start()
+        greet(nz)
+        keep = pltpu.make_async_copy(part_hbm.at[z], box_hbm.at[z], b_local)
+        keep.start()
+
+        def send(way, d):
+            to = z + d if way == UP else z - d
+            return remote(part_hbm.at[to], box_hbm.at[z], b_send.at[way, d], b_recv.at[way, d], {"expert": to})
+
+        def take(way, d):
+            dst = box_hbm.at[z - d if way == UP else z + d]
+            remote(dst, dst, b_send.at[way, d], b_recv.at[way, d], {"tensor": 1 - c}).wait_recv()
+
+        for d in range(nz - 1, 0, -1):
+            for way in (UP, DOWN):
+                pl.when(z + d < nz if way == UP else z >= d)(lambda way=way, d=d: send(way, d).start())
+        o_turned[...] = o_ref[...].T
+        loads[0].wait()
+        loads[1].wait()
+
+        def project(i, to):
+            d_o[to, :] = nn_dot(dh_ref[to, :], wo[...]).astype(bf16)
+
+        tiles(seq // TILE, project)
+
+        def head(h, carry):
+            def part(k):
+                return pl.ds(pl.multiple_of(k * cols + h * HD, HD), HD)
+
+            mine = part(0)
+            for i in reversed(range(nz)):
+                length = (i + 1) * full
+                row = pl.ds(i * full, full)
+                scores[:, :length] = nt_dot(d_o[row, mine], qkv_ref[:length, part(2)])
+
+                def harden(j, inner, i=i, length=length):
+                    local = pl.ds(pl.multiple_of(j * strip, strip), strip)
+                    to = pl.ds(pl.multiple_of(i * full + j * strip, strip), strip)
+                    mean = jnp.sum(
+                        d_o[to, mine].astype(f32) * o_ref[to, mine].astype(f32), axis=-1, keepdims=True
+                    )
+                    value = p_ref[h, to, :length].astype(f32) * (scores[local, :length] - mean)
+                    ds[local, :length] = value.astype(bf16)
+                    return inner
+
+                lax.fori_loop(0, full // strip, harden, 0)
+                d_s = ds[:, :length]
+                heads_ref[row, mine] = (nn_dot(d_s, qkv_ref[:length, part(1)]) * scale).astype(bf16)
+                d_k = tn_dot(d_s, qkv_ref[row, mine])
+                d_v = tn_dot(p_ref[h, row, :length], d_o[row, mine])
+                if i == nz - 1:
+                    dk[...], dv[...] = d_k, d_v
+                else:
+                    dk[:length, :] += d_k
+                    dv[:length, :] += d_v
+            heads_ref[:, part(1)] = (dk[...] * scale).astype(bf16)
+            heads_ref[:, part(2)] = dv[...].astype(bf16)
+            return carry
+
+        lax.fori_loop(0, heads, head, 0)
+
+        def turn(i, to):
+            turned[:, to] = heads_ref[to, :].T
+
+        tiles(seq // TILE, turn)
+        loads[2].wait()
+
+        def leave(i):
+            slot = lax.rem(i, 2)
+            if per > 1:
+                dst = grad_hbm.at[pl.ds(i * per, per)]
+            else:
+                many = block // TILE
+                to = pl.ds(pl.multiple_of(lax.rem(i, many) * TILE, TILE), TILE)
+                dst = grad_hbm.at[pl.ds(i // many, 1), :, to]
+            return pltpu.make_async_copy(slab.at[slot], dst, slab_sem.at[slot])
+
+        def write(i, to):
+            slot = lax.rem(i, 2)
+            pl.when(i >= 2)(lambda: leave(i).wait())
+            inner = nn_dot(turned[...], n1_ref[:, to]).astype(bf16)
+            outer = nn_dot(o_turned[...], dh_ref[:, to]).astype(bf16)
+            for j in range(per):
+                slab[slot, j, : 3 * cols, :] = inner[:, j * lane : (j + 1) * lane]
+                slab[slot, j, 3 * cols :, :] = outer[:, j * lane : (j + 1) * lane]
+            leave(i).start()
+
+        tiles(slabs, write)
+        leave(slabs - 2).wait()
+        leave(slabs - 1).wait()
+        keep.wait()
+        for d in range(1, nz):
+            for way in (UP, DOWN):
+                pl.when(z + d < nz if way == UP else z >= d)(lambda way=way, d=d: send(way, d).wait_send())
+                pl.when(z >= d if way == UP else z + d < nz)(lambda way=way, d=d: take(way, d))
+
+    return pl.pallas_call(
+        kernel,
+        out_shape=[
+            jax.ShapeDtypeStruct((seq, 3 * cols), bf16),
+            jax.ShapeDtypeStruct((groups, 4 * cols, block), bf16),
+            jax.ShapeDtypeStruct(part.shape, bf16),
+        ],
+        in_specs=[ANY, ANY, VMEM, VMEM, VMEM, ANY, ANY],
+        out_specs=[VMEM, ANY, ANY],
+        scratch_shapes=[
+            pltpu.SemaphoreType.DMA((2, nz)), pltpu.SemaphoreType.DMA((2, nz)), pltpu.SemaphoreType.DMA,
+            pltpu.VMEM((seq, width), bf16), pltpu.VMEM((seq, width), bf16), pltpu.VMEM((width, cols), bf16),
+            pltpu.VMEM((seq, cols), bf16), pltpu.VMEM((full, seq), f32), pltpu.VMEM((full, seq), bf16),
+            pltpu.VMEM((seq, HD), f32), pltpu.VMEM((seq, HD), f32),
+            pltpu.VMEM((3 * cols, seq), bf16), pltpu.VMEM((cols, seq), bf16), pltpu.VMEM((2, per, 4 * cols, lane), bf16),
+            pltpu.SemaphoreType.DMA((3,)), pltpu.SemaphoreType.DMA((2,)),
+        ],
+        compiler_params=params(name),
+    )(d_h, n1, qkv, probs, o, out_weight, part)
+
+
+def finish_gradients(nz, part, splits, small, name):
+    _, columns, block = part.shape
+    cols = columns // splits
+    n, rows, lanes = small.shape
+
+    def kernel(in_ref, small_ref, *rest):
+        outs, sum_ref, rest = rest[:splits], rest[splits], rest[splits + 1 :]
+        box, s_box, total, other, send_sem, recv_sem, s_send, s_recv, swap_sem = rest
+        z, c = here()
+        me = lax.axis_index("dp") * nz + z
+        barrier = pltpu.get_barrier_semaphore()
+
+        def peer(k):
+            at = lax.rem(me + k, n)
+            return at, {"dp": at // nz, "expert": lax.rem(at, nz)}
+
+        pl.semaphore_signal(barrier, inc=1, device_id={"tensor": 1 - c}, device_id_type=MESH)
+        for k in range(1, n):
+            pl.semaphore_signal(barrier, inc=1, device_id=peer(k)[1], device_id_type=MESH)
+        pl.semaphore_wait(barrier, n)
+
+        def send(way, d):
+            to = z + d if way == UP else z - d
+            return remote(in_ref.at[to], box.at[z], send_sem.at[way, d], recv_sem.at[way, d], {"expert": to})
+
+        def take(way, d):
+            dst = box.at[z - d if way == UP else z + d]
+            remote(dst, dst, send_sem.at[way, d], recv_sem.at[way, d], {"tensor": 1 - c}).wait_recv()
+
+        def send_small(k):
+            at, device = peer(k)
+            return remote(small_ref.at[at], s_box.at[k], s_send.at[k], s_recv.at[k], device)
+
+        for k in range(1, n):
+            send_small(k).start()
+        for d in range(nz - 1, 0, -1):
+            for way in (UP, DOWN):
+                pl.when(z + d < nz if way == UP else z >= d)(lambda way=way, d=d: send(way, d).start())
+        box[z] = in_ref[z]
+        total[...] = small_ref[me]
+        for k in range(1, n):
+            send_small(k).wait_recv()
+            total[...] += s_box[k]
+        swap = remote(total, other, swap_sem.at[0], swap_sem.at[1], {"tensor": 1 - c})
+        swap.start()
+        swap.wait_recv()
+        sum_ref[...] = total[...] + other[...]
+        for d in range(1, nz):
+            for way in (UP, DOWN):
+                pl.when(z + d < nz if way == UP else z >= d)(lambda way=way, d=d: send(way, d).wait_send())
+                pl.when(z >= d if way == UP else z + d < nz)(lambda way=way, d=d: take(way, d))
+        for j in range(splits):
+            for b in range(nz):
+                value = box[b, j * cols : (j + 1) * cols, :].astype(f32).T
+                outs[j][:, b * cols : (b + 1) * cols] = value
+        swap.wait_send()
+        for k in range(1, n):
+            send_small(k).wait_send()
+
+    return pl.pallas_call(
+        kernel,
+        out_shape=[jax.ShapeDtypeStruct((block, nz * cols), f32)] * splits + [jax.ShapeDtypeStruct((rows, lanes), f32)],
+        in_specs=[VMEM] * 2,
+        out_specs=[VMEM] * (splits + 1),
+        scratch_shapes=[
+            pltpu.VMEM(part.shape, bf16), pltpu.VMEM((n, rows, lanes), f32), pltpu.VMEM((rows, lanes), f32),
+            pltpu.VMEM((rows, lanes), f32), pltpu.SemaphoreType.DMA((2, nz)), pltpu.SemaphoreType.DMA((2, nz)),
+            pltpu.SemaphoreType.DMA((n,)), pltpu.SemaphoreType.DMA((n,)), pltpu.SemaphoreType.DMA((2,)),
+        ],
+        compiler_params=params(name),
+    )(part, small)
 
 
 PART = 512
@@ -904,21 +1231,28 @@
 
 def reduce_last(nz, d_heads, weights, x, gain, dh, products, h, name):
     rows, width = x.shape
+    cols = d_heads.shape[1] // 3
     n_in, n_scratch = len(products.inputs), len(products.scratch)
 
     def kernel(*refs):
-        p_refs, (d_ref, w_ref, x_ref, gain_ref, dh_ref, h_ref, in_ref, out_ref, gg_ref) = (
-            refs[:n_in], refs[n_in : n_in + 9],
+        p_refs, (d_ref, wq_hbm, wk_hbm, wv_hbm, x_ref, gain_ref, dh_ref, h_ref, in_ref, out_ref, gg_ref) = (
+            refs[:n_in], refs[n_in : n_in + 11],
         )
-        rest = refs[n_in + 9 :]
-        p_scratch, (d_part, b_part, own, sems), rest = (
-            rest[:n_scratch], rest[n_scratch : n_scratch + 4], rest[n_scratch + 4 :],
+        rest = refs[n_in + 11 :]
+        p_scratch, (d_part, b_part, own, sems, w_ref, w_sem), rest = (
+            rest[:n_scratch], rest[n_scratch : n_scratch + 6], rest[n_scratch + 6 :],
         )
+        mine = pl.ds(pl.multiple_of(lax.axis_index("expert") * cols, cols), cols)
+        loads = [
+            pltpu.make_async_copy(src.at[:, mine], w_ref.at[:, pl.ds(i * cols, cols)], w_sem.at[i])
+            for i, src in enumerate((wq_hbm, wk_hbm, wv_hbm))
+        ]
+        for load in loads:
+            load.start()
         d_scratch, b_scratch = rest[:REDUCE_SCRATCH], rest[REDUCE_SCRATCH:]
         d_total, b_total = d_scratch[3], b_scratch[3]
         products.bind(p_refs, p_scratch)
         first, second = Reducer(nz, d_part, *d_scratch), Reducer(nz, b_part, *b_scratch)
-        products.fetch(second.block)
         greet(nz)
         z, c = here()
         ends = first.ends()
@@ -955,6 +1289,9 @@
             pl.when(middle)(lambda: second.forward(s))
             return carry
 
+        for load in loads:
+            load.wait()
+        products.fetch(second.block)
         lax.fori_loop(0, nz, one, 0)
         lax.fori_loop(0, nz, two, 0)
         lax.fori_loop(0, nz - 1, three, 0)
@@ -997,16 +1334,17 @@
             jax.ShapeDtypeStruct((2 * rows, width), f32),
             jax.ShapeDtypeStruct((STRIP, width), f32),
         ],
-        in_specs=products.specs + [VMEM] * 6,
+        in_specs=products.specs + [VMEM] + [ANY] * 3 + [VMEM] * 4,
         out_specs=[ANY, ANY, VMEM],
         scratch_shapes=products.scratch
         + [
             pltpu.VMEM((nz * 2 * rows, width), bf16), pltpu.VMEM((nz * 2 * rows, width), bf16),
             pltpu.VMEM((2, rows, width), f32), pltpu.SemaphoreType.DMA((2, 3)),
+            pltpu.VMEM((width, 3 * cols), bf16), pltpu.SemaphoreType.DMA((3,)),
         ]
         + reduce_scratch(nz, rows, width) * 2,
         compiler_params=params(name),
-    )(*products.inputs, d_heads, weights, x, gain, dh, h)
+    )(*products.inputs, d_heads, *weights, x, gain, dh, h)
 
 
 def assemble(nz, box, columns):
@@ -1026,97 +1364,6 @@
         out_specs=[VMEM] * count,
         compiler_params=pltpu.CompilerParams(vmem_limit_bytes=40 * 1024 * 1024),
     )(box)
-
-
-def finish_gradients(nz, part, splits, small, experts, name):
-    n, rows, lanes = small.shape
-    block = part.shape[0] // nz
-    cols = part.shape[1] // splits
-    local, kinds, ffn, width = experts.shape
-
-    def kernel(part_ref, small_ref, experts_ref, *rest):
-        outs, (sum_ref,), e_outs = rest[:splits], rest[splits : splits + 1], rest[splits + 1 : splits + 1 + kinds]
-        (box, s_box, total, other, wide, send_sem, recv_sem, s_send, s_recv, swap_sem, out_sem) = rest[splits + 1 + kinds :]
-        z, c = here()
-        me = lax.axis_index("dp") * nz + z
-        barrier = pltpu.get_barrier_semaphore()
-
-        def peer(k):
-            at = lax.rem(me + k, n)
-            return at, {"dp": at // nz, "expert": lax.rem(at, nz)}
-
-        pl.semaphore_signal(barrier, inc=1, device_id={"tensor": 1 - c}, device_id_type=MESH)
-        for k in range(1, n):
-            pl.semaphore_signal(barrier, inc=1, device_id=peer(k)[1], device_id_type=MESH)
-        pl.semaphore_wait(barrier, n)
-
-        def send(way, d):
-            to = z + d if way == UP else z - d
-            src = part_ref.at[pl.ds(pl.multiple_of(to * block, block), block)]
-            return remote(src, box.at[z], send_sem.at[way, d], recv_sem.at[way, d], {"expert": to})
-
-        def take(way, d):
-            dst = box.at[z - d if way == UP else z + d]
-            remote(dst, dst, send_sem.at[way, d], recv_sem.at[way, d], {"tensor": 1 - c}).wait_recv()
-
-        def send_small(k):
-            at, device = peer(k)
-            return remote(small_ref.at[at], s_box.at[k], s_send.at[k], s_recv.at[k], device)
-
-        for k in range(1, n):
-            send_small(k).start()
-        for d in range(nz - 1, 0, -1):
-            for way in (UP, DOWN):
-                pl.when(z + d < nz if way == UP else z >= d)(lambda way=way, d=d: send(way, d).start())
-        box[z] = part_ref[pl.ds(pl.multiple_of(z * block, block), block), :]
-        leaves = [pltpu.make_async_copy(wide.at[i], e_outs[i], out_sem.at[i]) for i in range(kinds)]
-        for i in range(kinds):
-            for e in range(local):
-                def widen(at, i=i, e=e):
-                    wide[i, e, at, :] = experts_ref[e, i, at, :].astype(f32)
-
-                strips(ffn, widen)
-            leaves[i].start()
-        total[...] = small_ref[me]
-        for k in range(1, n):
-            send_small(k).wait_recv()
-            total[...] += s_box[k]
-        swap = remote(total, other, swap_sem.at[0], swap_sem.at[1], {"tensor": 1 - c})
-        swap.start()
-        swap.wait_recv()
-        sum_ref[...] = total[...] + other[...]
-        for d in range(1, nz):
-            for way in (UP, DOWN):
-                pl.when(z >= d if way == UP else z + d < nz)(lambda way=way, d=d: take(way, d))
-        for j in range(splits):
-            for b in range(nz):
-                outs[j][:, b * cols : (b + 1) * cols] = box[b, :, j * cols : (j + 1) * cols].astype(f32)
-        swap.wait_send()
-        for k in range(1, n):
-            send_small(k).wait_send()
-        for d in range(1, nz):
-            for way in (UP, DOWN):
-                pl.when(z + d < nz if way == UP else z >= d)(lambda way=way, d=d: send(way, d).wait_send())
-        for leave in leaves:
-            leave.wait()
-
-    return pl.pallas_call(
-        kernel,
-        out_shape=[jax.ShapeDtypeStruct((block, nz * cols), f32)] * splits
-        + [jax.ShapeDtypeStruct((rows, lanes), f32)]
-        + [jax.ShapeDtypeStruct((local, ffn, width), f32)] * kinds,
-        in_specs=[VMEM] * 3,
-        out_specs=[VMEM] * (splits + 1) + [ANY] * kinds,
-        scratch_shapes=[
-            pltpu.VMEM((nz, block, part.shape[1]), bf16), pltpu.VMEM((n, rows, lanes), f32),
-            pltpu.VMEM((rows, lanes), f32), pltpu.VMEM((rows, lanes), f32),
-            pltpu.VMEM((kinds, local, ffn, width), f32),
-            pltpu.SemaphoreType.DMA((2, nz)), pltpu.SemaphoreType.DMA((2, nz)),
-            pltpu.SemaphoreType.DMA((n,)), pltpu.SemaphoreType.DMA((n,)), pltpu.SemaphoreType.DMA((2,)),
-            pltpu.SemaphoreType.DMA((kinds,)),
-        ],
-        compiler_params=params(name),
-    )(part, small, experts)
 
 
 def cross_rows(left, right):
@@ -1168,31 +1415,28 @@
     x = own(tokens)
     marks = jnp.concatenate([segments, routes.T, jnp.zeros((7 - routes.shape[1], rows), jnp.int32)], axis=0)
     upstream = own(out_grad)
-    n1, dy, all_marks, qkv, p_low, o, n2, h, inverse_two = attend(
-        nz, x, gain1, upstream, marks, (q_weight, k_weight, v_weight), o_weight, gain2, 0
+    ndp = lax.axis_size("dp")
+    small_rows_weight = jnp.concatenate([router_weight.T, shared_gate_vector[None]], axis=0)
+    shared_weights = (shared_gate_weight, shared_up_weight, shared_down_weight)
+    (
+        n1, dy, all_marks, qkv, p_low, o, n2, h, inverse_two, logits, grad_s, da_s, db_s, gu_s, dgate_s,
+    ) = forward_layer(
+        nz, x, gain1, upstream, marks, (q_weight, k_weight, v_weight), o_weight, gain2, small_rows_weight, shared_weights,
+        ndp * nz, 0,
     )
     all_routes = jnp.transpose(all_marks[:, 1 : 1 + routes.shape[1]], (0, 2, 1)).reshape(seq, routes.shape[1])
-    wo = head_slice(o_weight)
-    w_heads = jnp.concatenate([head_slice(q_weight), head_slice(k_weight), head_slice(v_weight)], axis=1)
-    q, k, v = (qkv[:, i * head_cols : (i + 1) * head_cols].reshape(seq, heads, HD) for i in range(3))
-    probs = jax.nn.softmax(dot(n2, router_weight), axis=-1)
+
+    probs = jax.nn.softmax(logits[:, :expert_count], axis=-1)
     chosen = jnp.any(all_routes[:, :, None] == jnp.arange(expert_count)[None, None, :], axis=1)
     gates = jnp.where(chosen, probs, 0.0)
-    sigma = jax.nn.sigmoid(dot(n2, shared_gate_vector))
+    sigma = jax.nn.sigmoid(logits[:, expert_count:])
 
     turned = [jnp.swapaxes(w, 1, 2) for w in (expert_gate_weight, expert_up_weight, expert_down_weight)]
-    shared_weights = (shared_gate_weight, shared_up_weight, shared_down_weight)
-    ndp = lax.axis_size("dp")
-    grad_s, da_s, db_s, gu_s, dgate_s = hidden_layer(nz, n2, dy, sigma[None, :, None], shared_weights, ndp * nz)
-    n2_now, dgate_s = lax.optimization_barrier((n2, dgate_s))
-    gate = jnp.swapaxes(lax.dynamic_slice_in_dim(gates, z * local_count, local_count, 1), 0, 1)[:, :, None]
-    grad_e, da_e, db_e, gu_e, dgate_e = hidden_layer(nz, n2_now, dy, gate, turned, ndp)
-
-    d_expert = jnp.swapaxes(dgate_e[:, :, 0], 0, 1)
-    d_probs = lax.dynamic_update_slice_in_dim(jnp.zeros_like(probs), d_expert, z * local_count, 1)
-    d_probs = jnp.where(chosen, d_probs, 0.0)
+    grad_e, da_e, db_e, gu_e, dgate_e = hidden_layer(nz, n2, dy, gates, turned, ndp)
+
+    d_probs = jnp.where(chosen, dgate_e, 0.0)
     d_logits = probs * (d_probs - jnp.sum(probs * d_probs, axis=-1, keepdims=True))
-    d_vector = dgate_s[0] * (sigma * (1.0 - sigma))[:, None]
+    d_vector = dgate_s[:, expert_count:] * (sigma * (1.0 - sigma))
     small = jnp.concatenate([d_logits, d_vector], axis=1)
     small_high, small_low = two_parts(small)
     small_weights = jnp.concatenate([router_weight, shared_gate_vector[:, None]], axis=1)
@@ -1215,24 +1459,10 @@
     shared_part = over_dp(grad_s).reshape((nz,) + grad_s.shape[1:])
     expert_part = over_dp(grad_e).reshape(local_count, 3, ffn, -1)
     dhr, dh, grad_two = reduce_and_gather(nz, d_n2, h, gain2, upstream, 2)
-    shared_part, dhr = lax.optimization_barrier((shared_part, dhr))
-    shared_box = lax.all_to_all(shared_part, "expert", split_axis=0, concat_axis=0, tiled=True)
-    d_o = dot(dhr, wo).astype(bf16).reshape(seq, heads, HD)
-    grad_o = cross_rows(dhr, o)
-
-    d_v = jnp.einsum("hqk,qhd->khd", p_low, d_o, preferred_element_type=f32)
-    dp = jnp.einsum("qhd,khd->hqk", d_o, v, preferred_element_type=f32)
-    mean = jnp.sum(d_o.astype(f32) * o.reshape(seq, heads, HD).astype(f32), axis=-1).T
-    ds = (p_low.astype(f32) * (dp - mean[:, :, None])).astype(bf16)
-    d_q = jnp.einsum("hqk,khd->qhd", ds, k, preferred_element_type=f32) * scale
-    d_k = jnp.einsum("hqk,qhd->khd", ds, q, preferred_element_type=f32) * scale
-    d_heads = jnp.concatenate([t.reshape(seq, head_cols).astype(bf16) for t in (d_q, d_k, d_v)], axis=1)
-    s_gate, s_up, s_down = assemble(nz, shared_box, shared_cols)
-    d_heads, s_gate = lax.optimization_barrier((d_heads, s_gate))
-    grad_attention = jnp.concatenate(
-        [cross_rows(n1, d_heads).astype(bf16), grad_o.astype(bf16)], axis=1
+    d_heads, grad_attention, shared_box = attention_back(
+        nz, dhr, n1, qkv, p_low, o, o_weight, ndp * nz, shared_part, 1
     )
-    attention_part = over_dp(grad_attention)
+    attention_part = over_dp(grad_attention).reshape((nz,) + grad_attention.shape[1:])
     branch = Products(
         nz,
         [((gu_e, i), (turned[2], i)) for i in experts],
@@ -1241,7 +1471,7 @@
     )
     dh_now, _ = lax.optimization_barrier((dh, grad_attention))
     input_grad, layer_out, grad_one = reduce_last(
-        nz, d_heads, w_heads, x, gain1, dh_now, branch, h, 3
+        nz, d_heads, (q_weight, k_weight, v_weight), x, gain1, dh_now, branch, h, 3
     )
     stats = jnp.stack([inverse_one_rows, inverse_two[:, 0]])
 
@@ -1255,8 +1485,12 @@
     small_rows, expert_part = lax.optimization_barrier((small_rows, expert_part))
     count = ndp * nz
     small_blocks = jnp.swapaxes(small_rows.reshape(16, count, width // count), 0, 1)
-    g_q, g_k, g_v, g_o, small_all, *wide = finish_gradients(nz, attention_part, 4, small_blocks, expert_part, 6)
-    e_gate, e_up, e_down = (jnp.swapaxes(t, 1, 2) for t in wide)
+    s_gate, s_up, s_down = assemble(nz, shared_box, shared_cols)
+    e_gate, e_up, e_down = (jnp.swapaxes(expert_part[:, k].astype(f32), 1, 2) for k in range(3))
+    attention_part, small_blocks, e_gate, e_up, e_down, s_gate = lax.optimization_barrier(
+        (attention_part, small_blocks, e_gate, e_up, e_down, s_gate)
+    )
+    g_q, g_k, g_v, g_o, small_all = finish_gradients(nz, attention_part, 4, small_blocks, 6)
     g_one, g_two, g_router, g_vector = small_all[0], small_all[1], small_all[2 : 2 + expert_count].T, small_all[2 + expert_count]
     return (
         layer_out, input_grad, stats, g_one, g_q, g_k, g_v, g_o, g_two, g_router, g_vector,

time: 578 us -> 539 us (0.933)
  Pallas kernels: 444 us -> 481 us
  matrix products: 32.9 us -> 2.94 us
  local copies, waits for them, and re-layouts: 40.9 us -> 20.1 us
  waiting for transfers between devices: 14.4 us -> 0.09 us
  starting transfers between devices: 8.15 us -> 0.12 us
    pallas_call x1 -> x2, Pallas kernels: 132 us -> 202 us  [the longest x1 144 us: forward_layer(): pl.pallas_call(kernel, out_shape=[jax.ShapeDtypeStruct((seq, width), bf16...]
    pallas_call x2 -> x1, Pallas kernels: 96.8 us -> 61.9 us  [hidden_layer(): pl.pallas_call(kernel, out_shape=[jax.ShapeDtypeStruct((groups, experts *...]
    dot_general x7 -> x0, matrix products: 22.4 us -> none  [the longest x3 11.3 us: dot(): return jnp.dot(left, right, preferred_element_type=f32)]
    all_to_all x1 -> x0, waiting for transfers between devices: 14.4 us -> none  [body(): lax.all_to_all(shared_part, 'expert', split_axis=0, concat_axis=0, tiled=...]
    unnamed x54 -> x36, local copies, waits for them, and re-layouts: 18.4 us -> 10.1 us
    all_to_all x1 -> x0, starting transfers between devices: 7.72 us -> none  [body(): lax.all_to_all(shared_part, 'expert', split_axis=0, concat_axis=0, tiled=...]
    dot_general x3 -> x1, matrix products: 10.5 us -> 2.94 us  [cross_rows(): lax.dot_general(left, right, (((0,), (0,)), ((), ())), preferred_element_...]
    pallas_call x1, Pallas kernels: 91.5 us -> 97.8 us  [reduce_and_gather(): pl.pallas_call(kernel, out_shape=[jax.ShapeDtypeStruct((nz * 2 * rows, wi...]
  transfers between devices with their start and end apart: 4 -> 3, of which waited for: 1 -> 0; matrix products, arithmetic and copies ran while one was open for 10% -> 3% of each run, Pallas kernels for 42% -> 56%
where the time goes in v1:
time: 539 us; the launch traced here: 534 us
  Pallas kernels  481 us (89%)
  local copies, waits for them, and re-layouts  20.1 us (4%)
  other arithmetic  15.6 us (3%)
  between operations  14.5 us (3%)
    pallas_call x1, Pallas kernels, forward_layer(): pl.pallas_call(kernel, out_shape=[jax.ShapeDtypeStruct((seq, width), bf16...  144 us
    pallas_call x1, Pallas kernels, reduce_and_gather(): pl.pallas_call(kernel, out_shape=[jax.ShapeDtypeStruct((nz * 2 * rows, wi...  97.8 us
    pallas_call x1, Pallas kernels, reduce_last(): pl.pallas_call(kernel, out_shape=[jax.ShapeDtypeStruct((2 * rows, width),...  80.4 us
    pallas_call x1, Pallas kernels, hidden_layer(): pl.pallas_call(kernel, out_shape=[jax.ShapeDtypeStruct((groups, experts *...  61.9 us
    pallas_call x1, Pallas kernels, attention_back(): pl.pallas_call(kernel, out_shape=[jax.ShapeDtypeStruct((seq, 3 * cols), b...  57.6 us
    pallas_call x1, Pallas kernels, finish_gradients(): pl.pallas_call(kernel, out_shape=[jax.ShapeDtypeStruct((block, nz * cols)...  35.9 us
  transfers between devices with their start and end apart: 3, of which 0 were waited for; matrix products, arithmetic and copies ran while one was open for 3% of the time, Pallas kernels for 56%

profile of v1, /device:TPU:8, one launch (start us, length us, event | category | flops | bytes accessed | tf_op | source)
XLA Modules:
  0.0 534.1 jit_solution(9944545436750014024)
XLA Ops:
  7.3 1.3 broadcast_in_dim.48
  8.6 1.3 broadcast_in_dim.49
  9.9 0.7 broadcast_in_dim.42
  10.6 1.4 pad_maximum_fusion.small_ref
  12.0 1.4 add_add_fusion.marks_ref
  13.3 2.3 constant_dynamic-slice_fusion
  15.6 144.2 %shard_map.305 = (bf16[1024,2048]{1,0:T(8,128)(2,1)}, bf16[1024,2048]{1,0:T(8,128)(2,1)}, s32[4,8,256]{2,1,0:T(8,128)}, bf16[1024,768]{1,0:T(8,128)(2,1)}, bf16[...) custom-call(bf16[128,2048]{1,0:T(8,128)(2,1)} %get-tuple-element.122, ...), custom_call_target="tpu_custom_call" | custom-call | tf_op jit(solution)/shard_map/pallas_call | solution.py:830
  159.9 0.7 copy-done.14
  160.6 0.3 copy.67
  160.9 0.2 slice_reduce_fusion
  161.1 0.4 fusion.1
  161.5 1.1 broadcast_select_fusion.1
  162.6 61.9 %shard_map.306 = (bf16[4,4224,512]{2,1,0:T(8,128)(2,1)}, bf16[2,1024,768]{2,1,0:T(8,128)(2,1)}, bf16[2,1024,768]{2,1,0:T(8,128)(2,1)}, bf16[2,1024,768]{2,1,0:T(8,128)(2,1)}, f32[1024,8]{1,0:T(8,128)}) custom-call(bf16[1024,2048]{1,0:T(8,128)(2,1)} %get-tuple-element.63.n2_hbm, bf16[1024,2048]{1,0:T(8,128)(2,1)} %get-tuple-element.64.dy_hbm, ...), custom_call_target="tpu_custom_call" | custom-call | tf_op jit(solution)/shard_map/pallas_call | solution.py:490
  224.7 0.6 copy-done.13
  225.3 0.3 copy.78
  225.7 0.2 slice.44
  225.9 0.2 copy.76
  226.0 0.2 copy.70
  226.2 0.2 broadcast_subtract_fusion
  226.5 0.2 copy.75
  226.6 0.2 copy.74
  226.8 0.2 multiply_reduce_fusion.1
  227.1 0.2 copy.69
  227.3 0.2 copy.77
  227.5 0.9 pad.9.refs_13_
  228.4 0.8 pad.8.refs_12_
  229.1 97.8 %shard_map.307 = (bf16[1024,2048]{1,0:T(8,128)(2,1)}, f32[128,2048]{1,0:T(8,128)}, f32[16,2048]{1,0:T(8,128)}) custom-call(bf16[2,1024,768]{2,1,0:T(8,128)(2,1)} %get-tuple-element.69.refs_0_.refs_1_, bf16[2,1024,768]{2,1,0:T(8,128)(2,1)} %get-tuple-element.69.refs_0_.refs_1_, bf16[2,1024,768]{2,1,0:T(8,128)(2,1)} %get-tuple-element.70.refs_2_.refs_3_, ...), custom_call_target="tpu_custom_call" | custom-call | tf_op jit(solution)/shard_map/pallas_call | solution.py:1215
  326.9 57.6 %shard_map.308 = (bf16[1024,768]{1,0:T(8,128)(2,1)}, bf16[16,1024,128]{2,1,0:T(8,128)(2,1)}, bf16[4,2112,128]{2,1,0:T(8,128)(2,1)}) custom-call(bf16[1024,2048]{1,0:T(8,128)(2,1)} %get-tuple-element.76.dh_hbm, bf16[1024,2048]{1,0:T(8,128)(2,1)} %get-tuple-element.77.n1_hbm, bf16[1024,768]{1,0:T(8,128)(2,1)} %get-tuple-element.78.qkv_ref, ...), custom_call_target="tpu_custom_call" | custom-call | tf_op jit(solution)/shard_map/pallas_call | solution.py:992
  384.6 0.8 copy-done.11
  385.5 0.1 slice_reduce_fusion.1
  385.6 0.3 copy-done.2
  385.9 0.3 multiply_reduce_fusion
  386.2 0.6 pad_maximum_fusion.3
  386.8 2.9 fusion.7
  389.8 80.4 %shard_map.309 = (f32[256,2048]{1,0:T(8,128)}, f32[256,2048]{1,0:T(8,128)}, f32[16,2048]{1,0:T(8,128)}) custom-call(bf16[2,1024,768]{2,1,0:T(8,128)(2,1)} %get-tuple-element.67.refs_0_.refs_1_, bf16[2,1024,768]{2,1,0:T(8,128)(2,1)} %get-tuple-element.67.refs_0_.refs_1_, bf16[2,704,2048]{2,1,0:T(8,128)(2,1)} %bitcast.54, bf16[2,704,2048]{2,1,0:T(8,128)(2,1)} %bitcast.55, ...), custom_call_target="tpu_custom_call" | custom-call | tf_op jit(solution)/shard_map/pallas_call | solution.py:1330
  470.2 0.9 reduce_sum.48
  471.2 2.8 shard_map.310
  474.2 0.7 bitcast_bitcast_fusion.small_ref
  474.8 6.1 %convert_bitcast_fusion = (f32[2,512,704]{1,2,0:T(8,128)}, f32[2,512,704]{1,2,0:T(8,128)}, f32[2,512,704]{1,2,0:T(8,128)}) fusion(bf16[2,3,704,512]{3,2,1,0:T(8,128)(2,1)} %bitcast.64), kind=kLoop, calls=%fused_computation | loop fusion | flops 2162688 | bytes 12976128 | tf_op jit(solution)/shard_map/transpose | solution.py:1489
  480.9 35.9 %shard_map.311 = (f32[128,1024]{1,0:T(8,128)}, f32[128,1024]{1,0:T(8,128)}, f32[128,1024]{1,0:T(8,128)}, f32[128,1024]{1,0:T(8,128)}, f32[16,128]{1,0:T(8,128)}) custom-call(bf16[4,1024,128]{2,1,0:T(8,128)(2,1)} %bitcast.67, f32[16,16,128]{2,1,0:T(8,128)} %bitcast_bitcast_fusion.small_ref), custom_call_target="tpu_custom_call" | custom-call | tf_op jit(solution)/shard_map/pallas_call | solution.py:1072
  516.9 1.3 slice_bitcast_fusion.1
  518.2 1.3 slice_bitcast_fusion
  519.5 3.1 copy.88
  522.6 1.3 copy.89
  524.0 0.8 copy.90
  524.8 0.8 copy.91
  525.5 0.8 copy.92
  526.3 0.8 copy.93
  (51 shorter events, 0.7 us)
Async XLA Ops:
  7.2 319.7 %reduce-scatter.4.cloned.1.call-start = ((), (), s32[]{:S(2)}) async-start(), calls=%async_computation.3 | async-start | bytes 10813440 | tf_op jit(solution)/shard_map/reduce_scatter | solution.py:1457
  159.8 0.8 copy-start.14
  159.8 1.1 copy-start.1
  159.9 314.3 %reduce-scatter.8.cloned.1.call-start = ((), (), s32[]{:S(2)}) async-start(), calls=%async_computation.5 | async-start | bytes 21626880 | tf_op jit(solution)/shard_map/reduce_scatter | solution.py:1457
  224.6 0.7 copy-start.13
  224.6 0.8 copy-start.12
  224.6 1.1 copy-start.4
  224.6 2.2 copy-start.5
  224.6 256.3 %reduce-scatter.6.cloned.1.call-start = ((), (), s32[]{:S(2)}) async-start(), calls=%async_computation.4 | async-start | bytes 5242880 | tf_op jit(solution)/shard_map/reduce_scatter | solution.py:1457
  384.5 0.9 copy-start.11
  384.5 1.0 copy-start.10
  384.5 1.4 copy-start.2
  389.8 81.4 %copy-start = (bf16[4,2112,128]{2,1,0:T(8,128)(2,1)S(1)}, bf16[4,2112,128]{2,1,0:T(8,128)(2,1)}, u32[]{:S(2)}) copy-start(bf16[4,2112,128]{2,1,0:T(8,128)(2,1)} %get-tuple-element.94.box_ref) | copy-start | bytes 6488068
  480.9 41.7 %copy-start.3 = (f32[256,2048]{1,0:T(8,128)S(1)}, f32[256,2048]{1,0:T(8,128)}, u32[]{:S(2)}) copy-start(f32[256,2048]{1,0:T(8,128)} %get-tuple-element.141) | copy-start | bytes 6291460
  522.6 1.3 copy-start.9
  522.6 2.1 copy-start.8
  522.6 2.9 copy-start.7
  522.6 3.7 copy-start.6
Sparse Core Ops, SparseCore 0:
  160.0 96.2 reduce-scatter.3
  259.4 158.0 reduce-scatter.7
  420.7 52.6 reduce-scatter.5

commit v2 on v1

--- a/solution.py
+++ b/solution.py
@@ -295,10 +295,8 @@
         lax.fori_loop(0, self.nz, one, 0)
 
 
-def params(name, **more):
-    return pltpu.CompilerParams(
-        collective_id=name, has_side_effects=True, vmem_limit_bytes=56 * 1024 * 1024, **more
-    )
+def params(name, room=56):
+    return pltpu.CompilerParams(collective_id=name, has_side_effects=True, vmem_limit_bytes=room * 1024 * 1024)
 
 
 VMEM = pl.BlockSpec(memory_space=pltpu.VMEM)
@@ -1010,26 +1008,14 @@
     )(d_h, n1, qkv, probs, o, out_weight, part)
 
 
-def finish_gradients(nz, part, splits, small, name):
+def spread_turned(nz, part, splits, name):
     _, columns, block = part.shape
     cols = columns // splits
-    n, rows, lanes = small.shape
-
-    def kernel(in_ref, small_ref, *rest):
-        outs, sum_ref, rest = rest[:splits], rest[splits], rest[splits + 1 :]
-        box, s_box, total, other, send_sem, recv_sem, s_send, s_recv, swap_sem = rest
+
+    def kernel(in_ref, *rest):
+        outs, (box, send_sem, recv_sem) = rest[:splits], rest[splits:]
         z, c = here()
-        me = lax.axis_index("dp") * nz + z
-        barrier = pltpu.get_barrier_semaphore()
-
-        def peer(k):
-            at = lax.rem(me + k, n)
-            return at, {"dp": at // nz, "expert": lax.rem(at, nz)}
-
-        pl.semaphore_signal(barrier, inc=1, device_id={"tensor": 1 - c}, device_id_type=MESH)
-        for k in range(1, n):
-            pl.semaphore_signal(barrier, inc=1, device_id=peer(k)[1], device_id_type=MESH)
-        pl.semaphore_wait(barrier, n)
+        greet(nz)
 
         def send(way, d):
             to = z + d if way == UP else z - d
@@ -1039,24 +1025,10 @@
             dst = box.at[z - d if way == UP else z + d]
             remote(dst, dst, send_sem.at[way, d], recv_sem.at[way, d], {"tensor": 1 - c}).wait_recv()
 
-        def send_small(k):
-            at, device = peer(k)
-            return remote(small_ref.at[at], s_box.at[k], s_send.at[k], s_recv.at[k], device)
-
-        for k in range(1, n):
-            send_small(k).start()
         for d in range(nz - 1, 0, -1):
             for way in (UP, DOWN):
                 pl.when(z + d < nz if way == UP else z >= d)(lambda way=way, d=d: send(way, d).start())
         box[z] = in_ref[z]
-        total[...] = small_ref[me]
-        for k in range(1, n):
-            send_small(k).wait_recv()
-            total[...] += s_box[k]
-        swap = remote(total, other, swap_sem.at[0], swap_sem.at[1], {"tensor": 1 - c})
-        swap.start()
-        swap.wait_recv()
-        sum_ref[...] = total[...] + other[...]
         for d in range(1, nz):
             for way in (UP, DOWN):
                 pl.when(z + d < nz if way == UP else z >= d)(lambda way=way, d=d: send(way, d).wait_send())
@@ -1065,22 +1037,17 @@
             for b in range(nz):
                 value = box[b, j * cols : (j + 1) * cols, :].astype(f32).T
                 outs[j][:, b * cols : (b + 1) * cols] = value
-        swap.wait_send()
-        for k in range(1, n):
-            send_small(k).wait_send()
 
     return pl.pallas_call(
         kernel,
-        out_shape=[jax.ShapeDtypeStruct((block, nz * cols), f32)] * splits + [jax.ShapeDtypeStruct((rows, lanes), f32)],
-        in_specs=[VMEM] * 2,
-        out_specs=[VMEM] * (splits + 1),
+        out_shape=[jax.ShapeDtypeStruct((block, nz * cols), f32)] * splits,
+        in_specs=[VMEM],
+        out_specs=[VMEM] * splits,
         scratch_shapes=[
-            pltpu.VMEM(part.shape, bf16), pltpu.VMEM((n, rows, lanes), f32), pltpu.VMEM((rows, lanes), f32),
-            pltpu.VMEM((rows, lanes), f32), pltpu.SemaphoreType.DMA((2, nz)), pltpu.SemaphoreType.DMA((2, nz)),
-            pltpu.SemaphoreType.DMA((n,)), pltpu.SemaphoreType.DMA((n,)), pltpu.SemaphoreType.DMA((2,)),
+            pltpu.VMEM(part.shape, bf16), pltpu.SemaphoreType.DMA((2, nz)), pltpu.SemaphoreType.DMA((2, nz)),
         ],
         compiler_params=params(name),
-    )(part, small)
+    )(part)
 
 
 PART = 512
@@ -1229,16 +1196,19 @@
     )(*products.inputs, h, gain, upstream)
 
 
-def reduce_last(nz, d_heads, weights, x, gain, dh, products, h, name):
+def reduce_last(nz, d_heads, weights, x, gain, dh, products, h, small, box, name):
     rows, width = x.shape
     cols = d_heads.shape[1] // 3
+    n, small_rows, lanes = small.shape
+    box_rows, block = box.shape[1] // 3, box.shape[2]
     n_in, n_scratch = len(products.inputs), len(products.scratch)
 
     def kernel(*refs):
-        p_refs, (d_ref, wq_hbm, wk_hbm, wv_hbm, x_ref, gain_ref, dh_ref, h_ref, in_ref, out_ref, gg_ref) = (
-            refs[:n_in], refs[n_in : n_in + 11],
-        )
-        rest = refs[n_in + 11 :]
+        p_refs, (
+            d_ref, wq_hbm, wk_hbm, wv_hbm, x_ref, gain_ref, dh_ref, h_ref, small_ref, box_ref, in_ref, out_ref, sum_ref, *turned,
+        ) = refs[:n_in], refs[n_in : n_in + 16]
+        gg_ref, s_out, s_box, s_total, s_other, s_send, s_recv, swap_sem = refs[n_in + 16 : n_in + 24]
+        rest = refs[n_in + 24 :]
         p_scratch, (d_part, b_part, own, sems, w_ref, w_sem), rest = (
             rest[:n_scratch], rest[n_scratch : n_scratch + 6], rest[n_scratch + 6 :],
         )
@@ -1253,8 +1223,23 @@
         d_total, b_total = d_scratch[3], b_scratch[3]
         products.bind(p_refs, p_scratch)
         first, second = Reducer(nz, d_part, *d_scratch), Reducer(nz, b_part, *b_scratch)
-        greet(nz)
         z, c = here()
+        me = lax.axis_index("dp") * nz + z
+        barrier = pltpu.get_barrier_semaphore()
+
+        def peer(q):
+            to = lax.rem(me + q, n)
+            return to, {"dp": to // nz, "expert": lax.rem(to, nz)}
+
+        pl.semaphore_signal(barrier, inc=1, device_id={"tensor": 1 - c}, device_id_type=MESH)
+        for q in range(1, n):
+            pl.semaphore_signal(barrier, inc=1, device_id=peer(q)[1], device_id_type=MESH)
+        pl.semaphore_wait(barrier, n)
+
+        def send_small(q):
+            to, device = peer(q)
+            return remote(s_out.at[to], s_box.at[q], s_send.at[q], s_recv.at[q], device)
+
         ends = first.ends()
         middle = jnp.logical_not(ends)
 
@@ -1295,6 +1280,10 @@
         lax.fori_loop(0, nz, one, 0)
         lax.fori_loop(0, nz, two, 0)
         lax.fori_loop(0, nz - 1, three, 0)
+        for i in range(3):
+            for b in range(nz):
+                value = box_ref[b, i * box_rows : (i + 1) * box_rows, :].astype(f32).T
+                turned[i][:, b * box_rows : (b + 1) * box_rows] = value
         first.finish()
         gg_ref[...] = jnp.zeros_like(gg_ref)
 
@@ -1314,6 +1303,12 @@
 
         for copy in leave(0, in_ref):
             copy.start()
+        first_row = jnp.sum(gg_ref[...], axis=0, keepdims=True)
+        for q in range(n):
+            s_out[q] = small_ref[q]
+            s_out[q, :1, :] = first_row[:, q * lanes : (q + 1) * lanes]
+        for q in range(1, n):
+            send_small(q).start()
         second.finish()
 
         def last(at):
@@ -1322,8 +1317,19 @@
         strips(rows, last)
         for copy in leave(1, out_ref):
             copy.start()
+        s_total[...] = s_out[me]
+        for q in range(1, n):
+            send_small(q).wait_recv()
+            s_total[...] += s_box[q]
+        swap = remote(s_total, s_other, swap_sem.at[0], swap_sem.at[1], {"tensor": 1 - c})
+        swap.start()
         first.drain()
         second.drain()
+        swap.wait_recv()
+        sum_ref[...] = s_total[...] + s_other[...]
+        swap.wait_send()
+        for q in range(1, n):
+            send_small(q).wait_send()
         for copy in (*leave(0, in_ref), *leave(1, out_ref)):
             copy.wait()
 
@@ -1332,38 +1338,25 @@
         out_shape=[
             jax.ShapeDtypeStruct((2 * rows, width), f32),
             jax.ShapeDtypeStruct((2 * rows, width), f32),
-            jax.ShapeDtypeStruct((STRIP, width), f32),
-        ],
-        in_specs=products.specs + [VMEM] + [ANY] * 3 + [VMEM] * 4,
-        out_specs=[ANY, ANY, VMEM],
-        scratch_shapes=products.scratch
+            jax.ShapeDtypeStruct((small_rows, lanes), f32),
+        ]
+        + [jax.ShapeDtypeStruct((block, nz * box_rows), f32)] * 3,
+        in_specs=products.specs + [VMEM] + [ANY] * 3 + [VMEM] * 6,
+        out_specs=[ANY, ANY] + [VMEM] * 4,
+        scratch_shapes=[
+            pltpu.VMEM((STRIP, width), f32), pltpu.VMEM(small.shape, f32), pltpu.VMEM(small.shape, f32),
+            pltpu.VMEM((small_rows, lanes), f32), pltpu.VMEM((small_rows, lanes), f32),
+            pltpu.SemaphoreType.DMA((n,)), pltpu.SemaphoreType.DMA((n,)), pltpu.SemaphoreType.DMA((2,)),
+        ]
+        + products.scratch
         + [
             pltpu.VMEM((nz * 2 * rows, width), bf16), pltpu.VMEM((nz * 2 * rows, width), bf16),
             pltpu.VMEM((2, rows, width), f32), pltpu.SemaphoreType.DMA((2, 3)),
             pltpu.VMEM((width, 3 * cols), bf16), pltpu.SemaphoreType.DMA((3,)),
         ]
         + reduce_scratch(nz, rows, width) * 2,
-        compiler_params=params(name),
-    )(*products.inputs, d_heads, *weights, x, gain, dh, h)
-
-
-def assemble(nz, box, columns):
-    block = box.shape[2]
-    count = 3
-
-    def kernel(box_ref, *outs):
-        for k in range(count):
-            for b in range(nz):
-                value = box_ref[b, k * columns : (k + 1) * columns, :].astype(f32).T
-                outs[k][:, b * columns : (b + 1) * columns] = value
-
-    return pl.pallas_call(
-        kernel,
-        out_shape=[jax.ShapeDtypeStruct((block, nz * columns), f32)] * count,
-        in_specs=[VMEM],
-        out_specs=[VMEM] * count,
-        compiler_params=pltpu.CompilerParams(vmem_limit_bytes=40 * 1024 * 1024),
-    )(box)
+        compiler_params=params(name, 60),
+    )(*products.inputs, d_heads, *weights, x, gain, dh, h, small, box)
 
 
 def cross_rows(left, right):
@@ -1470,27 +1463,25 @@
         None,
     )
     dh_now, _ = lax.optimization_barrier((dh, grad_attention))
-    input_grad, layer_out, grad_one = reduce_last(
-        nz, d_heads, (q_weight, k_weight, v_weight), x, gain1, dh_now, branch, h, 3
-    )
-    stats = jnp.stack([inverse_one_rows, inverse_two[:, 0]])
-
     small_rows = jnp.concatenate(
         [
-            jnp.sum(grad_one, axis=0)[None], jnp.sum(grad_two, axis=0)[None], small_grad.T,
+            jnp.zeros((1, width), f32), jnp.sum(grad_two, axis=0)[None], small_grad.T,
             jnp.zeros((13 - expert_count, width), f32),
         ],
         axis=0,
     )
-    small_rows, expert_part = lax.optimization_barrier((small_rows, expert_part))
     count = ndp * nz
     small_blocks = jnp.swapaxes(small_rows.reshape(16, count, width // count), 0, 1)
-    s_gate, s_up, s_down = assemble(nz, shared_box, shared_cols)
+    input_grad, layer_out, small_all, s_gate, s_up, s_down = reduce_last(
+        nz, d_heads, (q_weight, k_weight, v_weight), x, gain1, dh_now, branch, h, small_blocks, shared_box, 3
+    )
+    stats = jnp.stack([inverse_one_rows, inverse_two[:, 0]])
+
     e_gate, e_up, e_down = (jnp.swapaxes(expert_part[:, k].astype(f32), 1, 2) for k in range(3))
-    attention_part, small_blocks, e_gate, e_up, e_down, s_gate = lax.optimization_barrier(
-        (attention_part, small_blocks, e_gate, e_up, e_down, s_gate)
+    attention_part, e_gate, e_up, e_down, small_all = lax.optimization_barrier(
+        (attention_part, e_gate, e_up, e_down, small_all)
     )
-    g_q, g_k, g_v, g_o, small_all = finish_gradients(nz, attention_part, 4, small_blocks, 6)
+    g_q, g_k, g_v, g_o = spread_turned(nz, attention_part, 4, 6)
     g_one, g_two, g_router, g_vector = small_all[0], small_all[1], small_all[2 : 2 + expert_count].T, small_all[2 + expert_count]
     return (
         layer_out, input_grad, stats, g_one, g_q, g_k, g_v, g_o, g_two, g_router, g_vector,

time: 539 us -> 536 us (level)
    pallas_call x2 -> x1, Pallas kernels: 38.8 us -> 30.9 us  [spread_turned(): pl.pallas_call(kernel, out_shape=[jax.ShapeDtypeStruct((block, nz * cols)...]
    unnamed x36 -> x46, local copies, waits for them, and re-layouts: 10.1 us -> 12.3 us
  transfers between devices with their start and end apart: 3 -> 3, of which waited for: 0 -> 0; matrix products, arithmetic and copies ran while one was open for 3% -> 3% of each run, Pallas kernels for 56% -> 57%
where the time goes in v2:
time: 536 us; the launch traced here: 532 us
  Pallas kernels  478 us (89%)
  local copies, waits for them, and re-layouts  20.2 us (4%)
  other arithmetic  15.4 us (3%)
  between operations  14.6 us (3%)
    pallas_call x1, Pallas kernels, forward_layer(): pl.pallas_call(kernel, out_shape=[jax.ShapeDtypeStruct((seq, width), bf16...  144 us
    pallas_call x1, Pallas kernels, reduce_and_gather(): pl.pallas_call(kernel, out_shape=[jax.ShapeDtypeStruct((nz * 2 * rows, wi...  97.8 us
    pallas_call x1, Pallas kernels, reduce_last(): pl.pallas_call(kernel, out_shape=[jax.ShapeDtypeStruct((2 * rows, width),...  85.6 us
    pallas_call x1, Pallas kernels, hidden_layer(): pl.pallas_call(kernel, out_shape=[jax.ShapeDtypeStruct((groups, experts *...  61.9 us
    pallas_call x1, Pallas kernels, attention_back(): pl.pallas_call(kernel, out_shape=[jax.ShapeDtypeStruct((seq, 3 * cols), b...  57.6 us
    pallas_call x1, Pallas kernels, spread_turned(): pl.pallas_call(kernel, out_shape=[jax.ShapeDtypeStruct((block, nz * cols)...  30.9 us
    unnamed x46, local copies, waits for them, and re-layouts  12.3 us
  transfers between devices with their start and end apart: 3, of which 0 were waited for; matrix products, arithmetic and copies ran while one was open for 3% of the time, Pallas kernels for 57%

profile of v2, /device:TPU:8, one launch (start us, length us, event | category | flops | bytes accessed | tf_op | source)
XLA Modules:
  0.0 531.6 jit_solution(14360654996977986234)
XLA Ops:
  7.3 1.3 broadcast_in_dim.45
  8.6 1.3 broadcast_in_dim.46
  9.9 0.7 broadcast_in_dim.40
  10.6 1.4 pad_maximum_fusion.small_ref
  12.0 1.4 add_add_fusion.marks_ref
  13.3 2.3 constant_dynamic-slice_fusion
  15.6 144.2 %shard_map.305 = (bf16[1024,2048]{1,0:T(8,128)(2,1)}, bf16[1024,2048]{1,0:T(8,128)(2,1)}, s32[4,8,256]{2,1,0:T(8,128)}, bf16[1024,768]{1,0:T(8,128)(2,1)}, bf16[...) custom-call(bf16[128,2048]{1,0:T(8,128)(2,1)} %get-tuple-element.114, ...), custom_call_target="tpu_custom_call" | custom-call | tf_op jit(solution)/shard_map/pallas_call | solution.py:828
  159.9 0.7 copy-done.16
  160.6 0.3 copy.67
  160.9 0.2 slice_reduce_fusion
  161.1 0.4 fusion.1
  161.5 1.1 broadcast_select_fusion.1
  162.6 61.9 %shard_map.306 = (bf16[4,4224,512]{2,1,0:T(8,128)(2,1)}, bf16[2,1024,768]{2,1,0:T(8,128)(2,1)}, bf16[2,1024,768]{2,1,0:T(8,128)(2,1)}, bf16[2,1024,768]{2,1,0:T(8,128)(2,1)}, f32[1024,8]{1,0:T(8,128)}) custom-call(bf16[1024,2048]{1,0:T(8,128)(2,1)} %get-tuple-element.59.n2_hbm, bf16[1024,2048]{1,0:T(8,128)(2,1)} %get-tuple-element.60.dy_hbm, ...), custom_call_target="tpu_custom_call" | custom-call | tf_op jit(solution)/shard_map/pallas_call | solution.py:488
  224.7 0.6 copy-done.15
  225.2 0.1 copy-done.14
  225.3 0.3 copy.78
  225.6 0.2 slice.44
  225.8 0.2 copy.76
  226.0 0.2 copy.70
  226.2 0.2 broadcast_subtract_fusion
  226.4 0.2 copy.75
  226.6 0.2 copy.74
  226.8 0.2 multiply_reduce_fusion.1
  227.0 0.2 copy.69
  227.3 0.2 copy.77
  227.5 0.9 pad.9.refs_13_
  228.4 0.8 pad.8.refs_12_
  229.1 97.8 %shard_map.307 = (bf16[1024,2048]{1,0:T(8,128)(2,1)}, f32[128,2048]{1,0:T(8,128)}, f32[16,2048]{1,0:T(8,128)}) custom-call(bf16[2,1024,768]{2,1,0:T(8,128)(2,1)} %get-tuple-element.65.refs_0_.refs_1_, bf16[2,1024,768]{2,1,0:T(8,128)(2,1)} %get-tuple-element.65.refs_0_.refs_1_, bf16[2,1024,768]{2,1,0:T(8,128)(2,1)} %get-tuple-element.66.refs_2_.refs_3_, ...), custom_call_target="tpu_custom_call" | custom-call | tf_op jit(solution)/shard_map/pallas_call | solution.py:1182
  327.0 57.6 %shard_map.308 = (bf16[1024,768]{1,0:T(8,128)(2,1)}, bf16[16,1024,128]{2,1,0:T(8,128)(2,1)}, bf16[4,2112,128]{2,1,0:T(8,128)(2,1)}) custom-call(bf16[1024,2048]{1,0:T(8,128)(2,1)} %get-tuple-element.72.dh_hbm, bf16[1024,2048]{1,0:T(8,128)(2,1)} %get-tuple-element.73.n1_hbm, bf16[1024,768]{1,0:T(8,128)(2,1)} %get-tuple-element.74.qkv_ref, ...), custom_call_target="tpu_custom_call" | custom-call | tf_op jit(solution)/shard_map/pallas_call | solution.py:990
  384.7 3.2 fusion.6
  388.1 0.1 slice_reduce_fusion.1
  388.2 0.3 multiply_reduce_fusion
  388.5 0.6 pad_maximum_fusion.3
  389.1 0.7 maximum_bitcast_fusion.refs_14_
  389.9 85.6 %shard_map.309 = (f32[256,2048]{1,0:T(8,128)}, f32[256,2048]{1,0:T(8,128)}, f32[16,128]{1,0:T(8,128)}, f32[128,2816]{1,0:T(8,128)}, f32[128,2816]{1,0:T(8,128)}, /*index=5*/f32[128,2816]{1,0:T(8,128)}) custom-call(bf16[2,1024,768]{2,1,0:T(8,128)(2,1)} %get-tuple-element.63.refs_0_.refs_1_, bf16[2,1024,768]{2,1,0:T(8,128)(2,1)} %get-tuple-element.63.refs_0_.refs_1_, ...), custom_call_target="tpu_custom_call" | custom-call | tf_op jit(solution)/shard_map/pallas_call | solution.py:1336
  475.5 6.1 %convert_bitcast_fusion = (f32[2,512,704]{1,2,0:T(8,128)}, f32[2,512,704]{1,2,0:T(8,128)}, f32[2,512,704]{1,2,0:T(8,128)}) fusion(bf16[2,3,704,512]{3,2,1,0:T(8,128)(2,1)} %bitcast.67), kind=kLoop, calls=%fused_computation | loop fusion | flops 2162688 | bytes 12976128 | tf_op jit(solution)/shard_map/transpose | solution.py:1480
  481.6 0.5 slice_bitcast_fusion.4
  482.2 0.6 slice_bitcast_fusion.3
  482.8 30.9 %shard_map.310 = (f32[128,1024]{1,0:T(8,128)}, f32[128,1024]{1,0:T(8,128)}, f32[128,1024]{1,0:T(8,128)}, f32[128,1024]{1,0:T(8,128)}) custom-call(bf16[4,1024,128]{2,1,0:T(8,128)(2,1)} %bitcast.70), custom_call_target="tpu_custom_call" | custom-call | tf_op jit(solution)/shard_map/pallas_call | solution.py:1041
  513.7 3.1 copy.90
  516.9 1.3 copy.91
  518.2 0.8 copy.92
  519.0 0.8 copy.93
  519.8 0.8 copy.94
  520.6 0.8 copy.95
  521.4 1.1 copy.96
  522.5 1.1 copy.97
  523.6 1.1 copy.98
  (61 shorter events, 0.7 us)
Async XLA Ops:
  7.2 319.8 %reduce-scatter.4.cloned.1.call-start = ((), (), s32[]{:S(2)}) async-start(), calls=%async_computation.3 | async-start | bytes 10813440 | tf_op jit(solution)/shard_map/reduce_scatter | solution.py:1450
  159.8 0.8 copy-start.16
  159.8 1.1 copy-start
  159.9 315.6 %reduce-scatter.8.cloned.1.call-start = ((), (), s32[]{:S(2)}) async-start(), calls=%async_computation.5 | async-start | bytes 21626880 | tf_op jit(solution)/shard_map/reduce_scatter | solution.py:1450
  224.5 0.7 copy-start.15
  224.6 0.8 copy-start.14
  224.6 1.1 copy-start.6
  224.6 2.2 copy-start.7
  224.6 257.0 %reduce-scatter.6.cloned.1.call-start = ((), (), s32[]{:S(2)}) async-start(), calls=%async_computation.4 | async-start | bytes 5242880 | tf_op jit(solution)/shard_map/reduce_scatter | solution.py:1450
  384.7 3.4 copy-start.13
  384.7 3.4 copy-start.12
  384.7 3.5 copy-start.1
  475.5 6.1 %copy-start.17 = (f32[16,128]{1,0:T(8,128)S(1)}, f32[16,128]{1,0:T(8,128)}, u32[]{:S(2)}) copy-start(f32[16,128]{1,0:T(8,128)} %get-tuple-element.89) | copy-start | bytes 24580
  481.6 35.2 %copy-start.2 = (f32[256,2048]{1,0:T(8,128)S(1)}, f32[256,2048]{1,0:T(8,128)}, u32[]{:S(2)}) copy-start(f32[256,2048]{1,0:T(8,128)} %get-tuple-element.133) | copy-start | bytes 6291460
  516.8 1.3 copy-start.11
  516.8 2.1 copy-start.10
  516.8 2.9 copy-start.9
  516.8 3.7 copy-start.8
  518.2 3.2 copy-start.5
  519.0 3.5 copy-start.4
  521.4 2.2 copy-start.3
Sparse Core Ops, SparseCore 0:
  160.0 96.2 reduce-scatter.3
  259.4 158.1 reduce-scatter.7
  420.8 54.4 reduce-scatter.5

commit v3 on v2

--- a/solution.py
+++ b/solution.py
@@ -869,7 +869,7 @@
     )(x, gain, upstream, marks, gain2, small, *weights, out_weight, *shared)
 
 
-def attention_back(nz, d_h, n1, qkv, probs, o, out_weight, groups, part, name):
+def attention_back(nz, d_h, n1, qkv, probs, o, out_weight, groups, part, n2, small, name):
     seq, width = d_h.shape
     heads = probs.shape[0]
     cols = o.shape[1]
@@ -881,14 +881,15 @@
     strip = 32
     scale = HD ** (-0.5)
 
-    def kernel(dh_hbm, n1_hbm, qkv_ref, p_ref, o_ref, wo_hbm, part_hbm, heads_ref, grad_hbm, box_hbm,
-               b_send, b_recv, b_local, dh_ref, n1_ref, wo, d_o, scores, ds, dk, dv, turned, o_turned, slab, in_sem, slab_sem):
+    def kernel(dh_hbm, n1_hbm, qkv_ref, p_ref, o_ref, wo_hbm, part_hbm, n2_hbm, small_ref, heads_ref, grad_hbm, box_hbm,
+               sum_ref, n2_ref, s_turned, b_send, b_recv, b_local, dh_ref, n1_ref, wo, d_o, scores, ds, dk, dv, turned, o_turned, slab, in_sem, slab_sem):
         z, c = here()
         at = pl.ds(pl.multiple_of(z * cols, cols), cols)
         loads = [
             pltpu.make_async_copy(wo_hbm.at[:, at], wo, in_sem.at[0]),
             pltpu.make_async_copy(dh_hbm, dh_ref, in_sem.at[1]),
             pltpu.make_async_copy(n1_hbm, n1_ref, in_sem.at[2]),
+            pltpu.make_async_copy(n2_hbm, n2_ref, in_sem.at[3]),
         ]
         for load in loads:
             load.start()
@@ -908,6 +909,7 @@
             for way in (UP, DOWN):
                 pl.when(z + d < nz if way == UP else z >= d)(lambda way=way, d=d: send(way, d).start())
         o_turned[...] = o_ref[...].T
+        s_turned[...] = small_ref[...].T
         loads[0].wait()
         loads[1].wait()
 
@@ -957,6 +959,7 @@
 
         tiles(seq // TILE, turn)
         loads[2].wait()
+        loads[3].wait()
 
         def leave(i):
             slot = lax.rem(i, 2)
@@ -973,6 +976,8 @@
             pl.when(i >= 2)(lambda: leave(i).wait())
             inner = nn_dot(turned[...], n1_ref[:, to]).astype(bf16)
             outer = nn_dot(o_turned[...], dh_ref[:, to]).astype(bf16)
+            both = nn_dot(s_turned[:32, :], n2_ref[:, to])
+            sum_ref[:, to] = both[:16, :] + both[16:, :]
             for j in range(per):
                 slab[slot, j, : 3 * cols, :] = inner[:, j * lane : (j + 1) * lane]
                 slab[slot, j, 3 * cols :, :] = outer[:, j * lane : (j + 1) * lane]
@@ -993,19 +998,21 @@
             jax.ShapeDtypeStruct((seq, 3 * cols), bf16),
             jax.ShapeDtypeStruct((groups, 4 * cols, block), bf16),
             jax.ShapeDtypeStruct(part.shape, bf16),
+            jax.ShapeDtypeStruct((16, width), f32),
         ],
-        in_specs=[ANY, ANY, VMEM, VMEM, VMEM, ANY, ANY],
-        out_specs=[VMEM, ANY, ANY],
+        in_specs=[ANY, ANY, VMEM, VMEM, VMEM, ANY, ANY, ANY, VMEM],
+        out_specs=[VMEM, ANY, ANY, VMEM],
         scratch_shapes=[
+            pltpu.VMEM((seq, width), bf16), pltpu.VMEM((small.shape[1], seq), bf16),
             pltpu.SemaphoreType.DMA((2, nz)), pltpu.SemaphoreType.DMA((2, nz)), pltpu.SemaphoreType.DMA,
             pltpu.VMEM((seq, width), bf16), pltpu.VMEM((seq, width), bf16), pltpu.VMEM((width, cols), bf16),
             pltpu.VMEM((seq, cols), bf16), pltpu.VMEM((full, seq), f32), pltpu.VMEM((full, seq), bf16),
             pltpu.VMEM((seq, HD), f32), pltpu.VMEM((seq, HD), f32),
             pltpu.VMEM((3 * cols, seq), bf16), pltpu.VMEM((cols, seq), bf16), pltpu.VMEM((2, per, 4 * cols, lane), bf16),
-            pltpu.SemaphoreType.DMA((3,)), pltpu.SemaphoreType.DMA((2,)),
+            pltpu.SemaphoreType.DMA((4,)), pltpu.SemaphoreType.DMA((2,)),
         ],
         compiler_params=params(name),
-    )(d_h, n1, qkv, probs, o, out_weight, part)
+    )(d_h, n1, qkv, probs, o, out_weight, part, n2, small)
 
 
 def spread_turned(nz, part, splits, name):
@@ -1309,20 +1316,20 @@
             s_out[q, :1, :] = first_row[:, q * lanes : (q + 1) * lanes]
         for q in range(1, n):
             send_small(q).start()
-        second.finish()
-
-        def last(at):
-            own[1, at, :] = h_ref[at, :] + b_total[at, :]
-
-        strips(rows, last)
-        for copy in leave(1, out_ref):
-            copy.start()
         s_total[...] = s_out[me]
         for q in range(1, n):
             send_small(q).wait_recv()
             s_total[...] += s_box[q]
         swap = remote(s_total, s_other, swap_sem.at[0], swap_sem.at[1], {"tensor": 1 - c})
         swap.start()
+        second.finish()
+
+        def last(at):
+            own[1, at, :] = h_ref[at, :] + b_total[at, :]
+
+        strips(rows, last)
+        for copy in leave(1, out_ref):
+            copy.start()
         first.drain()
         second.drain()
         swap.wait_recv()
@@ -1441,8 +1448,8 @@
         [((da_s, 0), shared_gate_weight), ((db_s, 0), shared_up_weight)],
         (jnp.pad(small_high, fill), jnp.pad(small_weights, fill)),
     )
-    small_grad = cross_rows(n2, jnp.concatenate([small_high, small_low], axis=1))
-    small_grad = small_grad[:, : expert_count + 1] + small_grad[:, expert_count + 1 :]
+    few = small.shape[1]
+    mixed = jnp.pad(small_high, ((0, 0), (2, 126 - few))) + jnp.pad(small_low, ((0, 0), (18, 110 - few)))
 
 
     def over_dp(grad):
@@ -1452,8 +1459,8 @@
     shared_part = over_dp(grad_s).reshape((nz,) + grad_s.shape[1:])
     expert_part = over_dp(grad_e).reshape(local_count, 3, ffn, -1)
     dhr, dh, grad_two = reduce_and_gather(nz, d_n2, h, gain2, upstream, 2)
-    d_heads, grad_attention, shared_box = attention_back(
-        nz, dhr, n1, qkv, p_low, o, o_weight, ndp * nz, shared_part, 1
+    d_heads, grad_attention, shared_box, small_grad = attention_back(
+        nz, dhr, n1, qkv, p_low, o, o_weight, ndp * nz, shared_part, n2, mixed, 1
     )
     attention_part = over_dp(grad_attention).reshape((nz,) + grad_attention.shape[1:])
     branch = Products(
@@ -1463,13 +1470,7 @@
         None,
     )
     dh_now, _ = lax.optimization_barrier((dh, grad_attention))
-    small_rows = jnp.concatenate(
-        [
-            jnp.zeros((1, width), f32), jnp.sum(grad_two, axis=0)[None], small_grad.T,
-            jnp.zeros((13 - expert_count, width), f32),
-        ],
-        axis=0,
-    )
+    small_rows = small_grad + jnp.pad(jnp.sum(grad_two, axis=0)[None], ((1, 14), (0, 0)))
     count = ndp * nz
     small_blocks = jnp.swapaxes(small_rows.reshape(16, count, width // count), 0, 1)
     input_grad, layer_out, small_all, s_gate, s_up, s_down = reduce_last(

time: 536 us -> 536 us (level)
    unnamed x46 -> x47, local copies, waits for them, and re-layouts: 12.3 us -> 13.8 us
where the time goes in v3:
time: 536 us; the launch traced here: 531 us
  Pallas kernels  479 us (89%)
  local copies, waits for them, and re-layouts  21.2 us (4%)
  other arithmetic  16.3 us (3%)
  between operations  14.5 us (3%)
    pallas_call x1, Pallas kernels, forward_layer(): pl.pallas_call(kernel, out_shape=[jax.ShapeDtypeStruct((seq, width), bf16...  144 us
    pallas_call x1, Pallas kernels, reduce_and_gather(): pl.pallas_call(kernel, out_shape=[jax.ShapeDtypeStruct((nz * 2 * rows, wi...  98.1 us
    pallas_call x1, Pallas kernels, reduce_last(): pl.pallas_call(kernel, out_shape=[jax.ShapeDtypeStruct((2 * rows, width),...  87.5 us
    pallas_call x1, Pallas kernels, hidden_layer(): pl.pallas_call(kernel, out_shape=[jax.ShapeDtypeStruct((groups, experts *...  61.9 us
    pallas_call x1, Pallas kernels, attention_back(): pl.pallas_call(kernel, out_shape=[jax.ShapeDtypeStruct((seq, 3 * cols), b...  57.7 us
    pallas_call x1, Pallas kernels, spread_turned(): pl.pallas_call(kernel, out_shape=[jax.ShapeDtypeStruct((block, nz * cols)...  29.5 us
    unnamed x47, local copies, waits for them, and re-layouts  13.8 us
  transfers between devices with their start and end apart: 3, of which 0 were waited for; matrix products, arithmetic and copies ran while one was open for 3% of the time, Pallas kernels for 57%

profile of v3, /device:TPU:8, one launch (start us, length us, event | category | flops | bytes accessed | tf_op | source)
XLA Modules:
  0.0 531.1 jit_solution(11217942423515745306)
XLA Ops:
  7.3 1.3 broadcast_in_dim.40
  8.6 1.3 broadcast_in_dim.41
  9.9 0.7 broadcast_in_dim.36
  10.6 1.4 pad_maximum_fusion.small_ref
  12.0 1.4 add_add_fusion.marks_ref
  13.3 2.3 constant_dynamic-slice_fusion
  15.6 144.2 %shard_map.305 = (bf16[1024,2048]{1,0:T(8,128)(2,1)}, bf16[1024,2048]{1,0:T(8,128)(2,1)}, s32[4,8,256]{2,1,0:T(8,128)}, bf16[1024,768]{1,0:T(8,128)(2,1)}, bf16[...) custom-call(bf16[128,2048]{1,0:T(8,128)(2,1)} %get-tuple-element.118, ...), custom_call_target="tpu_custom_call" | custom-call | tf_op jit(solution)/shard_map/pallas_call | solution.py:828
  160.0 0.7 copy-done.17
  160.6 0.3 copy.63
  160.9 0.2 slice_reduce_fusion
  161.1 0.4 fusion.1
  161.5 1.1 broadcast_select_fusion.1
  162.6 61.9 %shard_map.306 = (bf16[4,4224,512]{2,1,0:T(8,128)(2,1)}, bf16[2,1024,768]{2,1,0:T(8,128)(2,1)}, bf16[2,1024,768]{2,1,0:T(8,128)(2,1)}, bf16[2,1024,768]{2,1,0:T(8,128)(2,1)}, f32[1024,8]{1,0:T(8,128)}) custom-call(bf16[1024,2048]{1,0:T(8,128)(2,1)} %get-tuple-element.60.n2_hbm, bf16[1024,2048]{1,0:T(8,128)(2,1)} %get-tuple-element.61.dy_hbm, ...), custom_call_target="tpu_custom_call" | custom-call | tf_op jit(solution)/shard_map/pallas_call | solution.py:488
  224.7 0.6 copy-done.16
  225.3 0.4 copy-done.6
  225.6 0.2 slice.38
  225.8 0.2 copy.72
  226.0 0.2 copy.66
  226.2 0.2 broadcast_subtract_fusion
  226.4 0.2 copy.71
  226.6 0.2 copy.70
  226.8 0.2 multiply_reduce_fusion.1
  227.3 0.2 copy.73
  227.7 0.3 copy.74
  228.0 0.2 copy.76
  228.2 0.9 pad.21.refs_13_
  229.2 1.0 pad_add_fusion
  230.2 98.1 %shard_map.307 = (bf16[1024,2048]{1,0:T(8,128)(2,1)}, f32[128,2048]{1,0:T(8,128)}, f32[16,2048]{1,0:T(8,128)}) custom-call(bf16[2,1024,768]{2,1,0:T(8,128)(2,1)} %get-tuple-element.66.refs_0_.refs_1_, bf16[2,1024,768]{2,1,0:T(8,128)(2,1)} %get-tuple-element.66.refs_0_.refs_1_, bf16[2,1024,768]{2,1,0:T(8,128)(2,1)} %get-tuple-element.67.refs_2_.refs_3_, ...), custom_call_target="tpu_custom_call" | custom-call | tf_op jit(solution)/shard_map/pallas_call | solution.py:1189
  328.3 57.7 %shard_map.308 = (bf16[1024,768]{1,0:T(8,128)(2,1)}, bf16[16,1024,128]{2,1,0:T(8,128)(2,1)}, bf16[4,2112,128]{2,1,0:T(8,128)(2,1)}, f32[16,2048]{1,0:T(8,128)}) custom-call(bf16[1024,2048]{1,0:T(8,128)(2,1)} %get-tuple-element.73.dh_hbm, bf16[1024,2048]{1,0:T(8,128)(2,1)} %get-tuple-element.74.n1_hbm, bf16[1024,768]{1,0:T(8,128)(2,1)} %get-tuple-element.75.qkv_ref, ...), custom_call_target="tpu_custom_call" | custom-call | tf_op jit(solution)/shard_map/pallas_call | solution.py:995
  386.0 0.8 copy-done.13
  387.0 0.3 copy-done.1
  387.3 0.3 multiply_reduce_fusion
  387.6 0.6 pad_maximum_fusion.3
  388.2 0.7 bitcast_bitcast_fusion.refs_14_
  388.9 87.5 %shard_map.309 = (f32[256,2048]{1,0:T(8,128)}, f32[256,2048]{1,0:T(8,128)}, f32[16,128]{1,0:T(8,128)}, f32[128,2816]{1,0:T(8,128)}, f32[128,2816]{1,0:T(8,128)}, /*index=5*/f32[128,2816]{1,0:T(8,128)}) custom-call(bf16[2,1024,768]{2,1,0:T(8,128)(2,1)} %get-tuple-element.64.refs_0_.refs_1_, bf16[2,1024,768]{2,1,0:T(8,128)(2,1)} %get-tuple-element.64.refs_0_.refs_1_, ...), custom_call_target="tpu_custom_call" | custom-call | tf_op jit(solution)/shard_map/pallas_call | solution.py:1343
  476.4 6.1 %convert_bitcast_fusion = (f32[2,512,704]{1,2,0:T(8,128)}, f32[2,512,704]{1,2,0:T(8,128)}, f32[2,512,704]{1,2,0:T(8,128)}) fusion(bf16[2,3,704,512]{3,2,1,0:T(8,128)(2,1)} %bitcast.66), kind=kLoop, calls=%fused_computation | loop fusion | flops 2162688 | bytes 12976128 | tf_op jit(solution)/shard_map/transpose | solution.py:1481
  482.5 0.5 slice_bitcast_fusion.4
  483.1 0.6 slice_bitcast_fusion.3
  483.7 29.5 %shard_map.310 = (f32[128,1024]{1,0:T(8,128)}, f32[128,1024]{1,0:T(8,128)}, f32[128,1024]{1,0:T(8,128)}, f32[128,1024]{1,0:T(8,128)}) custom-call(bf16[4,1024,128]{2,1,0:T(8,128)(2,1)} %bitcast.69), custom_call_target="tpu_custom_call" | custom-call | tf_op jit(solution)/shard_map/pallas_call | solution.py:1048
  513.2 3.1 copy.90
  516.3 1.3 copy.91
  517.6 0.8 copy.92
  518.4 0.8 copy.93
  519.2 0.8 copy.94
  520.0 0.8 copy.95
  520.8 1.1 copy.96
  521.9 1.1 copy.97
  523.0 1.1 copy.98
  (58 shorter events, 1.0 us)
Async XLA Ops:
  7.2 321.1 %reduce-scatter.4.cloned.1.call-start = ((), (), s32[]{:S(2)}) async-start(), calls=%async_computation.3 | async-start | bytes 10813440 | tf_op jit(solution)/shard_map/reduce_scatter | solution.py:1457
  159.9 0.8 copy-start.17
  159.9 1.1 copy-start
  159.9 316.5 %reduce-scatter.8.cloned.1.call-start = ((), (), s32[]{:S(2)}) async-start(), calls=%async_computation.5 | async-start | bytes 21626880 | tf_op jit(solution)/shard_map/reduce_scatter | solution.py:1457
  224.6 0.7 copy-start.16
  224.6 1.0 copy-start.6
  224.6 2.2 copy-start.7
  224.6 257.9 %reduce-scatter.6.cloned.1.call-start = ((), (), s32[]{:S(2)}) async-start(), calls=%async_computation.4 | async-start | bytes 5242880 | tf_op jit(solution)/shard_map/reduce_scatter | solution.py:1457
  226.2 1.4 copy-start.15
  386.0 0.9 copy-start.13
  386.0 1.0 copy-start.12
  386.0 1.4 copy-start.1
  386.0 2.2 copy-start.14
  476.4 6.1 %copy-start.18 = (f32[16,128]{1,0:T(8,128)S(1)}, f32[16,128]{1,0:T(8,128)}, u32[]{:S(2)}) copy-start(f32[16,128]{1,0:T(8,128)} %get-tuple-element.91) | copy-start | bytes 24580
  482.5 33.8 %copy-start.2 = (f32[256,2048]{1,0:T(8,128)S(1)}, f32[256,2048]{1,0:T(8,128)}, u32[]{:S(2)}) copy-start(f32[256,2048]{1,0:T(8,128)} %get-tuple-element.137) | copy-start | bytes 6291460
  516.3 1.3 copy-start.11
  516.3 2.1 copy-start.10
  516.3 2.9 copy-start.9
  516.3 3.7 copy-start.8
  517.6 3.2 copy-start.5
  518.4 3.5 copy-start.4
  520.8 2.2 copy-start.3
Sparse Core Ops, SparseCore 0:
  160.0 96.2 reduce-scatter.3
  259.4 158.0 reduce-scatter.7
  420.8 54.2 reduce-scatter.5

commit v4 on v3

--- a/solution.py
+++ b/solution.py
@@ -507,8 +507,8 @@
     )(n2, dy, *weights, gate)
 
 
-def forward_layer(nz, x, gain, upstream, marks, weights, out_weight, gain2, small, shared, groups, name):
-    rows, width = x.shape
+def forward_layer(nz, x, upstream, marks, weights, out_weight, small, shared, groups, name):
+    rows, width = x.shape[0] // 2, x.shape[1]
     seq = nz * 2 * rows
     cols = weights[0].shape[1] // nz
     heads = cols // HD
@@ -521,12 +521,12 @@
     lane = min(block, TILE)
     per = TILE // lane
     slabs = width // TILE
-    gate_row = small.shape[0] - 1
-
-    def kernel(x_ref, gain_ref, up_ref, marks_ref, gain2_ref, small_ref, wq_hbm, wk_hbm, wv_hbm, wo_hbm, wg_hbm, wu_hbm, wd_hbm,
+    gate_row = small.shape[0] - 3
+
+    def kernel(x_ref, up_ref, marks_ref, small_ref, wq_hbm, wk_hbm, wv_hbm, wo_hbm, wg_hbm, wu_hbm, wd_hbm,
                n1_hbm, dy_hbm, all_ref, qkv_hbm, p_hbm, o_hbm, n2_hbm, h_ref, inv_ref, logit_ref, grad_hbm, da_hbm, db_hbm,
                gu_hbm, dgate_ref,
-               n1_ref, dy_ref, qkv_ref, p_ref, o_ref, n2_ref, own, w, scores, seg_q, seg_k, heads_in, acc, give, take_in, own2,
+               n1_ref, dy_ref, qkv_ref, p_ref, o_ref, n2_ref, own, w, scores, seg_k, heads_in, acc, give, take_in,
                inv_own, wo, wg, wu, wd, da, db, gu, turned, slab,
                w_sem, m_send, m_recv, m_local, a_send, a_recv, e_send, e_recv, i_sems, out_sem, slab_sem, *sems):
         z, c = here()
@@ -550,14 +550,14 @@
             load.start()
 
         def step(strip_at):
-            normed, _ = norm_rows(x_ref[strip_at, :].astype(f32), gain_ref[...])
+            normed, _ = norm_rows(x_ref[pl.ds(pl.multiple_of(c * rows + strip_at.start, STRIP), STRIP), :].astype(f32), small_ref[gate_row + 1 : gate_row + 2, :].astype(f32))
             own[strip_at, :] = normed.astype(bf16)
 
         strips(rows, step)
         greet(nz)
         n1 = Gather(nz, own, n1_ref, *sems[:5])
-        dy = Gather(nz, up_ref, dy_ref, *sems[5:10])
-        n2 = Gather(nz, own2, n2_ref, *sems[10:])
+        dy = Gather(nz, up_ref.at[pl.ds(pl.multiple_of(c * rows, rows), rows)], dy_ref, *sems[5:10])
+        n2 = Gather(nz, own, n2_ref, *sems[10:])
         n1.start_along(UP)
         n1.start_along(DOWN)
         n1.start_across()
@@ -608,7 +608,7 @@
         def label():
             for b in range(nz):
                 some = all_ref[b].astype(f32)
-                seg_q[b * full : (b + 1) * full, :] = some.T[:, :1]
+                dgate_ref[b * full : (b + 1) * full, :1] = some.T[:, :1]
                 seg_k[:, b * full : (b + 1) * full] = some[:1, :]
 
         def head(i):
@@ -629,7 +629,7 @@
                     row = pl.ds(pl.multiple_of(base + j * strip, strip), strip)
                     place_q = base + j * strip + lax.broadcasted_iota(jnp.int32, (strip, length), 0)
                     place_k = lax.broadcasted_iota(jnp.int32, (strip, length), 1)
-                    allowed = jnp.logical_and(place_k <= place_q, seg_k[:, :length] == seg_q[row, :])
+                    allowed = jnp.logical_and(place_k <= place_q, seg_k[:, :length] == dgate_ref[row, :1])
                     value = jnp.where(allowed, scores[local, :length] * scale, -jnp.inf)
                     value = jnp.exp(value - jnp.max(value, axis=-1, keepdims=True))
                     share = 1.0 / jnp.sum(value, axis=-1, keepdims=True)
@@ -713,10 +713,10 @@
 
         def norm_two(at):
             mixed = acc[pl.ds(pl.multiple_of(c * rows + at.start, STRIP), STRIP), :] + take_in[at, :].astype(f32)
-            h = x_ref[at, :].astype(f32) + mixed
-            normed, inverse = norm_rows(h, gain2_ref[...])
+            h = x_ref[pl.ds(pl.multiple_of(c * rows + at.start, STRIP), STRIP), :].astype(f32) + mixed
+            normed, inverse = norm_rows(h, small_ref[gate_row + 2 : gate_row + 3, :].astype(f32))
             h_ref[at, :] = h
-            own2[at, :] = normed.astype(bf16)
+            own[at, :] = normed.astype(bf16)
             inv_own[at, :] = jnp.broadcast_to(inverse, (STRIP, 128))
 
         strips(rows, norm_two)
@@ -842,16 +842,16 @@
             hidden_shape, hidden_shape, hidden_shape,
             jax.ShapeDtypeStruct((seq, small.shape[0]), f32),
         ],
-        in_specs=[VMEM] * 6 + [ANY] * 7,
+        in_specs=[VMEM] * 4 + [ANY] * 7,
         out_specs=[ANY, ANY, VMEM, ANY, ANY, ANY, ANY, VMEM, ANY, VMEM, ANY, ANY, ANY, ANY, VMEM],
         scratch_shapes=[
             pltpu.VMEM((seq, width), bf16), pltpu.VMEM((seq, width), bf16), pltpu.VMEM((seq, 3 * cols), bf16),
             pltpu.VMEM((heads, seq, seq), bf16), pltpu.VMEM((seq, cols), bf16), pltpu.VMEM((seq, width), bf16),
             pltpu.VMEM((rows, width), bf16), pltpu.VMEM((width, 3 * cols), bf16), pltpu.VMEM((full, seq), f32),
-            pltpu.VMEM((seq, 1), f32), pltpu.VMEM((1, seq), f32),
+            pltpu.VMEM((1, seq), f32),
             pltpu.VMEM((2, nz, full, cols), bf16),
             pltpu.VMEM((full, width), f32),
-            pltpu.VMEM((rows, width), bf16), pltpu.VMEM((rows, width), bf16), pltpu.VMEM((rows, width), bf16),
+            pltpu.VMEM((rows, width), bf16), pltpu.VMEM((rows, width), bf16),
             pltpu.VMEM((rows, 128), f32), pltpu.VMEM(out_weight.shape, bf16),
             pltpu.VMEM((width, held), bf16), pltpu.VMEM((width, held), bf16), pltpu.VMEM((width, held), bf16),
             pltpu.VMEM((seq, held), bf16), pltpu.VMEM((seq, held), bf16), pltpu.VMEM((seq, held), bf16),
@@ -866,7 +866,7 @@
         compiler_params=pltpu.CompilerParams(
             collective_id=name, has_side_effects=True, vmem_limit_bytes=63 * 1024 * 1024
         ),
-    )(x, gain, upstream, marks, gain2, small, *weights, out_weight, *shared)
+    )(x, upstream, marks, small, *weights, out_weight, *shared)
 
 
 def attention_back(nz, d_h, n1, qkv, probs, o, out_weight, groups, part, n2, small, name):
@@ -1146,7 +1146,7 @@
         lax.fori_loop(start, end, one, 0)
 
 
-def reduce_and_gather(nz, products, h, gain, upstream, name):
+def reduce_and_gather(nz, products, h, gains, upstream, name):
     rows, width = h.shape
     n_in, n_scratch = len(products.inputs), len(products.scratch)
 
@@ -1160,6 +1160,7 @@
         reducer = Reducer(nz, part, *scratch)
         products.fetch(reducer.block)
         greet(nz)
+        z, c = here()
         ends = reducer.ends()
 
         def one(s, carry):
@@ -1176,8 +1177,8 @@
         gg_ref[...] = jnp.zeros_like(gg_ref)
 
         def step(at):
-            change, along = norm_back(h_ref[at, :], gain_ref[...], total[at, :])
-            dh = up_ref[at, :].astype(f32) + change
+            change, along = norm_back(h_ref[at, :], gain_ref[gains.shape[0] - 1 :, :].astype(f32), total[at, :])
+            dh = up_ref[pl.ds(pl.multiple_of(c * rows + at.start, STRIP), STRIP), :].astype(f32) + change
             dh_ref[at, :] = dh
             own[at, :] = dh.astype(bf16)
             gg_ref[...] += along
@@ -1200,11 +1201,11 @@
         + reduce_scratch(nz, rows, width)
         + gather_sems(nz),
         compiler_params=params(name),
-    )(*products.inputs, h, gain, upstream)
-
-
-def reduce_last(nz, d_heads, weights, x, gain, dh, products, h, small, box, name):
-    rows, width = x.shape
+    )(*products.inputs, h, gains, upstream)
+
+
+def reduce_last(nz, d_heads, weights, x, gains, dh, products, h, small, box, name):
+    rows, width = dh.shape
     cols = d_heads.shape[1] // 3
     n, small_rows, lanes = small.shape
     box_rows, block = box.shape[1] // 3, box.shape[2]
@@ -1295,7 +1296,7 @@
         gg_ref[...] = jnp.zeros_like(gg_ref)
 
         def step(at):
-            change, along = norm_back(x_ref[at, :].astype(f32), gain_ref[...], d_total[at, :])
+            change, along = norm_back(x_ref[pl.ds(pl.multiple_of(c * rows + at.start, STRIP), STRIP), :].astype(f32), gain_ref[gains.shape[0] - 2 : gains.shape[0] - 1, :].astype(f32), d_total[at, :])
             own[0, at, :] = dh_ref[at, :] + change
             gg_ref[...] += along
 
@@ -1363,7 +1364,7 @@
         ]
         + reduce_scratch(nz, rows, width) * 2,
         compiler_params=params(name, 60),
-    )(*products.inputs, d_heads, *weights, x, gain, dh, h, small, box)
+    )(*products.inputs, d_heads, *weights, x, gains, dh, h, small, box)
 
 
 def cross_rows(left, right):
@@ -1401,27 +1402,22 @@
     heads = head_cols // HD
     seq = rows * nz
     scale = HD ** (-0.5)
-    gain1 = norm1_gain.astype(f32)[None]
-    gain2 = norm2_gain.astype(f32)[None]
-
-    def own(values):
-        return lax.dynamic_slice_in_dim(values, c * own_rows, own_rows, 0)
 
     def head_slice(values):
         return lax.dynamic_slice_in_dim(values, z * head_cols, head_cols, 1)
 
     x_all_rows = tokens.astype(f32)
     inverse_one_rows = lax.rsqrt(jnp.mean(x_all_rows * x_all_rows, axis=-1) + epsilon)
-    x = own(tokens)
     marks = jnp.concatenate([segments, routes.T, jnp.zeros((7 - routes.shape[1], rows), jnp.int32)], axis=0)
-    upstream = own(out_grad)
     ndp = lax.axis_size("dp")
-    small_rows_weight = jnp.concatenate([router_weight.T, shared_gate_vector[None]], axis=0)
+    small_rows_weight = jnp.concatenate(
+        [router_weight.T, shared_gate_vector[None], norm1_gain[None], norm2_gain[None]], axis=0
+    )
     shared_weights = (shared_gate_weight, shared_up_weight, shared_down_weight)
     (
         n1, dy, all_marks, qkv, p_low, o, n2, h, inverse_two, logits, grad_s, da_s, db_s, gu_s, dgate_s,
     ) = forward_layer(
-        nz, x, gain1, upstream, marks, (q_weight, k_weight, v_weight), o_weight, gain2, small_rows_weight, shared_weights,
+        nz, tokens, out_grad, marks, (q_weight, k_weight, v_weight), o_weight, small_rows_weight, shared_weights,
         ndp * nz, 0,
     )
     all_routes = jnp.transpose(all_marks[:, 1 : 1 + routes.shape[1]], (0, 2, 1)).reshape(seq, routes.shape[1])
@@ -1429,14 +1425,14 @@
     probs = jax.nn.softmax(logits[:, :expert_count], axis=-1)
     chosen = jnp.any(all_routes[:, :, None] == jnp.arange(expert_count)[None, None, :], axis=1)
     gates = jnp.where(chosen, probs, 0.0)
-    sigma = jax.nn.sigmoid(logits[:, expert_count:])
+    sigma = jax.nn.sigmoid(logits[:, expert_count : expert_count + 1])
 
     turned = [jnp.swapaxes(w, 1, 2) for w in (expert_gate_weight, expert_up_weight, expert_down_weight)]
     grad_e, da_e, db_e, gu_e, dgate_e = hidden_layer(nz, n2, dy, gates, turned, ndp)
 
     d_probs = jnp.where(chosen, dgate_e, 0.0)
     d_logits = probs * (d_probs - jnp.sum(probs * d_probs, axis=-1, keepdims=True))
-    d_vector = dgate_s[:, expert_count:] * (sigma * (1.0 - sigma))
+    d_vector = dgate_s[:, expert_count : expert_count + 1] * (sigma * (1.0 - sigma))
     small = jnp.concatenate([d_logits, d_vector], axis=1)
     small_high, small_low = two_parts(small)
     small_weights = jnp.concatenate([router_weight, shared_gate_vector[:, None]], axis=1)
@@ -1458,7 +1454,7 @@
 
     shared_part = over_dp(grad_s).reshape((nz,) + grad_s.shape[1:])
     expert_part = over_dp(grad_e).reshape(local_count, 3, ffn, -1)
-    dhr, dh, grad_two = reduce_and_gather(nz, d_n2, h, gain2, upstream, 2)
+    dhr, dh, grad_two = reduce_and_gather(nz, d_n2, h, small_rows_weight, out_grad, 2)
     d_heads, grad_attention, shared_box, small_grad = attention_back(
         nz, dhr, n1, qkv, p_low, o, o_weight, ndp * nz, shared_part, n2, mixed, 1
     )
@@ -1474,7 +1470,7 @@
     count = ndp * nz
     small_blocks = jnp.swapaxes(small_rows.reshape(16, count, width // count), 0, 1)
     input_grad, layer_out, small_all, s_gate, s_up, s_down = reduce_last(
-        nz, d_heads, (q_weight, k_weight, v_weight), x, gain1, dh_now, branch, h, small_blocks, shared_box, 3
+        nz, d_heads, (q_weight, k_weight, v_weight), tokens, small_rows_weight, dh_now, branch, h, small_blocks, shared_box, 3
     )
     stats = jnp.stack([inverse_one_rows, inverse_two[:, 0]])
 

time: 536 us -> 533 us (level)
  transfers between devices with their start and end apart: 3 -> 3, of which waited for: 0 -> 0; matrix products, arithmetic and copies ran while one was open for 3% -> 3% of each run, Pallas kernels for 57% -> 58%
where the time goes in v4:
time: 533 us; the launch traced here: 528 us
  Pallas kernels  480 us (90%)
  local copies, waits for them, and re-layouts  20.3 us (4%)
  between operations  14.5 us (3%)
  other arithmetic  13.8 us (3%)
    pallas_call x1, Pallas kernels, forward_layer(): pl.pallas_call(kernel, out_shape=[jax.ShapeDtypeStruct((seq, width), bf16...  145 us
    pallas_call x1, Pallas kernels, reduce_and_gather(): pl.pallas_call(kernel, out_shape=[jax.ShapeDtypeStruct((nz * 2 * rows, wi...  98.3 us
    pallas_call x1, Pallas kernels, reduce_last(): pl.pallas_call(kernel, out_shape=[jax.ShapeDtypeStruct((2 * rows, width),...  87.8 us
    pallas_call x1, Pallas kernels, hidden_layer(): pl.pallas_call(kernel, out_shape=[jax.ShapeDtypeStruct((groups, experts *...  61.9 us
    pallas_call x1, Pallas kernels, attention_back(): pl.pallas_call(kernel, out_shape=[jax.ShapeDtypeStruct((seq, 3 * cols), b...  57.6 us
    pallas_call x1, Pallas kernels, spread_turned(): pl.pallas_call(kernel, out_shape=[jax.ShapeDtypeStruct((block, nz * cols)...  29.5 us
    unnamed x47, local copies, waits for them, and re-layouts  13.8 us
  transfers between devices with their start and end apart: 3, of which 0 were waited for; matrix products, arithmetic and copies ran while one was open for 3% of the time, Pallas kernels for 58%

profile of v4, /device:TPU:8, one launch (start us, length us, event | category | flops | bytes accessed | tf_op | source)
XLA Modules:
  0.0 528.4 jit_solution(13124152871655436848)
XLA Ops:
  7.3 0.7 broadcast_in_dim.29
  8.0 0.7 broadcast_in_dim.30
  8.7 0.7 broadcast_in_dim.28
  9.4 1.4 add_add_fusion.marks_ref
  10.8 1.4 pad_maximum_fusion.small_ref.refs_15_.refs_11_
  12.2 144.5 %shard_map.305 = (bf16[1024,2048]{1,0:T(8,128)(2,1)}, bf16[1024,2048]{1,0:T(8,128)(2,1)}, s32[4,8,256]{2,1,0:T(8,128)}, bf16[1024,768]{1,0:T(8,128)(2,1)}, bf16[...) custom-call(bf16[256,2048]{1,0:T(8,128)(2,1)} %refs_10_.3, ...), custom_call_target="tpu_custom_call" | custom-call | tf_op jit(solution)/shard_map/pallas_call | solution.py:828
  156.8 0.7 copy-done.17
  157.5 0.3 copy.63
  157.8 0.2 slice_reduce_fusion
  158.0 0.4 fusion.1
  158.4 1.1 broadcast_select_fusion.1
  159.5 61.9 %shard_map.306 = (bf16[4,4224,512]{2,1,0:T(8,128)(2,1)}, bf16[2,1024,768]{2,1,0:T(8,128)(2,1)}, bf16[2,1024,768]{2,1,0:T(8,128)(2,1)}, bf16[2,1024,768]{2,1,0:T(8,128)(2,1)}, f32[1024,8]{1,0:T(8,128)}) custom-call(bf16[1024,2048]{1,0:T(8,128)(2,1)} %get-tuple-element.60.n2_hbm, bf16[1024,2048]{1,0:T(8,128)(2,1)} %get-tuple-element.61.dy_hbm, ...), custom_call_target="tpu_custom_call" | custom-call | tf_op jit(solution)/shard_map/pallas_call | solution.py:488
  221.6 0.6 copy-done.16
  222.2 0.4 copy-done.6
  222.5 0.2 slice.38
  222.7 0.2 copy.72
  222.9 0.2 copy.66
  223.1 0.2 broadcast_subtract_fusion
  223.3 0.2 copy.71
  223.5 0.2 copy.70
  223.7 0.2 multiply_reduce_fusion.1
  224.1 0.2 copy.73
  224.3 0.2 copy.77
  224.5 0.3 copy.74
  224.8 0.2 copy.76
  225.1 0.9 pad.21.refs_13_
  226.0 1.0 pad_add_fusion
  227.0 98.3 %shard_map.307 = (bf16[1024,2048]{1,0:T(8,128)(2,1)}, f32[128,2048]{1,0:T(8,128)}, f32[16,2048]{1,0:T(8,128)}) custom-call(bf16[2,1024,768]{2,1,0:T(8,128)(2,1)} %get-tuple-element.66.refs_0_.refs_1_, bf16[2,1024,768]{2,1,0:T(8,128)(2,1)} %get-tuple-element.66.refs_0_.refs_1_, bf16[2,1024,768]{2,1,0:T(8,128)(2,1)} %get-tuple-element.67.refs_2_.refs_3_, ...), custom_call_target="tpu_custom_call" | custom-call | tf_op jit(solution)/shard_map/pallas_call | solution.py:1190
  325.4 57.6 %shard_map.308 = (bf16[1024,768]{1,0:T(8,128)(2,1)}, bf16[16,1024,128]{2,1,0:T(8,128)(2,1)}, bf16[4,2112,128]{2,1,0:T(8,128)(2,1)}, f32[16,2048]{1,0:T(8,128)}) custom-call(bf16[1024,2048]{1,0:T(8,128)(2,1)} %get-tuple-element.73.dh_hbm, bf16[1024,2048]{1,0:T(8,128)(2,1)} %get-tuple-element.74.n1_hbm, bf16[1024,768]{1,0:T(8,128)(2,1)} %get-tuple-element.75.qkv_ref, ...), custom_call_target="tpu_custom_call" | custom-call | tf_op jit(solution)/shard_map/pallas_call | solution.py:995
  383.1 0.8 copy-done.13
  384.1 0.3 copy-done
  384.4 0.3 multiply_reduce_fusion
  384.7 0.6 pad_maximum_fusion.3
  385.3 0.7 bitcast_bitcast_fusion.refs_14_
  386.0 87.8 %shard_map.309 = (f32[256,2048]{1,0:T(8,128)}, f32[256,2048]{1,0:T(8,128)}, f32[16,128]{1,0:T(8,128)}, f32[128,2816]{1,0:T(8,128)}, f32[128,2816]{1,0:T(8,128)}, /*index=5*/f32[128,2816]{1,0:T(8,128)}) custom-call(bf16[2,1024,768]{2,1,0:T(8,128)(2,1)} %get-tuple-element.64.refs_0_.refs_1_, bf16[2,1024,768]{2,1,0:T(8,128)(2,1)} %get-tuple-element.64.refs_0_.refs_1_, ...), custom_call_target="tpu_custom_call" | custom-call | tf_op jit(solution)/shard_map/pallas_call | solution.py:1344
  473.8 6.1 %convert_bitcast_fusion = (f32[2,512,704]{1,2,0:T(8,128)}, f32[2,512,704]{1,2,0:T(8,128)}, f32[2,512,704]{1,2,0:T(8,128)}) fusion(bf16[2,3,704,512]{3,2,1,0:T(8,128)(2,1)} %bitcast.64), kind=kLoop, calls=%fused_computation | loop fusion | flops 2162688 | bytes 12976128 | tf_op jit(solution)/shard_map/transpose | solution.py:1477
  479.9 0.5 slice_bitcast_fusion.4
  480.4 0.6 slice_bitcast_fusion.3
  481.0 29.5 %shard_map.310 = (f32[128,1024]{1,0:T(8,128)}, f32[128,1024]{1,0:T(8,128)}, f32[128,1024]{1,0:T(8,128)}, f32[128,1024]{1,0:T(8,128)}) custom-call(bf16[4,1024,128]{2,1,0:T(8,128)(2,1)} %bitcast.67), custom_call_target="tpu_custom_call" | custom-call | tf_op jit(solution)/shard_map/pallas_call | solution.py:1048
  510.5 3.1 copy.90
  513.7 1.3 copy.91
  515.0 0.8 copy.92
  515.8 0.8 copy.93
  516.6 0.8 copy.94
  517.4 0.8 copy.95
  518.2 1.1 copy.96
  519.3 1.1 copy.97
  520.4 1.1 copy.98
  (57 shorter events, 0.8 us)
Async XLA Ops:
  7.2 318.2 %reduce-scatter.4.cloned.1.call-start = ((), (), s32[]{:S(2)}) async-start(), calls=%async_computation.3 | async-start | bytes 10813440 | tf_op jit(solution)/shard_map/reduce_scatter | solution.py:1453
  156.7 0.8 copy-start.17
  156.7 1.1 copy-start.1
  156.8 317.0 %reduce-scatter.8.cloned.1.call-start = ((), (), s32[]{:S(2)}) async-start(), calls=%async_computation.5 | async-start | bytes 21626880 | tf_op jit(solution)/shard_map/reduce_scatter | solution.py:1453
  221.5 0.7 copy-start.16
  221.5 1.0 copy-start.6
  221.5 2.2 copy-start.7
  221.5 258.4 %reduce-scatter.6.cloned.1.call-start = ((), (), s32[]{:S(2)}) async-start(), calls=%async_computation.4 | async-start | bytes 5242880 | tf_op jit(solution)/shard_map/reduce_scatter | solution.py:1453
  223.1 1.4 copy-start.15
  383.0 0.9 copy-start.13
  383.0 1.0 copy-start.12
  383.0 1.4 copy-start
  383.0 2.2 copy-start.14
  473.8 6.1 %copy-start.18 = (f32[16,128]{1,0:T(8,128)S(1)}, f32[16,128]{1,0:T(8,128)}, u32[]{:S(2)}) copy-start(f32[16,128]{1,0:T(8,128)} %get-tuple-element.91) | copy-start | bytes 24580
  479.9 33.7 %copy-start.2 = (f32[256,2048]{1,0:T(8,128)S(1)}, f32[256,2048]{1,0:T(8,128)}, u32[]{:S(2)}) copy-start(f32[256,2048]{1,0:T(8,128)} %get-tuple-element.135) | copy-start | bytes 6291460
  513.6 1.3 copy-start.11
  513.6 2.1 copy-start.10
  513.6 2.9 copy-start.9
  513.6 3.7 copy-start.8
  515.0 3.2 copy-start.5
  515.8 3.5 copy-start.4
  518.2 2.2 copy-start.3
Sparse Core Ops, SparseCore 0:
  156.9 96.2 reduce-scatter.3
  256.3 158.0 reduce-scatter.7
  417.7 54.2 reduce-scatter.5

commit v5 on v4

--- a/solution.py
+++ b/solution.py
@@ -905,7 +905,7 @@
             dst = box_hbm.at[z - d if way == UP else z + d]
             remote(dst, dst, b_send.at[way, d], b_recv.at[way, d], {"tensor": 1 - c}).wait_recv()
 
-        for d in range(nz - 1, 0, -1):
+        for d in range(1, nz):
             for way in (UP, DOWN):
                 pl.when(z + d < nz if way == UP else z >= d)(lambda way=way, d=d: send(way, d).start())
         o_turned[...] = o_ref[...].T

time: 533 us -> 534 us (level)
  no operation moved by 1% of the time
where the time goes in v5:
time: 534 us; the launch traced here: 529 us
  Pallas kernels  481 us (90%)
  local copies, waits for them, and re-layouts  20.3 us (4%)
  between operations  14.5 us (3%)
  other arithmetic  13.8 us (3%)
    pallas_call x1, Pallas kernels, forward_layer(): pl.pallas_call(kernel, out_shape=[jax.ShapeDtypeStruct((seq, width), bf16...  145 us
    pallas_call x1, Pallas kernels, reduce_and_gather(): pl.pallas_call(kernel, out_shape=[jax.ShapeDtypeStruct((nz * 2 * rows, wi...  98.3 us
    pallas_call x1, Pallas kernels, reduce_last(): pl.pallas_call(kernel, out_shape=[jax.ShapeDtypeStruct((2 * rows, width),...  90.7 us
    pallas_call x1, Pallas kernels, hidden_layer(): pl.pallas_call(kernel, out_shape=[jax.ShapeDtypeStruct((groups, experts *...  61.9 us
    pallas_call x1, Pallas kernels, attention_back(): pl.pallas_call(kernel, out_shape=[jax.ShapeDtypeStruct((seq, 3 * cols), b...  55.7 us
    pallas_call x1, Pallas kernels, spread_turned(): pl.pallas_call(kernel, out_shape=[jax.ShapeDtypeStruct((block, nz * cols)...  29.4 us
    unnamed x47, local copies, waits for them, and re-layouts  13.8 us
  transfers between devices with their start and end apart: 3, of which 0 were waited for; matrix products, arithmetic and copies ran while one was open for 3% of the time, Pallas kernels for 58%

profile of v5, /device:TPU:8, one launch (start us, length us, event | category | flops | bytes accessed | tf_op | source)
XLA Modules:
  0.0 529.3 jit_solution(4792658426960949929)
XLA Ops:
  7.3 0.7 broadcast_in_dim.29
  8.0 0.7 broadcast_in_dim.30
  8.7 0.7 broadcast_in_dim.28
  9.4 1.4 add_add_fusion.marks_ref
  10.8 1.4 pad_maximum_fusion.small_ref.refs_15_.refs_11_
  12.2 144.5 %shard_map.305 = (bf16[1024,2048]{1,0:T(8,128)(2,1)}, bf16[1024,2048]{1,0:T(8,128)(2,1)}, s32[4,8,256]{2,1,0:T(8,128)}, bf16[1024,768]{1,0:T(8,128)(2,1)}, bf16[...) custom-call(bf16[256,2048]{1,0:T(8,128)(2,1)} %refs_10_.3, ...), custom_call_target="tpu_custom_call" | custom-call | tf_op jit(solution)/shard_map/pallas_call | solution.py:828
  156.8 0.7 copy-done.17
  157.5 0.3 copy.63
  157.8 0.2 slice_reduce_fusion
  158.0 0.4 fusion.1
  158.4 1.1 broadcast_select_fusion.1
  159.5 61.9 %shard_map.306 = (bf16[4,4224,512]{2,1,0:T(8,128)(2,1)}, bf16[2,1024,768]{2,1,0:T(8,128)(2,1)}, bf16[2,1024,768]{2,1,0:T(8,128)(2,1)}, bf16[2,1024,768]{2,1,0:T(8,128)(2,1)}, f32[1024,8]{1,0:T(8,128)}) custom-call(bf16[1024,2048]{1,0:T(8,128)(2,1)} %get-tuple-element.60.n2_hbm, bf16[1024,2048]{1,0:T(8,128)(2,1)} %get-tuple-element.61.dy_hbm, ...), custom_call_target="tpu_custom_call" | custom-call | tf_op jit(solution)/shard_map/pallas_call | solution.py:488
  221.6 0.6 copy-done.16
  222.2 0.4 copy-done.6
  222.5 0.2 slice.38
  222.7 0.2 copy.72
  222.9 0.2 copy.66
  223.1 0.2 broadcast_subtract_fusion
  223.3 0.2 copy.71
  223.5 0.2 copy.70
  223.7 0.2 multiply_reduce_fusion.1
  224.1 0.2 copy.73
  224.3 0.2 copy.77
  224.5 0.3 copy.74
  224.8 0.2 copy.76
  225.1 0.9 pad.21.refs_13_
  226.0 1.0 pad_add_fusion
  227.0 98.3 %shard_map.307 = (bf16[1024,2048]{1,0:T(8,128)(2,1)}, f32[128,2048]{1,0:T(8,128)}, f32[16,2048]{1,0:T(8,128)}) custom-call(bf16[2,1024,768]{2,1,0:T(8,128)(2,1)} %get-tuple-element.66.refs_0_.refs_1_, bf16[2,1024,768]{2,1,0:T(8,128)(2,1)} %get-tuple-element.66.refs_0_.refs_1_, bf16[2,1024,768]{2,1,0:T(8,128)(2,1)} %get-tuple-element.67.refs_2_.refs_3_, ...), custom_call_target="tpu_custom_call" | custom-call | tf_op jit(solution)/shard_map/pallas_call | solution.py:1190
  325.4 55.7 %shard_map.308 = (bf16[1024,768]{1,0:T(8,128)(2,1)}, bf16[16,1024,128]{2,1,0:T(8,128)(2,1)}, bf16[4,2112,128]{2,1,0:T(8,128)(2,1)}, f32[16,2048]{1,0:T(8,128)}) custom-call(bf16[1024,2048]{1,0:T(8,128)(2,1)} %get-tuple-element.73.dh_hbm, bf16[1024,2048]{1,0:T(8,128)(2,1)} %get-tuple-element.74.n1_hbm, bf16[1024,768]{1,0:T(8,128)(2,1)} %get-tuple-element.75.qkv_ref, ...), custom_call_target="tpu_custom_call" | custom-call | tf_op jit(solution)/shard_map/pallas_call | solution.py:995
  381.1 0.8 copy-done.13
  382.1 0.3 copy-done
  382.4 0.3 multiply_reduce_fusion
  382.7 0.6 pad_maximum_fusion.3
  383.3 0.7 bitcast_bitcast_fusion.refs_14_
  384.0 90.7 %shard_map.309 = (f32[256,2048]{1,0:T(8,128)}, f32[256,2048]{1,0:T(8,128)}, f32[16,128]{1,0:T(8,128)}, f32[128,2816]{1,0:T(8,128)}, f32[128,2816]{1,0:T(8,128)}, /*index=5*/f32[128,2816]{1,0:T(8,128)}) custom-call(bf16[2,1024,768]{2,1,0:T(8,128)(2,1)} %get-tuple-element.64.refs_0_.refs_1_, bf16[2,1024,768]{2,1,0:T(8,128)(2,1)} %get-tuple-element.64.refs_0_.refs_1_, ...), custom_call_target="tpu_custom_call" | custom-call | tf_op jit(solution)/shard_map/pallas_call | solution.py:1344
  474.7 6.1 %convert_bitcast_fusion = (f32[2,512,704]{1,2,0:T(8,128)}, f32[2,512,704]{1,2,0:T(8,128)}, f32[2,512,704]{1,2,0:T(8,128)}) fusion(bf16[2,3,704,512]{3,2,1,0:T(8,128)(2,1)} %bitcast.64), kind=kLoop, calls=%fused_computation | loop fusion | flops 2162688 | bytes 12976128 | tf_op jit(solution)/shard_map/transpose | solution.py:1477
  480.8 0.5 slice_bitcast_fusion.4
  481.4 0.6 slice_bitcast_fusion.3
  481.9 29.4 %shard_map.310 = (f32[128,1024]{1,0:T(8,128)}, f32[128,1024]{1,0:T(8,128)}, f32[128,1024]{1,0:T(8,128)}, f32[128,1024]{1,0:T(8,128)}) custom-call(bf16[4,1024,128]{2,1,0:T(8,128)(2,1)} %bitcast.67), custom_call_target="tpu_custom_call" | custom-call | tf_op jit(solution)/shard_map/pallas_call | solution.py:1048
  511.4 3.1 copy.90
  514.6 1.3 copy.91
  515.9 0.8 copy.92
  516.7 0.8 copy.93
  517.5 0.8 copy.94
  518.3 0.8 copy.95
  519.1 1.1 copy.96
  520.2 1.1 copy.97
  521.3 1.1 copy.98
  (57 shorter events, 0.8 us)
Async XLA Ops:
  7.2 318.2 %reduce-scatter.4.cloned.1.call-start = ((), (), s32[]{:S(2)}) async-start(), calls=%async_computation.3 | async-start | bytes 10813440 | tf_op jit(solution)/shard_map/reduce_scatter | solution.py:1453
  156.7 0.8 copy-start.17
  156.7 1.1 copy-start.1
  156.8 317.9 %reduce-scatter.8.cloned.1.call-start = ((), (), s32[]{:S(2)}) async-start(), calls=%async_computation.5 | async-start | bytes 21626880 | tf_op jit(solution)/shard_map/reduce_scatter | solution.py:1453
  221.5 0.7 copy-start.16
  221.5 1.0 copy-start.6
  221.5 2.2 copy-start.7
  221.5 259.3 %reduce-scatter.6.cloned.1.call-start = ((), (), s32[]{:S(2)}) async-start(), calls=%async_computation.4 | async-start | bytes 5242880 | tf_op jit(solution)/shard_map/reduce_scatter | solution.py:1453
  223.1 1.4 copy-start.15
  381.1 0.9 copy-start.13
  381.1 1.0 copy-start.12
  381.1 1.4 copy-start
  381.1 2.2 copy-start.14
  474.7 6.1 %copy-start.18 = (f32[16,128]{1,0:T(8,128)S(1)}, f32[16,128]{1,0:T(8,128)}, u32[]{:S(2)}) copy-start(f32[16,128]{1,0:T(8,128)} %get-tuple-element.91) | copy-start | bytes 24580
  480.8 33.7 %copy-start.2 = (f32[256,2048]{1,0:T(8,128)S(1)}, f32[256,2048]{1,0:T(8,128)}, u32[]{:S(2)}) copy-start(f32[256,2048]{1,0:T(8,128)} %get-tuple-element.135) | copy-start | bytes 6291460
  514.5 1.3 copy-start.11
  514.5 2.1 copy-start.10
  514.5 2.9 copy-start.9
  514.5 3.7 copy-start.8
  515.9 3.2 copy-start.5
  516.7 3.5 copy-start.4
  519.1 2.2 copy-start.3
Sparse Core Ops, SparseCore 0:
  156.9 96.2 reduce-scatter.3
  256.3 158.1 reduce-scatter.7
  417.7 54.4 reduce-scatter.5
